TPU v7x, 32 devices: a whole 2x2x4 slice. The times are simulated.
32 devices in a mesh: slides: 2 (over y), tiles: 4 (over z), heads: 4 (over x, core).
Axes of the slice: x: 2, y: 2, z: 4, core: 2. Of those that a mesh axis runs over, the one named last changes fastest.
Arguments:
- pixels: bfloat16 [32, 4096, 192], P(('slides', 'tiles', 'heads')), parts along dimension 0, may hold values from -6 to 6
- w_stem: bfloat16 [192, 64], replicated, may hold values from -0.4375 to 0.4375
- w_conv1: bfloat16 [4, 9, 16, 32], replicated, may hold values from -0.5 to 0.5
- w_conv2: bfloat16 [4, 9, 32, 64], replicated, may hold values from -0.375 to 0.375
- w_key: bfloat16 [256, 512], P(None, 'heads'), may hold values from -0.375 to 0.375
- w_value: bfloat16 [256, 512], P(None, 'heads'), may hold values from -0.375 to 0.375
- queries: bfloat16 [512, 512], P(None, 'heads'), may hold values from -104 to 104
- tile_count: int32 [32], P(('slides', 'tiles', 'heads')), parts along dimension 0, may hold values from 0 to 1, as said below
- tissue: int32 [32], P(('slides', 'tiles', 'heads')), parts along dimension 0, may hold values from 17 to 256, as said below
- adjacency: int32 [32, 3], P(('slides', 'tiles', 'heads')), parts along dimension 0, may hold values from -1 to 0, as said below
Outputs:
- pooled: bfloat16 [1024, 512], P(('slides', 'tiles'), 'heads'), parts along dimension 0
There are 2 independent parts, one for each index of `slides`. A program takes and returns all parts, laid end to end along the dimension named above; an argument that names none is the same for every part. Nothing has to cross between parts.
Inputs may be any that keep to these rules, and one draw needn't show every extreme that they name: Device g (order of tiles+heads) holds tiles in its slots 0 to tile_count[g] - 1; the first device holds 1, the second 1; other devices may hold none. Tokens 0 to tissue[s] - 1 of slot s, raster order, are tissue; slot 0 is all tissue. `adjacency`: A code below 1 names a slot of the previous device along tiles+heads, a code c of 1 or more names slot c - 1 of the same device, earlier than the slot itself; -1 is background.
All inputs are finite; a program needn't handle non-finite values.
Results may differ from a plain program's by a relative error of at most 0.012.
The roundings to bfloat16 on the way count: a program that leaves them out, or rounds other values in their place, can miss the bound.
Values may be sent and summed in bfloat16 or wider, within the bound.
No kernel may reach another device: no remote copies, remote signals or barrier semaphores. Data moves between devices by JAX's collectives and lax.ppermute only.
A program may use at most 128 MiB of HBM per device.

v0:
```python
import jax
import jax.numpy as jnp
from jax import lax
from jax.sharding import PartitionSpec as P

STEM_GRID = 64
PATCH_DIM = 192
C_STEM = 64
C_OUT = 256
HEAD_DIM = 64
TOK_TILE = 256


NEG_BIG = -1e30
LN_EPS = 1e-05


def passed_along(block, axis, distance):
    devices = range(lax.axis_size(axis))
    route = [(i - distance, i) for i in devices if i - distance in devices]
    return lax.ppermute(block, axis, route)


def merged_2(array, axis, combine):
    everything = jax.tree.map(lambda part: lax.all_gather(part, axis), array)
    first = jax.tree.map(lambda part: part[0], everything)

    def lap(k, so_far):
        return combine(so_far, jax.tree.map(lambda part: part[k], everything))

    return lax.fori_loop(1, lax.axis_size(axis), lap, first)


def border_lines(feature_map):
    slot_n = feature_map.shape[0]
    side = feature_map.shape[1]
    channels = feature_map.shape[3]
    return jnp.stack([feature_map[:, side - 1], feature_map[:, :, side - 1]], axis=1).reshape(
        slot_n, 2, side * channels
    )


def bordered(inner, earlier, own_lines, adjacency):
    slot_n = inner.shape[0]
    side = inner.shape[1]
    channels = inner.shape[3]
    lines = jnp.concatenate([earlier, own_lines], axis=0)
    source_n = lines.shape[0]
    chooser = (
        adjacency[:, :, None] == jnp.arange(source_n, dtype=jnp.int32)[None, None, :]
    ).astype(jnp.bfloat16)
    above = (
        jnp.dot(chooser[:, 0], lines[:, 0], preferred_element_type=jnp.float32)
        .astype(jnp.bfloat16)
        .reshape(slot_n, side, channels)
    )
    beside = (
        jnp.dot(chooser[:, 1], lines[:, 1], preferred_element_type=jnp.float32)
        .astype(jnp.bfloat16)
        .reshape(slot_n, side, channels)
    )
    last_pixel = lines[:, 0].reshape(source_n, side, channels)[:, side - 1]
    corner = jnp.dot(chooser[:, 2], last_pixel, preferred_element_type=jnp.float32).astype(
        jnp.bfloat16
    )
    first_line = jnp.concatenate([corner[:, None], above], axis=1)
    lower = jnp.concatenate([beside[:, :, None], inner], axis=2)
    return jnp.concatenate([first_line[:, None], lower], axis=1)


def grouped_conv(padded, weight):
    groups_n = weight.shape[0]
    in_group = weight.shape[2]
    out_group = weight.shape[3]
    kernel = (
        weight.reshape(groups_n, 3, 3, in_group, out_group)
        .transpose(1, 2, 3, 0, 4)
        .reshape(3, 3, in_group, groups_n * out_group)
    )
    return lax.conv_general_dilated(
        padded,
        kernel,
        window_strides=(2, 2),
        padding="VALID",
        dimension_numbers=("NHWC", "HWIO", "NHWC"),
        feature_group_count=groups_n,
        preferred_element_type=jnp.float32,
    )


def partial_attention(query_heads, key_rows, value_rows, valid_rows):
    scores = jnp.einsum(
        "lhd,thd->hlt", query_heads, key_rows, preferred_element_type=jnp.float32
    ) * float(HEAD_DIM) ** (-0.5)
    scores = jnp.where(valid_rows[None, None, :] > 0.5, scores, NEG_BIG)
    row_peak = jnp.max(scores, axis=2)
    weights = jnp.exp(scores - row_peak[:, :, None]) * valid_rows[None, None, :]
    totals = jnp.sum(weights, axis=2)
    weighted = jnp.einsum(
        "hlt,thd->lhd", weights.astype(jnp.bfloat16), value_rows, preferred_element_type=jnp.float32
    )
    latent_n = query_heads.shape[0]
    return (row_peak.T, totals.T, weighted.reshape(latent_n, -1))


def softmax_merge(first, second):
    joint = jnp.maximum(first[0], second[0])
    scale_one = jnp.exp(first[0] - joint)
    scale_two = jnp.exp(second[0] - joint)
    totals = first[1] * scale_one + second[1] * scale_two
    weighted = first[2] * jnp.repeat(scale_one, HEAD_DIM, axis=1) + second[2] * jnp.repeat(
        scale_two, HEAD_DIM, axis=1
    )
    return (joint, totals, weighted)


def per_device(
    pixels, w_stem, w_conv1, w_conv2, w_key, w_value, queries, tile_count, tissue, adjacency
):
    slot_n = pixels.shape[0]
    slot_live = (jnp.arange(slot_n, dtype=jnp.int32) < tile_count[0]).astype(jnp.float32)
    stem_flat = jnp.dot(
        pixels.reshape(slot_n * STEM_GRID * STEM_GRID, PATCH_DIM),
        w_stem,
        preferred_element_type=jnp.float32,
    )
    stem_map = (
        jnp.maximum(stem_flat, 0.0).reshape(slot_n, STEM_GRID, STEM_GRID, C_STEM)
        * slot_live[:, None, None, None]
    ).astype(jnp.bfloat16)
    stem_lines = border_lines(stem_map)
    stem_prior = passed_along(stem_lines, ("tiles", "heads"), 1)
    middle = grouped_conv(bordered(stem_map, stem_prior, stem_lines, adjacency), w_conv1)
    middle = (jnp.maximum(middle, 0.0) * slot_live[:, None, None, None]).astype(jnp.bfloat16)
    middle_lines = border_lines(middle)
    middle_prior = passed_along(middle_lines, ("tiles", "heads"), 1)
    deepest = jnp.maximum(
        grouped_conv(bordered(middle, middle_prior, middle_lines, adjacency), w_conv2), 0.0
    )
    token_n = slot_n * TOK_TILE
    deepest = deepest.reshape(token_n, C_OUT)
    centred = deepest - jnp.mean(deepest, axis=1, keepdims=True)
    normed = (
        centred * lax.rsqrt(jnp.mean(centred * centred, axis=1, keepdims=True) + LN_EPS)
    ).astype(jnp.bfloat16)
    in_tile = (jnp.arange(TOK_TILE, dtype=jnp.int32)[None, :] < tissue[:, None]).astype(jnp.float32)
    valid = (in_tile * slot_live[:, None]).reshape(token_n).astype(jnp.bfloat16)
    latent_n = queries.shape[0]
    head_local = queries.shape[1] // HEAD_DIM
    head_width = head_local * HEAD_DIM
    weight_both = jnp.concatenate([w_key, w_value], axis=1)
    query_heads = queries.reshape(latent_n, head_local, HEAD_DIM)

    def attend_rows(running, normed_rows, valid_rows):
        projected = jnp.dot(normed_rows, weight_both, preferred_element_type=jnp.float32).astype(
            jnp.bfloat16
        )
        key_rows = projected[:, :head_width].reshape(-1, head_local, HEAD_DIM)
        value_rows = projected[:, head_width:].reshape(-1, head_local, HEAD_DIM)
        return softmax_merge(
            running, partial_attention(query_heads, key_rows, value_rows, valid_rows)
        )

    start_state = (
        jnp.full((latent_n, head_local), NEG_BIG, jnp.float32),
        jnp.zeros((latent_n, head_local), jnp.float32),
        jnp.zeros((latent_n, head_width), jnp.float32),
    )
    normed_rows = lax.all_gather(normed, "heads", axis=0, tiled=True)
    valid_rows = lax.all_gather(valid, "heads", axis=0, tiled=True)
    row_total = normed_rows.shape[0]
    blocks = (
        normed_rows.reshape(row_total // token_n, token_n, C_OUT),
        valid_rows.reshape(row_total // token_n, token_n),
    )

    def scan_step(inner_state, block_pair):
        return (attend_rows(inner_state, block_pair[0], block_pair[1]), None)

    softmax_state = lax.scan(scan_step, start_state, blocks)[0]
    tile_n = lax.axis_size("tiles")
    share = latent_n // tile_n
    merged = merged_2(softmax_state, "tiles", softmax_merge)
    first_row = lax.axis_index("tiles") * share
    totals = lax.dynamic_slice_in_dim(merged[1], first_row, share, 0)
    weighted = lax.dynamic_slice_in_dim(merged[2], first_row, share, 0)
    return (weighted / jnp.repeat(totals, HEAD_DIM, axis=1)).astype(jnp.bfloat16)


def solution(mesh):
    in_specs = (
        P(("slides", "tiles", "heads"), None, None),
        P(),
        P(),
        P(),
        P(None, "heads"),
        P(None, "heads"),
        P(None, "heads"),
        P(("slides", "tiles", "heads")),
        P(("slides", "tiles", "heads")),
        P(("slides", "tiles", "heads"), None),
    )
    out_specs = P(("slides", "tiles"), "heads")
    return jax.shard_map(
        per_device, mesh=mesh, in_specs=in_specs, out_specs=out_specs, check_vma=False
    )
```

profile of v0, /device:TPU:0, one launch (start us, length us, event | category | flops | bytes accessed | tf_op | source)
XLA Modules:
  0.0 160.6 jit_solution(8616740887920046742)
XLA Ops:
  7.3 0.6 copy-done
  8.0 1.2 fusion.19
  9.2 1.1 convert_element_type.93
  10.3 1.4 slice.83
  11.7 2.4 %copy.115 = bf16[1,64,1,64]{3,1,2,0:T(8,128)(2,1)S(1)} copy(bf16[1,64,1,64]{2,1,3,0:T(8,128)(2,1)} %slice.83) | data formatting | bytes 16384
  14.5 2.4 %collective-permute-start = (bf16[1,2,4096]{2,1,0:T(2,128)(2,1)S(1)}, bf16[1,2,4096]{2,1,0:T(2,128)(2,1)S(1)}, u32[]{:S(2)}, u32[]{:S(2)}) collective-permute-start(bf16[1,2,4096]{2,1,0:T(2,128)(2,1)S(1)} %pad_maximum_fusion.2), channel_id=1, source_target_pairs={{0,1},{1,2},{2,3},{3,4},{4,5},{5,6},{6,7},{7,8},{8,9},{9,10},{10,1... | collective-permute-start | bytes 49160 | tf_op jit(solution)/shard_map/ppermute | solution.py:21
  16.9 2.1 %convert_element_type.97 = bf16[1,64,64,4,16]{2,1,4,3,0:T(8,128)(2,1)} reshape(bf16[4096,64]{0,1:T(8,128)(2,1)S(1)} %fusion.19) | data formatting | bytes 1048576 | tf_op jit(solution)/shard_map/convert_element_type | solution.py:130
  19.1 2.9 %copy.91 = bf16[1,64,64,4,16]{2,4,3,1,0:T(8,128)(2,1)} copy(bf16[1,64,64,4,16]{2,1,4,3,0:T(8,128)(2,1)} %convert_element_type.97) | data formatting | bytes 1048576 | tf_op jit(solution)/shard_map/convert_element_type | solution.py:130
  22.7 0.1 slice_reduce_fusion
  22.8 0.1 fusion.31
  23.0 3.2 %concatenate.63 = bf16[1,64,1,4,16]{2,4,3,1,0:T(8,128)(2,1)} reshape(bf16[4096]{0:T(1024)(128)(2,1)S(1)} %convert_element_type.96) | data formatting | bytes 16384 | tf_op jit(solution)/shard_map/concatenate | solution.py:67
  26.1 0.1 fusion.30
  26.6 0.1 fusion.23
  26.7 0.1 concatenate.62
  26.9 2.1 %maximum_maximum_fusion.1 = bf16[1,65,65,4,16]{2,4,3,1,0:T(8,128)(2,1)S(1)} fusion(bf16[1,64,64,4,16]{2,4,3,1,0:T(8,128)(2,1)} %copy.91, bf16[1,64,1,4,16]{2,4,3,1,0:T(8,128)(2,1)} %concatenate.63, bf16[1,1,64,4,16]{2,4,3,1,0:T(8,128)(2,1)S(1)} %copy.89, bf16[1,1,1,4,16]{2,4,3,1,0:T(8,128)(2,1)S(1)} %concatenate.62), kind=kLoop, calls=%fused_computation.51 | loop fusion | flops 2163200 | bytes 1081600 | tf_op jit(solution)/shard_map/concatenate | solution.py:68
  29.0 13.2 %copy.92 = bf16[1,65,65,4,16]{4,0,3,2,1:T(2,128)(2,1)} copy(bf16[1,65,65,4,16]{2,4,3,1,0:T(8,128)(2,1)S(1)} %maximum_maximum_fusion.1) | data formatting | bytes 1081600 | tf_op jit(solution)/shard_map/concatenate | solution.py:68
  42.2 22.5 %fusion.39 = (bf16[32,32,4,32]{3,2,1,0:T(4,128)(2,1)S(1)}, bf16[1,32,32,4,32]{4,0,3,2,1:T(2,128)(2,1)}) fusion(f32[]{:T(128)} %bitcast.6, bf16[1,65,65,4,16]{4,0,3,2,1:T(2,128)(2,1)} %copy.92, bf16[4,3,3,16,32]{4,3,2,1,0:T(8,128)(2,1)S(1)} %bitcast.205), kind=kOutput, calls=%fused_computation.90 | convolution fusion | flops 38141952 | bytes 1101956 | tf_op jit(solution)/shard_map/conv_general_dilated | solution.py:80
  64.7 0.5 convert_element_type.99
  65.3 4.5 %collective-permute-start.1 = (bf16[1,2,4096]{2,0,1:T(2,128)(2,1)S(1)}, bf16[1,2,4096]{2,0,1:T(2,128)(2,1)S(1)}, u32[]{:S(2)}, u32[]{:S(2)}) collective-permute-start(bf16[1,2,4096]{2,0,1:T(2,128)(2,1)S(1)} %pad_maximum_fusion.1), channel_id=1, source_target_pairs={{0,1},{1,2},{2,3},{3,4},{4,5},{5,6},{6,7},{7,8},{8,9},{9,10},{10,1... | collective-permute-start | bytes 49160 | tf_op jit(solution)/shard_map/ppermute | solution.py:21
  69.9 5.1 %all-gather.3 = bf16[4,1,256]{2,1,0:T(2,128)(2,1)S(1)} all-gather(bf16[1,1,256]{2,1,0:T(2,128)(2,1)S(1)} %reshape.325), channel_id=1, replica_groups=mesh['slides'=2,'tiles'=4,'heads'=4] {'heads'}, dimensions={0}, use_global_device_ids=true | all-gather | bytes 2560 | tf_op jit(solution)/shard_map/all_gather | solution.py:170
  75.0 0.1 copy.102
  75.1 5.2 %copy.99 = bf16[1,32,32,4,32]{2,4,3,1,0:T(8,128)(2,1)S(1)} copy(bf16[1,32,32,4,32]{4,0,3,2,1:T(2,128)(2,1)} %get-tuple-element.341) | data formatting | bytes 524288 | tf_op jit(solution)/shard_map/convert_element_type | solution.py:134
  80.4 0.1 fusion.32
  80.6 0.1 fusion.28
  80.8 3.1 %concatenate.65 = bf16[1,32,1,4,32]{2,4,3,1,0:T(8,128)(2,1)} reshape(bf16[4096]{0:T(1024)(128)(2,1)S(1)} %convert_element_type.102) | data formatting | bytes 16384 | tf_op jit(solution)/shard_map/concatenate | solution.py:67
  84.1 0.1 fusion.24
  84.2 0.2 concatenate.64
  84.5 2.8 %maximum_maximum_fusion = bf16[1,33,33,4,32]{2,4,3,1,0:T(8,128)(2,1)} fusion(bf16[1,32,32,4,32]{2,4,3,1,0:T(8,128)(2,1)S(1)} %copy.99, bf16[1,32,1,4,32]{2,4,3,1,0:T(8,128)(2,1)} %concatenate.65, bf16[1,1,32,4,32]{2,4,3,1,0:T(8,128)(2,1)S(1)} %copy.97, bf16[1,1,1,4,32]{2,4,3,1,0:T(8,128)(2,1)S(1)} %concatenate.64), kind=kLoop, calls=%fused_computation.50 | loop fusion | flops 1115136 | bytes 557568 | tf_op jit(solution)/shard_map/concatenate | solution.py:68
  87.3 6.1 %copy.100 = bf16[1,33,33,4,32]{4,0,3,2,1:T(2,128)(2,1)} copy(bf16[1,33,33,4,32]{2,4,3,1,0:T(8,128)(2,1)} %maximum_maximum_fusion) | data formatting | bytes 557568 | tf_op jit(solution)/shard_map/concatenate | solution.py:68
  93.4 5.4 %fusion.40 = (f32[16,16]{1,0:T(8,128)S(1)}, f32[1,16,16,4,64]{4,0,3,2,1:T(1,128)S(1)}) fusion(bf16[1,33,33,4,32]{4,0,3,2,1:T(2,128)(2,1)} %copy.100, bf16[4,3,3,32,64]{4,3,2,1,0:T(8,128)(2,1)S(1)} %bitcast.204), kind=kOutput, calls=%fused_computation.91 | convolution fusion | flops 37879552 | bytes 689408 | tf_op jit(solution)/shard_map/conv_general_dilated | solution.py:80
  99.0 0.5 broadcast.180
  99.5 3.4 %multiply_reduce_fusion = (f32[16,16]{1,0:T(8,128)S(1)}, f32[16,16,4,64]{3,2,1,0:T(4,128)S(1)}) fusion(f32[1,16,16,4,64]{4,0,3,2,1:T(1,128)S(1)} %get-tuple-element.343, f32[16,16]{1,0:T(8,128)S(1)} %broadcast_multiply_fusion, f32[]{:T(128)} %broadcast.180), kind=kLoop, calls=%fused_computation.52 | loop fusion | flops 196352 | bytes 526340 | tf_op jit(solution)/shard_map/reduce_sum | solution.py:144
  102.9 0.3 max.55
  103.4 0.1 multiply_convert_fusion
  103.5 7.7 %all_gather.25 = bf16[1024,256]{1,0:T(8,128)(2,1)} all-gather(bf16[256,256]{1,0:T(8,128)(2,1)S(1)} %multiply_convert_fusion), channel_id=1, replica_groups=mesh['slides'=2,'tiles'=4,'heads'=4] {'heads'}, dimensions={0}, use_global_device_ids=true | all-gather | bytes 655360 | tf_op jit(solution)/shard_map/all_gather | solution.py:169
  111.2 9.0 %while.35 = (s32[]{:T(128)}, f32[512,2]{0,1:T(2,128)S(1)}, f32[512,2]{0,1:T(2,128)S(1)}, f32[512,128]{0,1:T(8,128)S(1)}, bf16[4,256]{1,0:T(4,128)(2,1)S(1)}, /*i...) while((s32[]{:T(128)}, f32[512,2]{0,1:T(2,128)S(1)}, ...), condition=%wide.region_5.6_spmd.clone, body=%wide.region_2.5_spmd.clone.sunk | while | flops 103357440 | bytes 5174392 | solution.py:180
  111.2 1.1 convolution_convert_fusion.2
  112.4 0.4 fusion.71
  112.8 0.2 fusion.73
  113.1 0.3 fusion.75
  113.5 1.1 convolution_convert_fusion.2
  114.7 0.4 fusion.71
  115.0 0.2 fusion.73
  115.3 0.3 fusion.75
  115.7 1.1 convolution_convert_fusion.2
  116.9 0.4 fusion.71
  117.3 0.2 fusion.73
  117.5 0.3 fusion.75
  118.0 1.1 convolution_convert_fusion.2
  119.2 0.4 fusion.71
  119.5 0.2 fusion.73
  119.8 0.3 fusion.75
  120.2 0.7 copy-done.1
  121.0 13.4 %all-gather = f32[2048,2]{0,1:T(2,128)S(1)} all-gather(f32[512,2]{0,1:T(2,128)S(1)} %get-tuple-element.226), channel_id=2, replica_groups=mesh['slides'=2,'tiles'=4,'heads'=4] {'tiles'}, dimensions={0}, use_global_device_ids=true | all-gather | bytes 20480 | tf_op jit(solution)/shard_map/all_gather | solution.py:25
  134.3 13.3 %all-gather.1 = f32[2048,2]{0,1:T(2,128)S(1)} all-gather(f32[512,2]{0,1:T(2,128)S(1)} %get-tuple-element.227), channel_id=3, replica_groups=mesh['slides'=2,'tiles'=4,'heads'=4] {'tiles'}, dimensions={0}, use_global_device_ids=true | all-gather | bytes 20480 | tf_op jit(solution)/shard_map/all_gather | solution.py:25
  147.6 2.1 %all-gather.6.cloned.1.call-done = f32[2048,128]{0,1:T(8,128)} async-done(((f32[512,128]{0,1:T(8,128)}), f32[2048,128]{0,1:T(8,128)}) %all-gather.6.cloned.1.call-update) | async-done | bytes 1048592 | tf_op jit(solution)/shard_map/all_gather | solution.py:25
  149.7 2.0 %reshape.318 = f32[4,512,128]{1,0,2:T(4,128)S(1)} reshape(f32[2048,128]{0,1:T(8,128)} %all-gather.6.cloned.1.call-done) | data formatting | bytes 2097152 | tf_op jit(solution)/shard_map/all_gather | solution.py:25
  151.7 1.2 while.34
  151.8 0.2 constant_dynamic-slice_fusion.4
  152.0 0.1 fusion.63
  152.2 0.2 constant_dynamic-slice_fusion.4
  152.4 0.1 fusion.63
  152.6 0.2 constant_dynamic-slice_fusion.4
  153.0 0.7 copy.106
  (84 shorter events, 2.4 us)
Async XLA Ops:
  6.5 1.4 copy-start
  6.5 143.2 %all-gather.6.cloned.1.call-start = ((), (), s32[]{:S(2)}) async-start(), calls=%async_computation | async-start | bytes 1310720 | tf_op jit(solution)/shard_map/all_gather | solution.py:25
  9.1 7.7 %copy-start.7 = (s32[1,3]{1,0:T(1,128)S(1)}, s32[1,3]{1,0:T(1,128)}, u32[]{:S(2)}) copy-start(s32[1,3]{1,0:T(1,128)} %param.23) | copy-start | bytes 40
  9.1 7.8 %copy-start.3 = (bf16[256,128]{1,0:T(8,128)(2,1)S(1)}, bf16[256,128]{1,0:T(8,128)(2,1)}, u32[]{:S(2)}) copy-start(bf16[256,128]{1,0:T(8,128)(2,1)} %param.19) | copy-start | bytes 196612
  9.2 7.8 %copy-start.4 = (bf16[256,128]{1,0:T(8,128)(2,1)S(1)}, bf16[256,128]{1,0:T(8,128)(2,1)}, u32[]{:S(2)}) copy-start(bf16[256,128]{1,0:T(8,128)(2,1)} %param.18) | copy-start | bytes 196612
  14.5 8.1 %collective-permute-start = (bf16[1,2,4096]{2,1,0:T(2,128)(2,1)S(1)}, bf16[1,2,4096]{2,1,0:T(2,128)(2,1)S(1)}, u32[]{:S(2)}, u32[]{:S(2)}) collective-permute-start(bf16[1,2,4096]{2,1,0:T(2,128)(2,1)S(1)} %pad_maximum_fusion.2), channel_id=1, source_target_pairs={{0,1},{1,2},{2,3},{3,4},{4,5},{5,6},{6,7},{7,8},{8,9},{9,10},{10,1... | collective-permute-start | bytes 49160 | tf_op jit(solution)/shard_map/ppermute | solution.py:21
  29.0 13.2 %copy-start.6 = (bf16[4,9,16,32]{3,2,1,0:T(8,128)(2,1)S(1)}, bf16[4,9,16,32]{3,2,1,0:T(8,128)(2,1)}, u32[]{:S(2)}) copy-start(bf16[4,9,16,32]{3,2,1,0:T(8,128)(2,1)} %param.16) | copy-start | bytes 110596
  42.2 32.7 %copy-start.2 = (bf16[512,128]{1,0:T(8,128)(2,1)S(1)}, bf16[512,128]{1,0:T(8,128)(2,1)}, u32[]{:S(2)}) copy-start(bf16[512,128]{1,0:T(8,128)(2,1)} %param.20) | copy-start | bytes 393220
  65.3 15.0 %collective-permute-start.1 = (bf16[1,2,4096]{2,0,1:T(2,128)(2,1)S(1)}, bf16[1,2,4096]{2,0,1:T(2,128)(2,1)S(1)}, u32[]{:S(2)}, u32[]{:S(2)}) collective-permute-start(bf16[1,2,4096]{2,0,1:T(2,128)(2,1)S(1)} %pad_maximum_fusion.1), channel_id=1, source_target_pairs={{0,1},{1,2},{2,3},{3,4},{4,5},{5,6},{6,7},{7,8},{8,9},{9,10},{10,1... | collective-permute-start | bytes 49160 | tf_op jit(solution)/shard_map/ppermute | solution.py:21
  87.3 6.1 %copy-start.5 = (bf16[4,9,32,64]{3,2,1,0:T(8,128)(2,1)S(1)}, bf16[4,9,32,64]{3,2,1,0:T(8,128)(2,1)}, u32[]{:S(2)}) copy-start(bf16[4,9,32,64]{3,2,1,0:T(8,128)(2,1)} %param.17) | copy-start | bytes 442372
  120.2 0.7 copy-start.1
  149.7 2.0 %slice-start = ((f32[2048,128]{0,1:T(8,128)}), f32[512,128]{0,1:T(8,128)S(1)}, s32[]{:S(2)}) async-start(f32[2048,128]{0,1:T(8,128)} %all-gather.6.cloned.1.call-done), calls=%async_computation.1 | async-start | bytes 524288 | tf_op jit(solution)/shard_map/slice | solution.py:26
Sparse Core Ops, SparseCore 0:
  121.1 28.5 all-gather.5
where the time goes:
time: 161 us
  local copies, waits for them, and re-layouts  48.7 us (30%)
  blocking collectives  39.4 us (24%)
  matrix products  37.1 us (23%)
  between operations  15.2 us (9%)
  other arithmetic  10.8 us (7%)
  starting transfers between devices  6.87 us (4%)
  waiting for transfers between devices  2.12 us (1%)
    conv_general_dilated x2, matrix products, grouped_conv(): lax.conv_general_dilated(padded, kernel, window_strides=(2, 2), padding='...  27.9 us
    all_gather x2, blocking collectives, merged_2(): everything = jax.tree.map(lambda part: lax.all_gather(part, axis), array)  26.6 us
    concatenate x2, local copies, waits for them, and re-layouts, bordered(): return jnp.concatenate([first_line[:, None], lower], axis=1)  19.3 us
    all_gather x1, blocking collectives, per_device(): normed_rows = lax.all_gather(normed, 'heads', axis=0, tiled=True)  7.71 us
    ppermute x2, starting transfers between devices, passed_along(): return lax.ppermute(block, axis, route)  6.87 us
    concatenate x2, local copies, waits for them, and re-layouts, bordered(): lower = jnp.concatenate([beside[:, :, None], inner], axis=2)  6.28 us
    convert_element_type x3, local copies, waits for them, and re-layouts, per_device(): stem_map = (jnp.maximum(stem_flat, 0.0).reshape(slot_n, STEM_GRID, STEM_G...  6.14 us
    convert_element_type x2, local copies, waits for them, and re-layouts, per_device(): (jnp.maximum(middle, 0.0) * slot_live[:, None, None, None]).astype(jnp.bf...  5.74 us
  transfers between devices with their start and end apart: 3, of which 1 were waited for; matrix products, arithmetic and copies ran while one was open for 7% of the time, Pallas kernels for 0%

commit v1 on v0

v1 whole, which is shorter than its diff:
```python
import jax
import jax.numpy as jnp
from jax import lax
from jax.experimental import pallas as pl
from jax.experimental.pallas import tpu as pltpu
from jax.sharding import PartitionSpec as P

HEAD_DIM = 64
NEG_BIG = -1e30
LN_EPS = 1e-05
F32 = jnp.float32
BF16 = jnp.bfloat16
VMEM = pltpu.VMEM
SMEM = pltpu.SMEM
MIB = 1 << 20


def vmem_spec():
    return pl.BlockSpec(memory_space=VMEM)


def smem_spec():
    return pl.BlockSpec(memory_space=SMEM)


def expand_weights(flat, in_group, out_group, dense_ref):
    groups = flat.shape[0] // (9 * in_group)
    wide = groups * out_group
    source = lax.broadcasted_iota(jnp.int32, (out_group, wide), 0)
    target = lax.broadcasted_iota(jnp.int32, (out_group, wide), 1)
    spread = (lax.rem(target, out_group) == source).astype(BF16)
    tiled = jnp.dot(flat, spread, preferred_element_type=F32)
    row = lax.broadcasted_iota(jnp.int32, tiled.shape, 0)
    lane = lax.broadcasted_iota(jnp.int32, tiled.shape, 1)
    own = lax.div(row, 9 * in_group) == lax.div(lane, out_group)
    tiled = jnp.where(own, tiled, 0.0).astype(BF16)
    dense_ref[...] = jnp.zeros_like(dense_ref)
    for group in range(groups):
        for tap_row in range(3):
            for tap_col in range(3):
                py, px = int(tap_row != 1), int(tap_col != 1)
                block = 2 * int(tap_row == 0) + int(tap_col == 0)
                first = (9 * group + 3 * tap_row + tap_col) * in_group
                to_row = (2 * py + px) * groups * in_group + group * in_group
                dense_ref[pl.ds(to_row, in_group), pl.ds(block * wide, wide)] = tiled[
                    first : first + in_group
                ]


def shifted_down(x):
    row = lax.broadcasted_iota(jnp.int32, x.shape, 0)
    return jnp.where(row == 0, 0.0, pltpu.roll(x, 1, 0))


def stem_kernel(side, count_ref, adjacency_ref, w_ref, pixels_hbm, cells_ref, border_ref,
                pixels, stem, sems):
    chunk_n = sems.shape[0]
    rows = pixels.shape[0] // chunk_n
    copies = [
        pltpu.make_async_copy(
            pixels_hbm.at[0, pl.ds(k * rows, rows)], pixels.at[pl.ds(k * rows, rows)], sems.at[k]
        )
        for k in range(chunk_n)
    ]
    for copy in copies:
        copy.start()
    live = (count_ref[0] > 0).astype(F32)
    weight = w_ref[...]
    channels = weight.shape[1]
    doubled = jnp.concatenate([weight, weight], axis=1)
    half = side // 2
    lane = lax.broadcasted_iota(jnp.int32, (half, 2 * channels), 1)
    left = lane < channels
    lines = rows // side
    for k in range(chunk_n):
        copies[k].wait()
        out = jnp.dot(pixels[pl.ds(k * rows, rows)], doubled, preferred_element_type=F32)
        stem[pl.ds(k * rows, rows)] = jnp.maximum(out, 0.0) * live
        for y in range(k * lines, (k + 1) * lines):
            even = stem[pl.ds(y * side, half, stride=2)]
            odd = stem[pl.ds(y * side + 1, half, stride=2)]
            cells_ref[pl.ds((y // 2) * half, half), pl.ds((y % 2) * 2 * channels, 2 * channels)] = (
                jnp.where(left, even, odd).astype(BF16)
            )
    border_ref[pl.ds(0, 2 * half)] = cells_ref[pl.ds((half - 2) * half, 2 * half)]
    for which in range(2):
        x = side - 4 + 2 * which
        for py in range(2):
            even = stem[pl.ds(py * side + x, half, stride=2 * side)]
            odd = stem[pl.ds(py * side + x + 1, half, stride=2 * side)]
            border_ref[
                pl.ds((2 + which) * half, half), pl.ds(py * 2 * channels, 2 * channels)
            ] = jnp.where(left, even, odd).astype(BF16)
    facts = border_ref.shape[0] - 4 * half
    row = lax.broadcasted_iota(jnp.int32, (facts, border_ref.shape[1]), 0)
    above = (adjacency_ref[0, 0] == 0).astype(F32)
    beside = (adjacency_ref[0, 1] == 0).astype(F32)
    told = jnp.where(row == 0, live, jnp.where(row == 1, above, jnp.where(row == 2, beside, 0.0)))
    border_ref[pl.ds(4 * half, facts)] = told.astype(BF16)


def conv_kernel(half, in_group, cells_ref, w1_ref, w2_ref, partial_ref, dense1_ref, dense2_ref,
                wide):
    expand_weights(w1_ref[...], in_group, w1_ref.shape[1], dense1_ref)
    positions, channels = partial_ref.shape
    chunk = 8 * half
    wide[pl.ds(0, half)] = jnp.zeros((half, wide.shape[1]), F32)
    row = lax.broadcasted_iota(jnp.int32, (chunk, channels), 0)
    first = lax.rem(row, half) == 0
    dense = dense1_ref[...]
    for k in range(positions // chunk):
        wide[pl.ds(half + k * chunk, chunk)] = jnp.dot(
            cells_ref[pl.ds(k * chunk, chunk)], dense, preferred_element_type=F32
        )
        here = pl.ds(half + k * chunk, chunk)
        up = pl.ds(k * chunk, chunk)
        lane = [pl.ds(b * channels, channels) for b in range(4)]
        before = wide[here, lane[1]] + wide[up, lane[3]]
        before = jnp.where(first, 0.0, pltpu.roll(before, 1, 0))
        partial_ref[pl.ds(k * chunk, chunk)] = wide[here, lane[0]] + wide[up, lane[2]] + before
    expand_weights(w2_ref[...], w2_ref.shape[0] // 36, w2_ref.shape[1], dense2_ref)


def token_kernel(count_ref, tissue_ref, adjacency_ref, partial_ref, prior_ref, second_ref,
                 dense1_ref, dense2_ref, token_ref, middle, lines, cells, wide, whole):
    positions, channels = partial_ref.shape
    half = 32
    while half * half > positions:
        half //= 2
    quarter = half // 2
    live = (count_ref[0] > 0).astype(F32)
    above = (adjacency_ref[0, 0] == 0).astype(F32)
    beside = (adjacency_ref[0, 1] == 0).astype(F32)
    corner = (adjacency_ref[0, 2] == 0).astype(F32)
    lane = [slice(b * channels, (b + 1) * channels) for b in range(4)]
    dense1 = dense1_ref[...]
    prior = jnp.dot(prior_ref[pl.ds(0, 4 * half)], dense1, preferred_element_type=F32)
    second = jnp.dot(second_ref[pl.ds(0, 2 * half)], dense1, preferred_element_type=F32)
    facts = prior_ref[pl.ds(4 * half, 16), pl.ds(0, channels)].astype(F32)
    live_prior, above_prior, beside_prior = facts[0:1], facts[1:2], facts[2:3]
    row_30 = prior[0:half]
    row_31 = prior[half : 2 * half]
    col_30 = prior[2 * half : 3 * half]
    col_31 = prior[3 * half : 4 * half]
    at_zero = lax.broadcasted_iota(jnp.int32, (half, channels), 0) == 0
    middle[...] = jnp.maximum(partial_ref[...], 0.0) * live
    top = above * (row_31[:, lane[2]] + shifted_down(row_31[:, lane[3]]))
    top = top + jnp.where(at_zero, corner * row_31[half - 1 : half, lane[3]], 0.0)
    side = beside * (col_31[:, lane[1]] + shifted_down(col_31[:, lane[3]]))
    top_sum = partial_ref[pl.ds(0, half)] + top
    side_sum = partial_ref[pl.ds(0, half, stride=half)] + side
    side_sum = side_sum + jnp.where(at_zero, top, 0.0)
    middle[pl.ds(0, half)] = jnp.maximum(top_sum, 0.0) * live
    middle[pl.ds(0, half, stride=half)] = jnp.maximum(side_sum, 0.0) * live
    last = second[2 * half - 1 : 2 * half]
    over_last = second[half - 1 : half]
    left_last = second[2 * half - 2 : 2 * half - 1]
    row_sum = row_31[:, lane[0]] + row_30[:, lane[2]]
    row_sum = row_sum + shifted_down(row_31[:, lane[1]] + row_30[:, lane[3]])
    row_sum = row_sum + jnp.where(
        at_zero, beside_prior * (last[:, lane[1]] + over_last[:, lane[3]]), 0.0
    )
    col_sum = col_31[:, lane[0]] + col_30[:, lane[1]]
    col_sum = col_sum + shifted_down(col_31[:, lane[2]] + col_30[:, lane[3]])
    col_sum = col_sum + jnp.where(
        at_zero, above_prior * (last[:, lane[2]] + left_last[:, lane[3]]), 0.0
    )
    lines[pl.ds(0, half)] = jnp.maximum(row_sum, 0.0) * live_prior
    lines[pl.ds(half, half)] = jnp.maximum(col_sum, 0.0) * live_prior
    for i in range(half):
        for px in range(2):
            cells[
                pl.ds((i // 2) * quarter, quarter), pl.ds((2 * (i % 2) + px) * channels, channels)
            ] = middle[pl.ds(i * half + px, quarter, stride=2)].astype(BF16)
    tokens = quarter * quarter
    cells[pl.ds(tokens, 2 * quarter)] = jnp.zeros((2 * quarter, cells.shape[1]), BF16)
    for parity in range(2):
        cells[pl.ds(tokens, quarter), pl.ds((2 + parity) * channels, channels)] = lines[
            pl.ds(parity, quarter, stride=2)
        ].astype(BF16)
        cells[pl.ds(tokens + quarter, quarter), pl.ds((2 * parity + 1) * channels, channels)] = (
            lines[pl.ds(half + parity, quarter, stride=2)].astype(BF16)
        )
    out_n = dense2_ref.shape[1] // 4
    wide[...] = jnp.dot(cells[...], dense2_ref[...], preferred_element_type=F32)
    block = [pl.ds(b * out_n, out_n) for b in range(4)]
    body, up = pl.ds(quarter, tokens - quarter), pl.ds(0, tokens - quarter)
    topmost = pl.ds(0, quarter)
    above_rows, beside_rows = pl.ds(tokens, quarter), pl.ds(tokens + quarter, quarter)
    at_zero = lax.broadcasted_iota(jnp.int32, (quarter, out_n), 0) == 0
    wide[body, block[0]] = wide[body, block[0]] + wide[up, block[2]]
    wide[topmost, block[0]] = wide[topmost, block[0]] + above * wide[above_rows, block[2]]
    before = wide[pl.ds(0, tokens), block[1]]
    up_left = jnp.concatenate(
        [above * wide[above_rows, block[3]], wide[up, block[3]]], axis=0
    )
    before = before + up_left
    row = lax.broadcasted_iota(jnp.int32, before.shape, 0)
    before = jnp.where(lax.rem(row, quarter) == 0, 0.0, pltpu.roll(before, 1, 0))
    deep = wide[pl.ds(0, tokens), block[0]] + before
    left = beside * (wide[beside_rows, block[1]] + shifted_down(wide[beside_rows, block[3]]))
    left = left + jnp.where(
        at_zero, corner * wide[pl.ds(tokens + quarter - 1, 1), block[3]], 0.0
    )
    spots = pl.ds(0, quarter, stride=quarter)
    pieces = []
    for part in range(out_n // 128):
        column = slice(part * 128, (part + 1) * 128)
        whole[part] = deep[:, column]
        whole[part, spots] = whole[part, spots] + left[:, column]
        pieces.append(whole[part])
    deep = jnp.maximum(jnp.concatenate(pieces, axis=1), 0.0)
    centred = deep - jnp.mean(deep, axis=1, keepdims=True)
    spread = jnp.mean(centred * centred, axis=1, keepdims=True)
    token_ref[pl.ds(0, tokens)] = (centred * lax.rsqrt(spread + LN_EPS)).astype(BF16)
    known = (live * tissue_ref[0].astype(F32)) * jnp.ones((16, out_n), F32)
    token_ref[pl.ds(tokens, 16)] = known.astype(BF16)


def attention_kernel(place_ref, t0, t1, t2, t3, wk_ref, wv_ref, q_ref, out_ref, keys, values):
    token_refs = (t0, t1, t2, t3)
    tokens = t0.shape[0] - 16
    width = wk_ref.shape[1]
    both = jnp.concatenate([wk_ref[...], wv_ref[...]], axis=1)
    masks = []
    lane_token = lax.broadcasted_iota(jnp.int32, (1, tokens), 1).astype(F32)
    for b, ref in enumerate(token_refs):
        made = jnp.dot(ref[pl.ds(0, tokens)], both, preferred_element_type=F32).astype(BF16)
        keys[pl.ds(b * tokens, tokens)] = made[:, :width]
        values[pl.ds(b * tokens, tokens)] = made[:, width:]
        known = ref[pl.ds(tokens, 16), pl.ds(0, tokens)].astype(F32)[0:1]
        masks.append(jnp.where(lane_token < known, 0.0, NEG_BIG))
    bias = jnp.concatenate(masks, axis=1)
    place = place_ref[0]
    part_n, part_rows = out_ref.shape[0], out_ref.shape[1] - 16
    lane = lax.broadcasted_iota(jnp.int32, (part_rows, width), 1)
    row8 = lax.broadcasted_iota(jnp.int32, (8, part_rows), 0)
    key_all = keys[...]
    value_all = values[...]
    for k in range(part_n):
        part = place ^ k
        q = q_ref[pl.ds(pl.multiple_of(part * part_rows, part_rows), part_rows)].astype(F32)
        q = q * (float(HEAD_DIM) ** -0.5)
        joined = None
        facts = jnp.zeros((part_rows, width), F32)
        head_n = width // HEAD_DIM
        for h in range(head_n):
            mine = lax.div(lane, HEAD_DIM) == h
            q_h = jnp.where(mine, q, 0.0).astype(BF16)
            scores = lax.dot_general(
                q_h, key_all, (((1,), (1,)), ((), ())), preferred_element_type=F32
            )
            scores = scores + bias
            peak = jnp.max(scores, axis=1, keepdims=True)
            weights = jnp.exp(scores - peak)
            total = jnp.sum(weights, axis=1, keepdims=True)
            summed = jnp.dot(weights.astype(BF16), value_all, preferred_element_type=F32)
            joined = summed if joined is None else jnp.where(mine, summed, joined)
            facts = jnp.where(lane == h, peak, facts)
            facts = jnp.where(lane == head_n + h, total, facts)
        out_ref[k, pl.ds(0, part_rows)] = joined.astype(BF16)
        turned = facts.T[0:8]
        high = turned.astype(BF16).astype(F32)
        rest = turned - high
        mid = rest.astype(BF16).astype(F32)
        low = rest - mid
        upper = jnp.where(row8 < 4, high, pltpu.roll(mid, 4, 0))
        out_ref[k, pl.ds(part_rows, 16)] = jnp.concatenate([upper, low], axis=0).astype(BF16)


def merge_kernel(head_n, m0, m1, m2, m3, out_ref):
    part_rows = out_ref.shape[0]
    width = out_ref.shape[1]
    stats = []
    for ref in (m0, m1, m2, m3):
        coded = ref[pl.ds(part_rows, 16)].astype(F32)
        upper, low = coded[0:8], coded[8:16]
        stats.append(upper + pltpu.roll(upper, 4, 0) + low)
    row8 = lax.broadcasted_iota(jnp.int32, stats[0].shape, 0)
    peak = jnp.maximum(jnp.maximum(stats[0], stats[1]), jnp.maximum(stats[2], stats[3]))
    scales = [jnp.exp(jnp.where(row8 < head_n, s - peak, 0.0)) for s in stats]
    totals = [c * pltpu.roll(s, 8 - head_n, 0) for c, s in zip(scales, stats)]
    total = totals[0] + totals[1] + totals[2] + totals[3]
    total = jnp.where(row8 < head_n, total, 1.0)
    scales = [c / total for c in scales]
    packed = jnp.concatenate(scales + [jnp.zeros((part_rows - 32, part_rows), F32)], axis=0)
    turned = packed.T
    lane = lax.broadcasted_iota(jnp.int32, (part_rows, width), 1)
    result = jnp.zeros((part_rows, width), F32)
    for k, ref in enumerate((m0, m1, m2, m3)):
        scale = jnp.broadcast_to(turned[:, 8 * k : 8 * k + 1], (part_rows, width))
        for h in range(1, head_n):
            scale = jnp.where(
                lax.div(lane, HEAD_DIM) == h, turned[:, 8 * k + h : 8 * k + h + 1], scale
            )
        result = result + ref[pl.ds(0, part_rows)].astype(F32) * scale
    out_ref[...] = result.astype(BF16)


def swapped(x, axis, distance):
    return lax.ppermute(x, axis, [(i, i ^ distance) for i in range(lax.axis_size(axis))])


def per_device(
    pixels, w_stem, w_conv1, w_conv2, w_key, w_value, queries, tile_count, tissue, adjacency
):
    slot_n, area, patch = pixels.shape
    assert slot_n == 1
    side = int(round(area**0.5))
    half, quarter = side // 2, side // 4
    channels = w_stem.shape[1]
    groups, _, in1, out1 = w_conv1.shape
    _, _, in2, out2 = w_conv2.shape
    mid_n, out_n = groups * out1, groups * out2
    tokens = quarter * quarter
    border_rows = 4 * half + 16
    chunk_n = 4

    cells, border = pl.pallas_call(
        lambda *refs: stem_kernel(side, *refs),
        name="stem",
        out_shape=(
            jax.ShapeDtypeStruct((half * half, 4 * channels), BF16),
            jax.ShapeDtypeStruct((border_rows, 4 * channels), BF16),
        ),
        in_specs=[smem_spec(), smem_spec(), vmem_spec(), pl.BlockSpec(memory_space=pl.ANY)],
        out_specs=(vmem_spec(), vmem_spec()),
        scratch_shapes=[
            VMEM((area, patch), BF16),
            VMEM((area, 2 * channels), F32),
            pltpu.SemaphoreType.DMA((chunk_n,)),
        ],
        compiler_params=pltpu.CompilerParams(vmem_limit_bytes=20 * MIB),
    )(tile_count, adjacency, w_stem, pixels)

    line = ("tiles", "heads")
    line_n = lax.axis_size("tiles") * lax.axis_size("heads")
    second = lax.ppermute(border, line, [(i, i + 2) for i in range(line_n - 2)])
    partial, dense1, dense2 = pl.pallas_call(
        lambda *refs: conv_kernel(half, in1, *refs),
        name="conv",
        out_shape=(
            jax.ShapeDtypeStruct((half * half, mid_n), F32),
            jax.ShapeDtypeStruct((4 * channels, 4 * mid_n), BF16),
            jax.ShapeDtypeStruct((4 * mid_n, 4 * out_n), BF16),
        ),
        in_specs=[vmem_spec()] * 3,
        out_specs=(vmem_spec(),) * 3,
        scratch_shapes=[VMEM((half * half + half, 4 * mid_n), F32)],
        compiler_params=pltpu.CompilerParams(vmem_limit_bytes=20 * MIB),
        cost_estimate=pl.CostEstimate(flops=10**9, bytes_accessed=4 * 10**6, transcendentals=0),
    )(cells, w_conv1.reshape(groups * 9 * in1, out1), w_conv2.reshape(groups * 9 * in2, out2))

    odd = lax.rem(lax.axis_index(line), 2) == 1
    prior = lax.ppermute(
        jnp.where(odd, second, border), line, [(i, i ^ 1) for i in range(line_n)]
    )
    message = pl.pallas_call(
        token_kernel,
        name="token",
        out_shape=jax.ShapeDtypeStruct((tokens + 16, out_n), BF16),
        in_specs=[smem_spec()] * 3 + [vmem_spec()] * 5,
        out_specs=vmem_spec(),
        scratch_shapes=[
            VMEM((half * half, mid_n), F32),
            VMEM((2 * half, mid_n), F32),
            VMEM((tokens + 2 * quarter, 4 * mid_n), BF16),
            VMEM((tokens + 2 * quarter, 4 * out_n), F32),
            VMEM((out_n // 128, tokens, 128), F32),
        ],
        compiler_params=pltpu.CompilerParams(vmem_limit_bytes=20 * MIB),
    )(tile_count, tissue, adjacency, partial, prior, second, dense1, dense2)

    far = swapped(message, "heads", 2)
    near = swapped(message, "heads", 1)
    far_near = swapped(far, "heads", 1)

    tile_n = lax.axis_size("tiles")
    latent_n, width = queries.shape
    head_n = width // HEAD_DIM
    share = latent_n // tile_n
    few = tile_n == 4
    part_n = 4
    part_rows = latent_n // part_n
    place = lax.axis_index("tiles") if few else jnp.int32(0)
    parts = pl.pallas_call(
        attention_kernel,
        name="attention",
        out_shape=jax.ShapeDtypeStruct((part_n, part_rows + 16, width), BF16),
        in_specs=[smem_spec()] + [vmem_spec()] * 7,
        out_specs=vmem_spec(),
        scratch_shapes=[VMEM((4 * tokens, width), BF16), VMEM((4 * tokens, width), BF16)],
        compiler_params=pltpu.CompilerParams(vmem_limit_bytes=24 * MIB),
    )(place.astype(jnp.int32).reshape(1), message, near, far, far_near, w_key, w_value, queries)

    if few:
        received = [parts[0]] + [swapped(parts[k], "tiles", k) for k in range(1, 4)]
        return pl.pallas_call(
            lambda *refs: merge_kernel(head_n, *refs),
            name="merge",
            out_shape=jax.ShapeDtypeStruct((part_rows, width), BF16),
            in_specs=[vmem_spec()] * 4,
            out_specs=vmem_spec(),
        )(*received)
    coded = parts[:, part_rows:].astype(F32)
    stats = coded[:, 0:4] + coded[:, 4:8] + coded[:, 8:12]
    stats = stats.transpose(0, 2, 1).reshape(tile_n, share, 4)
    weighted = parts[:, :part_rows].reshape(tile_n, share, width)
    stats = lax.all_to_all(stats, "tiles", 0, 0)
    weighted = lax.all_to_all(weighted, "tiles", 0, 0).astype(F32)
    peaks, totals = stats[..., :head_n], stats[..., head_n : 2 * head_n]
    scale = jnp.exp(peaks - jnp.max(peaks, axis=0, keepdims=True))
    scale = scale / jnp.sum(scale * totals, axis=0, keepdims=True)
    return jnp.sum(weighted * jnp.repeat(scale, HEAD_DIM, axis=2), axis=0).astype(BF16)


def solution(mesh):
    in_specs = (
        P(("slides", "tiles", "heads"), None, None),
        P(),
        P(),
        P(),
        P(None, "heads"),
        P(None, "heads"),
        P(None, "heads"),
        P(("slides", "tiles", "heads")),
        P(("slides", "tiles", "heads")),
        P(("slides", "tiles", "heads"), None),
    )
    out_specs = P(("slides", "tiles"), "heads")
    return jax.shard_map(
        per_device, mesh=mesh, in_specs=in_specs, out_specs=out_specs, check_vma=False
    )
```

time: 161 us -> 42 us (0.26)
  local copies, waits for them, and re-layouts: 48.7 us -> 4.54 us
  blocking collectives: 39.4 us -> 0 us
  matrix products: 37.1 us -> 0 us
  between operations: 15.2 us -> 1.45 us
  other arithmetic: 10.8 us -> 0.01 us
  waiting for transfers between devices: 2.12 us -> 12.8 us
  Pallas kernels: 0 us -> 10.2 us
  starting transfers between devices: 6.87 us -> 12.7 us
    all_gather x4 -> x0, blocking collectives: 39.4 us -> none  [the longest x2 26.6 us: merged_2(): everything = jax.tree.map(lambda part: lax.all_gather(part, axis), array)]
    conv_general_dilated x2 -> x0, matrix products: 27.9 us -> none  [grouped_conv(): lax.conv_general_dilated(padded, kernel, window_strides=(2, 2), padding='...]
    concatenate x10 -> x0, local copies, waits for them, and re-layouts: 26.4 us -> none  [the longest x2 19.3 us: bordered(): return jnp.concatenate([first_line[:, None], lower], axis=1)]
    ppermute x2 -> x8, waiting for transfers between devices: 0.01 us -> 12.8 us  [the longest x6 11.1 us: swapped(): lax.ppermute(x, axis, [(i, i ^ distance) for i in range(lax.axis_size(axi...]
    convert_element_type x6 -> x0, local copies, waits for them, and re-layouts: 12.6 us -> none  [the longest x3 6.14 us: per_device(): stem_map = (jnp.maximum(stem_flat, 0.0).reshape(slot_n, STEM_GRID, STEM_G...]
    pallas_call x0 -> x5, Pallas kernels: none -> 10.2 us  [the longest x1 3.26 us: per_device(): pl.pallas_call(attention_kernel, name='attention', out_shape=jax.ShapeDty...]
    dot_general x19 -> x0, matrix products: 9.22 us -> none  [the longest x4 4.52 us: attend_rows(): jnp.dot(normed_rows, weight_both, preferred_element_type=jnp.float32)]
    ppermute x2 -> x8, starting transfers between devices: 6.87 us -> 12.7 us  [the longest x6 7.76 us: swapped(): lax.ppermute(x, axis, [(i, i ^ distance) for i in range(lax.axis_size(axi...]
  transfers between devices with their start and end apart: 3 -> 8, of which waited for: 1 -> 6; matrix products, arithmetic and copies ran while one was open for 7% -> 0% of each run, Pallas kernels for 0% -> 2%
where the time goes in v1:
time: 42 us; the launch traced here: 41.7 us
  waiting for transfers between devices  12.8 us (30%)
  starting transfers between devices  12.7 us (30%)
  Pallas kernels  10.2 us (24%)
  local copies, waits for them, and re-layouts  4.54 us (11%)
  between operations  1.45 us (3%)
    ppermute x6, waiting for transfers between devices, swapped(): lax.ppermute(x, axis, [(i, i ^ distance) for i in range(lax.axis_size(axi...  11.1 us
    ppermute x6, starting transfers between devices, swapped(): lax.ppermute(x, axis, [(i, i ^ distance) for i in range(lax.axis_size(axi...  7.76 us
    ppermute x1, starting transfers between devices, per_device(): second = lax.ppermute(border, line, [(i, i + 2) for i in range(line_n - 2)])  4.85 us
    unnamed x22, local copies, waits for them, and re-layouts  3.91 us
    pallas_call x1, Pallas kernels, per_device(): pl.pallas_call(attention_kernel, name='attention', out_shape=jax.ShapeDty...  3.26 us
    pallas_call x1, Pallas kernels, per_device(): pl.pallas_call(lambda *refs: stem_kernel(side, *refs), name='stem', out_s...  2.9 us
    pallas_call x1, Pallas kernels, per_device(): pl.pallas_call(lambda *refs: merge_kernel(head_n, *refs), name='merge', o...  1.8 us
    pallas_call x1, Pallas kernels, per_device(): pl.pallas_call(token_kernel, name='token', out_shape=jax.ShapeDtypeStruct...  1.49 us
  transfers between devices with their start and end apart: 8, of which 6 were waited for; matrix products, arithmetic and copies ran while one was open for 0% of the time, Pallas kernels for 2%

profile of v1, /device:TPU:0, one launch (start us, length us, event | category | flops | bytes accessed | tf_op | source)
XLA Modules:
  0.0 41.7 jit_solution(3835119619744358072)
XLA Ops:
  0.0 0.0 copy-start.9
  0.0 0.0 copy-start.3
  0.7 3.2 %copy.12.refs_3_ = bf16[1,4096,192]{2,1,0:T(8,128)(2,1)S(1)} copy(bf16[1,4096,192]{1,2,0:T(8,128)(2,1)} %param.10) | data formatting | bytes 3145728 | tf_op args[0]
  3.8 0.0 copy-done.9
  3.8 0.0 copy-start.4
  3.8 0.0 copy-start.5
  3.9 0.1 copy.11.refs_2_
  4.0 0.0 copy-done.3
  4.0 2.9 %stem.1 = (bf16[1024,256]{1,0:T(8,128)(2,1)S(1)}, bf16[144,256]{1,0:T(8,128)(2,1)S(1)}) custom-call(s32[1]{0:T(128)S(6)} %copy.13.refs_0_.count_ref, s32[1,3]{1,0:T(1,128)S(1)} %copy-done.3, bf16[192,64]{1,0:T(8,128)(2,1)S(1)} %copy.11.refs_2_, bf16[1,4096,192]{2,1,0:T(8,128)(2,1)S(1)} %copy.12.refs_3_), custom_call_target="tpu_custom_call" | custom-call | tf_op jit(solution)/shard_map/stem/pallas_call | solution.py:319
  6.9 4.8 %collective-permute-start = (bf16[144,256]{1,0:T(8,128)(2,1)S(1)}, bf16[144,256]{1,0:T(8,128)(2,1)S(1)}, u32[]{:S(2)}, u32[]{:S(2)}) collective-permute-start(bf16[144,256]{1,0:T(8,128)(2,1)S(1)} %get-tuple-element.12), channel_id=1, source_target_pairs={{0,2},{1,3},{2,4},{3,5},{4,6},{5,7},{6,8},{7,9},{8,10},{9,11},{10,... | collective-permute-start | bytes 221192 | tf_op jit(solution)/shard_map/ppermute | solution.py:338
  12.4 1.3 %collective-permute-done.second_ref = bf16[144,256]{1,0:T(8,128)(2,1)S(1)} collective-permute-done((bf16[144,256]{1,0:T(8,128)(2,1)S(1)}, bf16[144,256]{1,0:T(8,128)(2,1)S(1)}, u32[]{:S(2)}, u32[]{:S(2)}) %collective-permute-start) | collective-permute-done | bytes 73760 | tf_op jit(solution)/shard_map/ppermute | solution.py:338
  13.7 0.1 collective-permute-start.1
  13.8 0.0 copy-done.4
  13.8 0.0 copy-done.5
  13.8 0.0 copy-start
  13.8 0.0 copy-start.1
  13.8 0.0 copy-start.2
  13.9 0.8 %conv.1 = (f32[1024,128]{1,0:T(8,128)S(1)}, bf16[256,512]{1,0:T(8,128)(2,1)S(1)}, bf16[512,1024]{1,0:T(8,128)(2,1)S(1)}) custom-call(bf16[1024,256]{1,0:T(8,128)(2,1)S(1)} %get-tuple-element.10.refs_0_, bf16[576,32]{1,0:T(8,128)(2,1)S(1)} %bitcast.12, bf16[1152,64]{1,0:T(8,128)(2,1)S(1)} %bitcast.11), custom_call_target="tpu_custom_call" | custom-call | flops 1000000000 | bytes 4000000 | tf_op jit(solution)/shard_map/conv/pallas_call | solution.py:339
  14.6 0.4 collective-permute-done.1.prior_ref
  15.1 1.5 %token_.1.t0 = bf16[272,256]{1,0:T(8,128)(2,1)S(1)} custom-call(s32[1]{0:T(128)S(6)} %copy.13.refs_0_.count_ref, s32[1]{0:T(128)S(6)} %copy.14.tissue_ref, s32[1,3]{1,0:T(1,128)S(1)} %copy-done.3, f32[1024,128]{1,0:T(8,128)S(1)} %get-tuple-element.11.partial_ref, bf16[144,256]{1,0:T(8,128)(2,1)S(1)} %collective-permute-done.1.prior_ref, ...), custom_call_target="tpu_custom_call" | custom-call | tf_op jit(solution)/shard_map/token/pallas_call | solution.py:358
  16.5 2.4 %collective-permute-start.3 = (bf16[272,256]{1,0:T(8,128)(2,1)S(1)}, bf16[272,256]{1,0:T(8,128)(2,1)S(1)}, u32[]{:S(2)}, u32[]{:S(2)}) collective-permute-start(bf16[272,256]{1,0:T(8,128)(2,1)S(1)} %token_.1.t0), channel_id=1, source_target_pairs={{0,2},{1,3},{2,0},{3,1},{4,6},{5,7},{6,4},{7,5},{8,10},{9,11},{10,... | collective-permute-start | bytes 417800 | tf_op jit(solution)/shard_map/ppermute | solution.py:301
  19.0 0.0 collective-permute-start.2
  19.0 4.0 %collective-permute-done.3.t2 = bf16[272,256]{1,0:T(8,128)(2,1)S(1)} collective-permute-done((bf16[272,256]{1,0:T(8,128)(2,1)S(1)}, bf16[272,256]{1,0:T(8,128)(2,1)S(1)}, u32[]{:S(2)}, u32[]{:S(2)}) %collective-permute-start.3) | collective-permute-done | bytes 139296 | tf_op jit(solution)/shard_map/ppermute | solution.py:301
  23.0 0.0 collective-permute-start.4
  23.0 0.0 collective-permute-done.2.t1
  23.0 1.4 %collective-permute-done.4.t3 = bf16[272,256]{1,0:T(8,128)(2,1)S(1)} collective-permute-done((bf16[272,256]{1,0:T(8,128)(2,1)S(1)}, bf16[272,256]{1,0:T(8,128)(2,1)S(1)}, u32[]{:S(2)}, u32[]{:S(2)}) %collective-permute-start.4) | collective-permute-done | bytes 139296 | tf_op jit(solution)/shard_map/ppermute | solution.py:301
  24.3 0.0 copy-done
  24.3 0.0 copy-done.1
  24.3 0.0 copy-done.2
  24.3 3.3 %attention.1 = bf16[4,144,128]{2,1,0:T(8,128)(2,1)S(1)} custom-call(s32[1]{0:T(128)} %bitcast.place_ref, bf16[272,256]{1,0:T(8,128)(2,1)S(1)} %token_.1.t0, bf16[272,256]{1,0:T(8,128)(2,1)S(1)} %collective-permute-done.2.t1, bf16[272,256]{1,0:T(8,128)(2,1)S(1)} %collective-permute-done.3.t2, bf16[272,256]{1,0:T(8,128)(2,1)S(1)} %collective-permute-done.4.t3, ...), custom_call_target="tpu_custom_call" | custom-call | tf_op jit(solution)/shard_map/attention/pallas_call | solution.py:386
  27.6 0.6 %slice_bitcast_fusion = (bf16[144,128]{1,0:T(8,128)(2,1)S(1)}, bf16[144,128]{1,0:T(8,128)(2,1)S(1)}, bf16[144,128]{1,0:T(8,128)(2,1)S(1)}, bf16[144,128]{1,0:T(8,128)(2,1)}) fusion(bf16[4,144,128]{2,1,0:T(8,128)(2,1)S(1)} %attention.1), kind=kLoop, calls=%fused_computation.1 | loop fusion | bytes 294912 | tf_op jit(solution)/shard_map/squeeze | solution.py:397
  28.2 2.7 %collective-permute-start.5 = (bf16[144,128]{1,0:T(8,128)(2,1)S(1)}, bf16[144,128]{1,0:T(8,128)(2,1)S(1)}, u32[]{:S(2)}, u32[]{:S(2)}) collective-permute-start(bf16[144,128]{1,0:T(8,128)(2,1)S(1)} %get-tuple-element.17), channel_id=1, source_target_pairs={{0,4},{4,0},{8,12},{12,8},{1,5},{5,1},{9,13},{13,9},{2,6},{6,2},{1... | collective-permute-start | bytes 110600 | tf_op jit(solution)/shard_map/ppermute | solution.py:301
  31.0 2.6 %collective-permute-start.6 = (bf16[144,128]{1,0:T(8,128)(2,1)S(1)}, bf16[144,128]{1,0:T(8,128)(2,1)S(1)}, u32[]{:S(2)}, u32[]{:S(2)}) collective-permute-start(bf16[144,128]{1,0:T(8,128)(2,1)S(1)} %get-tuple-element.16), channel_id=1, source_target_pairs={{0,8},{4,12},{8,0},{12,4},{1,9},{5,13},{9,1},{13,5},{2,10},{6,14},... | collective-permute-start | bytes 110600 | tf_op jit(solution)/shard_map/ppermute | solution.py:301
  33.6 0.0 collective-permute-start.7
  33.6 0.0 collective-permute-done.5.refs_1_
  33.6 0.0 copy-start.6
  33.6 3.0 %collective-permute-done.6.refs_2_ = bf16[144,128]{1,0:T(8,128)(2,1)S(1)} collective-permute-done((bf16[144,128]{1,0:T(8,128)(2,1)S(1)}, bf16[144,128]{1,0:T(8,128)(2,1)S(1)}, u32[]{:S(2)}, u32[]{:S(2)}) %collective-permute-start.6) | collective-permute-done | bytes 36896 | tf_op jit(solution)/shard_map/ppermute | solution.py:301
  36.5 0.0 copy-start.7
  36.6 2.8 %collective-permute-done.7.refs_3_ = bf16[144,128]{1,0:T(8,128)(2,1)S(1)} collective-permute-done((bf16[144,128]{1,0:T(8,128)(2,1)S(1)}, bf16[144,128]{1,0:T(8,128)(2,1)S(1)}, u32[]{:S(2)}, u32[]{:S(2)}) %collective-permute-start.7) | collective-permute-done | bytes 36896 | tf_op jit(solution)/shard_map/ppermute | solution.py:301
  39.3 0.0 copy-start.8
  39.3 0.0 copy-done.6
  39.3 0.0 copy-done.7
  39.3 0.6 %copy-done.8 = bf16[144,128]{1,0:T(8,128)(2,1)} copy-done((bf16[144,128]{1,0:T(8,128)(2,1)}, bf16[144,128]{1,0:T(8,128)(2,1)S(1)}, u32[]{:S(2)}) %copy-start.8) | copy-done | bytes 36888
  39.9 1.8 %merge.1 = bf16[128,128]{1,0:T(8,128)(2,1)} custom-call(bf16[144,128]{1,0:T(8,128)(2,1)} %get-tuple-element.18.refs_0_, bf16[144,128]{1,0:T(8,128)(2,1)} %copy-done.6, bf16[144,128]{1,0:T(8,128)(2,1)} %copy-done.7, bf16[144,128]{1,0:T(8,128)(2,1)} %copy-done.8), custom_call_target="tpu_custom_call" | custom-call | tf_op jit(solution)/shard_map/merge/pallas_call | solution.py:398
  (1 shorter events, 0.0 us)
Async XLA Ops:
  0.0 3.8 %copy-start.9 = (bf16[192,64]{0,1:T(8,128)(2,1)S(1)}, bf16[192,64]{0,1:T(8,128)(2,1)}, u32[]{:S(2)}) copy-start(bf16[192,64]{0,1:T(8,128)(2,1)} %param.11) | copy-start | bytes 73732
  0.0 4.0 %copy-start.3 = (s32[1,3]{1,0:T(1,128)S(1)}, s32[1,3]{1,0:T(1,128)}, u32[]{:S(2)}) copy-start(s32[1,3]{1,0:T(1,128)} %adjacency_ref.1) | copy-start | bytes 40
  3.8 10.0 %copy-start.4 = (bf16[4,9,32,64]{3,2,1,0:T(8,128)(2,1)S(1)}, bf16[4,9,32,64]{3,2,1,0:T(8,128)(2,1)}, u32[]{:S(2)}) copy-start(bf16[4,9,32,64]{3,2,1,0:T(8,128)(2,1)} %param.13) | copy-start | bytes 442372
  3.8 10.0 %copy-start.5 = (bf16[4,9,16,32]{3,2,1,0:T(8,128)(2,1)S(1)}, bf16[4,9,16,32]{3,2,1,0:T(8,128)(2,1)}, u32[]{:S(2)}) copy-start(bf16[4,9,16,32]{3,2,1,0:T(8,128)(2,1)} %param.12) | copy-start | bytes 110596
  6.9 6.8 %collective-permute-start = (bf16[144,256]{1,0:T(8,128)(2,1)S(1)}, bf16[144,256]{1,0:T(8,128)(2,1)S(1)}, u32[]{:S(2)}, u32[]{:S(2)}) collective-permute-start(bf16[144,256]{1,0:T(8,128)(2,1)S(1)} %get-tuple-element.12), channel_id=1, source_target_pairs={{0,2},{1,3},{2,4},{3,5},{4,6},{5,7},{6,8},{7,9},{8,10},{9,11},{10,... | collective-permute-start | bytes 221192 | tf_op jit(solution)/shard_map/ppermute | solution.py:338
  13.7 1.3 %collective-permute-start.1 = (bf16[144,256]{1,0:T(8,128)(2,1)S(1)}, bf16[144,256]{1,0:T(8,128)(2,1)S(1)}, u32[]{:S(2)}, u32[]{:S(2)}) collective-permute-start(bf16[144,256]{1,0:T(8,128)(2,1)S(1)} %broadcast_select_fusion), channel_id=1, source_target_pairs={{0,1},{1,0},{2,3},{3,2},{4,5},{5,4},{6,7},{7,6},{8,9},{9,8},{10,11... | collective-permute-start | bytes 221192 | tf_op jit(solution)/shard_map/ppermute | solution.py:355
  13.8 10.5 %copy-start = (bf16[512,128]{1,0:T(8,128)(2,1)S(1)}, bf16[512,128]{1,0:T(8,128)(2,1)}, u32[]{:S(2)}) copy-start(bf16[512,128]{1,0:T(8,128)(2,1)} %q_ref.1) | copy-start | bytes 393220
  13.8 10.5 %copy-start.1 = (bf16[256,128]{1,0:T(8,128)(2,1)S(1)}, bf16[256,128]{1,0:T(8,128)(2,1)}, u32[]{:S(2)}) copy-start(bf16[256,128]{1,0:T(8,128)(2,1)} %wk_ref.1) | copy-start | bytes 196612
  13.8 10.5 %copy-start.2 = (bf16[256,128]{1,0:T(8,128)(2,1)S(1)}, bf16[256,128]{1,0:T(8,128)(2,1)}, u32[]{:S(2)}) copy-start(bf16[256,128]{1,0:T(8,128)(2,1)} %wv_ref.1) | copy-start | bytes 196612
  16.5 6.4 %collective-permute-start.3 = (bf16[272,256]{1,0:T(8,128)(2,1)S(1)}, bf16[272,256]{1,0:T(8,128)(2,1)S(1)}, u32[]{:S(2)}, u32[]{:S(2)}) collective-permute-start(bf16[272,256]{1,0:T(8,128)(2,1)S(1)} %token_.1.t0), channel_id=1, source_target_pairs={{0,2},{1,3},{2,0},{3,1},{4,6},{5,7},{6,4},{7,5},{8,10},{9,11},{10,... | collective-permute-start | bytes 417800 | tf_op jit(solution)/shard_map/ppermute | solution.py:301
  19.0 4.0 %collective-permute-start.2 = (bf16[272,256]{1,0:T(8,128)(2,1)S(1)}, bf16[272,256]{1,0:T(8,128)(2,1)S(1)}, u32[]{:S(2)}, u32[]{:S(2)}) collective-permute-start(bf16[272,256]{1,0:T(8,128)(2,1)S(1)} %token_.1.t0), channel_id=1, source_target_pairs={{0,1},{1,0},{2,3},{3,2},{4,5},{5,4},{6,7},{7,6},{8,9},{9,8},{10,11... | collective-permute-start | bytes 417800 | tf_op jit(solution)/shard_map/ppermute | solution.py:301
  23.0 1.4 %collective-permute-start.4 = (bf16[272,256]{1,0:T(8,128)(2,1)S(1)}, bf16[272,256]{1,0:T(8,128)(2,1)S(1)}, u32[]{:S(2)}, u32[]{:S(2)}) collective-permute-start(bf16[272,256]{1,0:T(8,128)(2,1)S(1)} %collective-permute-done.3.t2), channel_id=1, source_target_pairs={{0,1},{1,0},{2,3},{3,2},{4,5},{5,4},{6,7},{7,6},{8,9},{9,8},{10,11... | collective-permute-start | bytes 417800 | tf_op jit(solution)/shard_map/ppermute | solution.py:301
  28.2 5.3 %collective-permute-start.5 = (bf16[144,128]{1,0:T(8,128)(2,1)S(1)}, bf16[144,128]{1,0:T(8,128)(2,1)S(1)}, u32[]{:S(2)}, u32[]{:S(2)}) collective-permute-start(bf16[144,128]{1,0:T(8,128)(2,1)S(1)} %get-tuple-element.17), channel_id=1, source_target_pairs={{0,4},{4,0},{8,12},{12,8},{1,5},{5,1},{9,13},{13,9},{2,6},{6,2},{1... | collective-permute-start | bytes 110600 | tf_op jit(solution)/shard_map/ppermute | solution.py:301
  31.0 5.6 %collective-permute-start.6 = (bf16[144,128]{1,0:T(8,128)(2,1)S(1)}, bf16[144,128]{1,0:T(8,128)(2,1)S(1)}, u32[]{:S(2)}, u32[]{:S(2)}) collective-permute-start(bf16[144,128]{1,0:T(8,128)(2,1)S(1)} %get-tuple-element.16), channel_id=1, source_target_pairs={{0,8},{4,12},{8,0},{12,4},{1,9},{5,13},{9,1},{13,5},{2,10},{6,14},... | collective-permute-start | bytes 110600 | tf_op jit(solution)/shard_map/ppermute | solution.py:301
  33.6 5.8 %collective-permute-start.7 = (bf16[144,128]{1,0:T(8,128)(2,1)S(1)}, bf16[144,128]{1,0:T(8,128)(2,1)S(1)}, u32[]{:S(2)}, u32[]{:S(2)}) collective-permute-start(bf16[144,128]{1,0:T(8,128)(2,1)S(1)} %get-tuple-element.15), channel_id=1, source_target_pairs={{0,12},{4,8},{8,4},{12,0},{1,13},{5,9},{9,5},{13,1},{2,14},{6,10},... | collective-permute-start | bytes 110600 | tf_op jit(solution)/shard_map/ppermute | solution.py:301
  33.6 5.8 %copy-start.6 = (bf16[144,128]{1,0:T(8,128)(2,1)}, bf16[144,128]{1,0:T(8,128)(2,1)S(1)}, u32[]{:S(2)}) copy-start(bf16[144,128]{1,0:T(8,128)(2,1)S(1)} %collective-permute-done.5.refs_1_) | copy-start | bytes 110596
  36.5 2.8 %copy-start.7 = (bf16[144,128]{1,0:T(8,128)(2,1)}, bf16[144,128]{1,0:T(8,128)(2,1)S(1)}, u32[]{:S(2)}) copy-start(bf16[144,128]{1,0:T(8,128)(2,1)S(1)} %collective-permute-done.6.refs_2_) | copy-start | bytes 110596
  39.3 0.6 %copy-start.8 = (bf16[144,128]{1,0:T(8,128)(2,1)}, bf16[144,128]{1,0:T(8,128)(2,1)S(1)}, u32[]{:S(2)}) copy-start(bf16[144,128]{1,0:T(8,128)(2,1)S(1)} %collective-permute-done.7.refs_3_) | copy-start | bytes 110596

commit v2 on v1

--- a/solution.py
+++ b/solution.py
@@ -13,6 +13,7 @@
 VMEM = pltpu.VMEM
 SMEM = pltpu.SMEM
 MIB = 1 << 20
+STEM_VMEM = 60 * MIB
 
 
 def vmem_spec():
@@ -52,51 +53,60 @@
     return jnp.where(row == 0, 0.0, pltpu.roll(x, 1, 0))
 
 
-def stem_kernel(side, count_ref, adjacency_ref, w_ref, pixels_hbm, cells_ref, border_ref,
-                pixels, stem, sems):
-    chunk_n = sems.shape[0]
-    rows = pixels.shape[0] // chunk_n
+def stem_kernel(side, count_any, tissue_any, adjacency_any, w_any, pixels_any, cells_ref,
+                border_ref, tiny_ref, facts_ref, count, tissue, adjacency, weight, pixels,
+                even_lines, odd_lines, sems):
     copies = [
-        pltpu.make_async_copy(
-            pixels_hbm.at[0, pl.ds(k * rows, rows)], pixels.at[pl.ds(k * rows, rows)], sems.at[k]
-        )
-        for k in range(chunk_n)
+        pltpu.make_async_copy(source, target, sems.at[k])
+        for k, (source, target) in enumerate((
+            (pixels_any, pixels), (w_any, weight), (count_any, count), (tissue_any, tissue),
+            (adjacency_any, adjacency),
+        ))
     ]
     for copy in copies:
         copy.start()
-    live = (count_ref[0] > 0).astype(F32)
-    weight = w_ref[...]
-    channels = weight.shape[1]
-    doubled = jnp.concatenate([weight, weight], axis=1)
-    half = side // 2
-    lane = lax.broadcasted_iota(jnp.int32, (half, 2 * channels), 1)
-    left = lane < channels
-    lines = rows // side
-    for k in range(chunk_n):
-        copies[k].wait()
-        out = jnp.dot(pixels[pl.ds(k * rows, rows)], doubled, preferred_element_type=F32)
-        stem[pl.ds(k * rows, rows)] = jnp.maximum(out, 0.0) * live
-        for y in range(k * lines, (k + 1) * lines):
-            even = stem[pl.ds(y * side, half, stride=2)]
-            odd = stem[pl.ds(y * side + 1, half, stride=2)]
-            cells_ref[pl.ds((y // 2) * half, half), pl.ds((y % 2) * 2 * channels, 2 * channels)] = (
-                jnp.where(left, even, odd).astype(BF16)
-            )
+    channels, half = weight.shape[0], side // 2
+    rows, span = 4 * half, 4 * side
+    row = lax.broadcasted_iota(jnp.int32, (rows, 2 * span), 0)
+    column = lax.broadcasted_iota(jnp.int32, (rows, 2 * span), 1)
+    line = 2 * lax.div(lax.rem(row, 2 * half), half) + lax.div(row, 2 * half)
+    wanted = line * side + 2 * lax.rem(row, half)
+    pick = (lax.rem(column, span) == wanted + lax.div(column, span)).astype(BF16)
+    for copy in copies:
+        copy.wait()
+    live = (count[0, 0] > 0).astype(F32)
+    gates = [(adjacency[0, k] == 0).astype(F32) for k in range(3)]
+    row = lax.broadcasted_iota(jnp.int32, facts_ref.shape, 0)
+    facts = jnp.zeros(facts_ref.shape, F32)
+    for k, fact in enumerate([live] + gates + [live * tissue[0, 0].astype(F32)]):
+        facts = jnp.where(row == k, fact, facts)
+    facts_ref[...] = facts.astype(BF16)
+    flat = jnp.dot(weight[...], pixels[0], preferred_element_type=F32)
+    flat = (jnp.maximum(flat, 0.0) * live).astype(BF16)
+    blank = jnp.zeros((channels, span), BF16)
+    for k in range(side // 4):
+        four = flat[:, k * span : (k + 1) * span]
+        both = jnp.concatenate(
+            [jnp.concatenate([four, blank], axis=0), jnp.concatenate([blank, four], axis=0)],
+            axis=1,
+        )
+        sorted_ = lax.dot_general(
+            pick, both, (((1,), (1,)), ((), ())), preferred_element_type=F32
+        )
+        here = pl.ds(k * 2 * half, 2 * half)
+        even_lines[here] = sorted_[: 2 * half]
+        odd_lines[here] = sorted_[2 * half :]
+        cells_ref[here, pl.ds(0, 2 * channels)] = sorted_[: 2 * half].astype(BF16)
+        cells_ref[here, pl.ds(2 * channels, 2 * channels)] = sorted_[2 * half :].astype(BF16)
     border_ref[pl.ds(0, 2 * half)] = cells_ref[pl.ds((half - 2) * half, 2 * half)]
     for which in range(2):
-        x = side - 4 + 2 * which
-        for py in range(2):
-            even = stem[pl.ds(py * side + x, half, stride=2 * side)]
-            odd = stem[pl.ds(py * side + x + 1, half, stride=2 * side)]
+        for py, lines in enumerate((even_lines, odd_lines)):
             border_ref[
                 pl.ds((2 + which) * half, half), pl.ds(py * 2 * channels, 2 * channels)
-            ] = jnp.where(left, even, odd).astype(BF16)
-    facts = border_ref.shape[0] - 4 * half
-    row = lax.broadcasted_iota(jnp.int32, (facts, border_ref.shape[1]), 0)
-    above = (adjacency_ref[0, 0] == 0).astype(F32)
-    beside = (adjacency_ref[0, 1] == 0).astype(F32)
-    told = jnp.where(row == 0, live, jnp.where(row == 1, above, jnp.where(row == 2, beside, 0.0)))
-    border_ref[pl.ds(4 * half, facts)] = told.astype(BF16)
+            ] = lines[pl.ds(half - 2 + which, half, stride=half)].astype(BF16)
+    border_ref[pl.ds(4 * half, 16)] = facts_ref[...]
+    tiny_ref[pl.ds(0, 16)] = cells_ref[pl.ds((half - 1) * half - 16, 16)]
+    tiny_ref[pl.ds(16, 16)] = cells_ref[pl.ds(half * half - 16, 16)]
 
 
 def conv_kernel(half, in_group, cells_ref, w1_ref, w2_ref, partial_ref, dense1_ref, dense2_ref,
@@ -121,21 +131,20 @@
     expand_weights(w2_ref[...], w2_ref.shape[0] // 36, w2_ref.shape[1], dense2_ref)
 
 
-def token_kernel(count_ref, tissue_ref, adjacency_ref, partial_ref, prior_ref, second_ref,
-                 dense1_ref, dense2_ref, token_ref, middle, lines, cells, wide, whole):
+def token_kernel(facts_ref, partial_ref, prior_ref, second_ref, dense1_ref,
+                 dense2_ref, token_ref, middle, lines, cells, wide, whole):
     positions, channels = partial_ref.shape
     half = 32
     while half * half > positions:
         half //= 2
     quarter = half // 2
-    live = (count_ref[0] > 0).astype(F32)
-    above = (adjacency_ref[0, 0] == 0).astype(F32)
-    beside = (adjacency_ref[0, 1] == 0).astype(F32)
-    corner = (adjacency_ref[0, 2] == 0).astype(F32)
+    live, above, beside, corner, known = [
+        facts_ref[pl.ds(0, 16), pl.ds(0, 1)].astype(F32)[k : k + 1] for k in range(5)
+    ]
     lane = [slice(b * channels, (b + 1) * channels) for b in range(4)]
     dense1 = dense1_ref[...]
     prior = jnp.dot(prior_ref[pl.ds(0, 4 * half)], dense1, preferred_element_type=F32)
-    second = jnp.dot(second_ref[pl.ds(0, 2 * half)], dense1, preferred_element_type=F32)
+    second = jnp.dot(second_ref[...], dense1, preferred_element_type=F32)
     facts = prior_ref[pl.ds(4 * half, 16), pl.ds(0, channels)].astype(F32)
     live_prior, above_prior, beside_prior = facts[0:1], facts[1:2], facts[2:3]
     row_30 = prior[0:half]
@@ -152,9 +161,7 @@
     side_sum = side_sum + jnp.where(at_zero, top, 0.0)
     middle[pl.ds(0, half)] = jnp.maximum(top_sum, 0.0) * live
     middle[pl.ds(0, half, stride=half)] = jnp.maximum(side_sum, 0.0) * live
-    last = second[2 * half - 1 : 2 * half]
-    over_last = second[half - 1 : half]
-    left_last = second[2 * half - 2 : 2 * half - 1]
+    over_last, left_last, last = second[15:16], second[30:31], second[31:32]
     row_sum = row_31[:, lane[0]] + row_30[:, lane[2]]
     row_sum = row_sum + shifted_down(row_31[:, lane[1]] + row_30[:, lane[3]])
     row_sum = row_sum + jnp.where(
@@ -213,14 +220,15 @@
     centred = deep - jnp.mean(deep, axis=1, keepdims=True)
     spread = jnp.mean(centred * centred, axis=1, keepdims=True)
     token_ref[pl.ds(0, tokens)] = (centred * lax.rsqrt(spread + LN_EPS)).astype(BF16)
-    known = (live * tissue_ref[0].astype(F32)) * jnp.ones((16, out_n), F32)
-    token_ref[pl.ds(tokens, 16)] = known.astype(BF16)
-
-
-def attention_kernel(place_ref, t0, t1, t2, t3, wk_ref, wv_ref, q_ref, out_ref, keys, values):
+    token_ref[pl.ds(tokens, 16)] = jnp.broadcast_to(known, (16, out_n)).astype(BF16)
+
+
+def attention_kernel(place_ref, t0, t1, t2, t3, wk_ref, wv_ref, q_ref, *rest):
+    out_refs, (keys, values, sums, facts_all) = rest[:-4], rest[-4:]
     token_refs = (t0, t1, t2, t3)
     tokens = t0.shape[0] - 16
-    width = wk_ref.shape[1]
+    latent_n, width = q_ref.shape
+    head_n = width // HEAD_DIM
     both = jnp.concatenate([wk_ref[...], wv_ref[...]], axis=1)
     masks = []
     lane_token = lax.broadcasted_iota(jnp.int32, (1, tokens), 1).astype(F32)
@@ -231,69 +239,65 @@
         known = ref[pl.ds(tokens, 16), pl.ds(0, tokens)].astype(F32)[0:1]
         masks.append(jnp.where(lane_token < known, 0.0, NEG_BIG))
     bias = jnp.concatenate(masks, axis=1)
-    place = place_ref[0]
-    part_n, part_rows = out_ref.shape[0], out_ref.shape[1] - 16
+    part_rows = latent_n // len(out_refs)
     lane = lax.broadcasted_iota(jnp.int32, (part_rows, width), 1)
-    row8 = lax.broadcasted_iota(jnp.int32, (8, part_rows), 0)
     key_all = keys[...]
     value_all = values[...]
-    for k in range(part_n):
-        part = place ^ k
-        q = q_ref[pl.ds(pl.multiple_of(part * part_rows, part_rows), part_rows)].astype(F32)
-        q = q * (float(HEAD_DIM) ** -0.5)
-        joined = None
+    for k in range(len(out_refs)):
+        here = pl.ds(k * part_rows, part_rows)
+        q = q_ref[here].astype(F32) * (float(HEAD_DIM) ** -0.5)
+        q = jnp.concatenate(
+            [jnp.where(lax.div(lane, HEAD_DIM) == h, q, 0.0) for h in range(head_n)], axis=0
+        ).astype(BF16)
+        scores = lax.dot_general(
+            q, key_all, (((1,), (1,)), ((), ())), preferred_element_type=F32
+        )
+        scores = scores + bias
+        peak = jnp.max(scores, axis=1, keepdims=True)
+        weights = jnp.exp(scores - peak)
+        total = jnp.sum(weights, axis=1, keepdims=True)
+        summed = jnp.dot(weights.astype(BF16), value_all, preferred_element_type=F32)
+        joined = summed[:part_rows]
         facts = jnp.zeros((part_rows, width), F32)
-        head_n = width // HEAD_DIM
         for h in range(head_n):
-            mine = lax.div(lane, HEAD_DIM) == h
-            q_h = jnp.where(mine, q, 0.0).astype(BF16)
-            scores = lax.dot_general(
-                q_h, key_all, (((1,), (1,)), ((), ())), preferred_element_type=F32
-            )
-            scores = scores + bias
-            peak = jnp.max(scores, axis=1, keepdims=True)
-            weights = jnp.exp(scores - peak)
-            total = jnp.sum(weights, axis=1, keepdims=True)
-            summed = jnp.dot(weights.astype(BF16), value_all, preferred_element_type=F32)
-            joined = summed if joined is None else jnp.where(mine, summed, joined)
-            facts = jnp.where(lane == h, peak, facts)
-            facts = jnp.where(lane == head_n + h, total, facts)
-        out_ref[k, pl.ds(0, part_rows)] = joined.astype(BF16)
-        turned = facts.T[0:8]
-        high = turned.astype(BF16).astype(F32)
-        rest = turned - high
-        mid = rest.astype(BF16).astype(F32)
-        low = rest - mid
-        upper = jnp.where(row8 < 4, high, pltpu.roll(mid, 4, 0))
-        out_ref[k, pl.ds(part_rows, 16)] = jnp.concatenate([upper, low], axis=0).astype(BF16)
-
-
-def merge_kernel(head_n, m0, m1, m2, m3, out_ref):
-    part_rows = out_ref.shape[0]
-    width = out_ref.shape[1]
-    stats = []
-    for ref in (m0, m1, m2, m3):
-        coded = ref[pl.ds(part_rows, 16)].astype(F32)
-        upper, low = coded[0:8], coded[8:16]
-        stats.append(upper + pltpu.roll(upper, 4, 0) + low)
+            mine = slice(h * part_rows, (h + 1) * part_rows)
+            joined = jnp.where(lax.div(lane, HEAD_DIM) == h, summed[mine], joined)
+            facts = jnp.where(lane == h, peak[mine], facts)
+            facts = jnp.where(lane == head_n + h, total[mine], facts)
+        sums[here] = joined
+        facts_all[here] = facts
+    for k, out_ref in enumerate(out_refs):
+        part = place_ref[0] ^ k
+        there = pl.ds(pl.multiple_of(part * part_rows, part_rows), part_rows)
+        out_ref[pl.ds(0, part_rows)] = sums[there]
+        out_ref[pl.ds(part_rows, 8)] = facts_all[there].T[0:8]
+
+
+def merge_kernel(head_n, *refs):
+    in_refs, out_ref = refs[:-1], refs[-1]
+    part_rows, width = out_ref.shape
+    stats = [ref[pl.ds(part_rows, 8)] for ref in in_refs]
     row8 = lax.broadcasted_iota(jnp.int32, stats[0].shape, 0)
-    peak = jnp.maximum(jnp.maximum(stats[0], stats[1]), jnp.maximum(stats[2], stats[3]))
+    peak = stats[0]
+    for s in stats[1:]:
+        peak = jnp.maximum(peak, s)
     scales = [jnp.exp(jnp.where(row8 < head_n, s - peak, 0.0)) for s in stats]
-    totals = [c * pltpu.roll(s, 8 - head_n, 0) for c, s in zip(scales, stats)]
-    total = totals[0] + totals[1] + totals[2] + totals[3]
+    total = scales[0] * pltpu.roll(stats[0], 8 - head_n, 0)
+    for c, s in zip(scales[1:], stats[1:]):
+        total = total + c * pltpu.roll(s, 8 - head_n, 0)
     total = jnp.where(row8 < head_n, total, 1.0)
     scales = [c / total for c in scales]
-    packed = jnp.concatenate(scales + [jnp.zeros((part_rows - 32, part_rows), F32)], axis=0)
-    turned = packed.T
+    blank = jnp.zeros((part_rows - 8 * len(scales), part_rows), F32)
+    turned = jnp.concatenate(scales + [blank], axis=0).T
     lane = lax.broadcasted_iota(jnp.int32, (part_rows, width), 1)
     result = jnp.zeros((part_rows, width), F32)
-    for k, ref in enumerate((m0, m1, m2, m3)):
-        scale = jnp.broadcast_to(turned[:, 8 * k : 8 * k + 1], (part_rows, width))
+    for k, ref in enumerate(in_refs):
+        scale = turned[:, 8 * k : 8 * k + 1]
         for h in range(1, head_n):
             scale = jnp.where(
                 lax.div(lane, HEAD_DIM) == h, turned[:, 8 * k + h : 8 * k + h + 1], scale
             )
-        result = result + ref[pl.ds(0, part_rows)].astype(F32) * scale
+        result = result + ref[pl.ds(0, part_rows)] * scale
     out_ref[...] = result.astype(BF16)
 
 
@@ -314,28 +318,38 @@
     mid_n, out_n = groups * out1, groups * out2
     tokens = quarter * quarter
     border_rows = 4 * half + 16
-    chunk_n = 4
-
-    cells, border = pl.pallas_call(
+
+    cells, border, tiny, facts = pl.pallas_call(
         lambda *refs: stem_kernel(side, *refs),
         name="stem",
         out_shape=(
             jax.ShapeDtypeStruct((half * half, 4 * channels), BF16),
             jax.ShapeDtypeStruct((border_rows, 4 * channels), BF16),
+            jax.ShapeDtypeStruct((32, 4 * channels), BF16),
+            jax.ShapeDtypeStruct((16, 4 * channels), BF16),
         ),
-        in_specs=[smem_spec(), smem_spec(), vmem_spec(), pl.BlockSpec(memory_space=pl.ANY)],
-        out_specs=(vmem_spec(), vmem_spec()),
+        in_specs=[pl.BlockSpec(memory_space=pl.ANY)] * 5,
+        out_specs=(vmem_spec(),) * 4,
         scratch_shapes=[
-            VMEM((area, patch), BF16),
-            VMEM((area, 2 * channels), F32),
-            pltpu.SemaphoreType.DMA((chunk_n,)),
+            SMEM((1, 1), jnp.int32),
+            SMEM((1, 1), jnp.int32),
+            SMEM((1, 3), jnp.int32),
+            VMEM((channels, patch), BF16),
+            VMEM((1, patch, area), BF16),
+            VMEM((half * half, 2 * channels), F32),
+            VMEM((half * half, 2 * channels), F32),
+            pltpu.SemaphoreType.DMA((5,)),
         ],
-        compiler_params=pltpu.CompilerParams(vmem_limit_bytes=20 * MIB),
-    )(tile_count, adjacency, w_stem, pixels)
+        compiler_params=pltpu.CompilerParams(vmem_limit_bytes=STEM_VMEM),
+    )(
+        tile_count.reshape(1, 1), tissue.reshape(1, 1), adjacency, w_stem.T,
+        jnp.swapaxes(pixels, 1, 2),
+    )
 
     line = ("tiles", "heads")
     line_n = lax.axis_size("tiles") * lax.axis_size("heads")
-    second = lax.ppermute(border, line, [(i, i + 2) for i in range(line_n - 2)])
+    prior = lax.ppermute(border, line, [(i, i + 1) for i in range(line_n - 1)])
+    second = lax.ppermute(tiny, line, [(i, i + 2) for i in range(line_n - 2)])
     partial, dense1, dense2 = pl.pallas_call(
         lambda *refs: conv_kernel(half, in1, *refs),
         name="conv",
@@ -351,15 +365,11 @@
         cost_estimate=pl.CostEstimate(flops=10**9, bytes_accessed=4 * 10**6, transcendentals=0),
     )(cells, w_conv1.reshape(groups * 9 * in1, out1), w_conv2.reshape(groups * 9 * in2, out2))
 
-    odd = lax.rem(lax.axis_index(line), 2) == 1
-    prior = lax.ppermute(
-        jnp.where(odd, second, border), line, [(i, i ^ 1) for i in range(line_n)]
-    )
     message = pl.pallas_call(
         token_kernel,
         name="token",
         out_shape=jax.ShapeDtypeStruct((tokens + 16, out_n), BF16),
-        in_specs=[smem_spec()] * 3 + [vmem_spec()] * 5,
+        in_specs=[vmem_spec()] * 6,
         out_specs=vmem_spec(),
         scratch_shapes=[
             VMEM((half * half, mid_n), F32),
@@ -369,7 +379,7 @@
             VMEM((out_n // 128, tokens, 128), F32),
         ],
         compiler_params=pltpu.CompilerParams(vmem_limit_bytes=20 * MIB),
-    )(tile_count, tissue, adjacency, partial, prior, second, dense1, dense2)
+    )(facts, partial, prior, second, dense1, dense2)
 
     far = swapped(message, "heads", 2)
     near = swapped(message, "heads", 1)
@@ -383,31 +393,38 @@
     part_n = 4
     part_rows = latent_n // part_n
     place = lax.axis_index("tiles") if few else jnp.int32(0)
+    place = place.astype(jnp.int32).reshape(1)
     parts = pl.pallas_call(
         attention_kernel,
         name="attention",
-        out_shape=jax.ShapeDtypeStruct((part_n, part_rows + 16, width), BF16),
+        out_shape=(jax.ShapeDtypeStruct((part_rows + 8, width), F32),) * part_n,
         in_specs=[smem_spec()] + [vmem_spec()] * 7,
-        out_specs=vmem_spec(),
-        scratch_shapes=[VMEM((4 * tokens, width), BF16), VMEM((4 * tokens, width), BF16)],
-        compiler_params=pltpu.CompilerParams(vmem_limit_bytes=24 * MIB),
-    )(place.astype(jnp.int32).reshape(1), message, near, far, far_near, w_key, w_value, queries)
+        out_specs=(vmem_spec(),) * part_n,
+        scratch_shapes=[
+            VMEM((4 * tokens, width), BF16),
+            VMEM((4 * tokens, width), BF16),
+            VMEM((latent_n, width), F32),
+            VMEM((latent_n, width), F32),
+        ],
+        compiler_params=pltpu.CompilerParams(vmem_limit_bytes=20 * MIB),
+    )(place, message, near, far, far_near, w_key, w_value, queries)
 
     if few:
-        received = [parts[0]] + [swapped(parts[k], "tiles", k) for k in range(1, 4)]
+        received = [swapped(parts[k], "tiles", k) for k in (3, 2, 1)]
         return pl.pallas_call(
             lambda *refs: merge_kernel(head_n, *refs),
             name="merge",
             out_shape=jax.ShapeDtypeStruct((part_rows, width), BF16),
             in_specs=[vmem_spec()] * 4,
             out_specs=vmem_spec(),
-        )(*received)
-    coded = parts[:, part_rows:].astype(F32)
-    stats = coded[:, 0:4] + coded[:, 4:8] + coded[:, 8:12]
+            compiler_params=pltpu.CompilerParams(vmem_limit_bytes=4 * MIB),
+        )(parts[0], *received)
+    parts = jnp.stack(parts)
+    stats = parts[:, part_rows : part_rows + 4]
     stats = stats.transpose(0, 2, 1).reshape(tile_n, share, 4)
     weighted = parts[:, :part_rows].reshape(tile_n, share, width)
     stats = lax.all_to_all(stats, "tiles", 0, 0)
-    weighted = lax.all_to_all(weighted, "tiles", 0, 0).astype(F32)
+    weighted = lax.all_to_all(weighted, "tiles", 0, 0)
     peaks, totals = stats[..., :head_n], stats[..., head_n : 2 * head_n]
     scale = jnp.exp(peaks - jnp.max(peaks, axis=0, keepdims=True))
     scale = scale / jnp.sum(scale * totals, axis=0, keepdims=True)

time: 42 us -> 36.7 us (0.87)
  local copies, waits for them, and re-layouts: 4.54 us -> 1.06 us
  starting transfers between devices: 12.7 us -> 15.1 us
  waiting for transfers between devices: 12.8 us -> 10.4 us
  Pallas kernels: 10.2 us -> 8.4 us
    unnamed x22 -> x14, local copies, waits for them, and re-layouts: 3.91 us -> 1.06 us
    ppermute x2, starting transfers between devices: 4.92 us -> 6.76 us  [the longest x1 4.4 us: per_device(): second = lax.ppermute(tiny, line, [(i, i + 2) for i in range(line_n - 2)])]
    ppermute x2, waiting for transfers between devices: 1.71 us -> 0.01 us  [the longest x1 0.01 us: per_device(): prior = lax.ppermute(border, line, [(i, i + 1) for i in range(line_n - 1)])]
    pallas_call x1, Pallas kernels: 3.26 us -> 2.38 us  [per_device(): pl.pallas_call(attention_kernel, name='attention', out_shape=(jax.ShapeDt...]
    pallas_call x1, Pallas kernels: 1.8 us -> 0.97 us  [per_device(): pl.pallas_call(lambda *refs: merge_kernel(head_n, *refs), name='merge', o...]
    ppermute x6, waiting for transfers between devices: 11.1 us -> 10.4 us  [swapped(): lax.ppermute(x, axis, [(i, i ^ distance) for i in range(lax.axis_size(axi...]
    squeeze x1 -> x0, local copies, waits for them, and re-layouts: 0.63 us -> none  [per_device(): received = [parts[0]] + [swapped(parts[k], 'tiles', k) for k in range(1, 4)]]
    pallas_call x1, Pallas kernels: 1.49 us -> 0.94 us  [per_device(): pl.pallas_call(token_kernel, name='token', out_shape=jax.ShapeDtypeStruct...]
  transfers between devices with their start and end apart: 8 -> 8, of which waited for: 6 -> 4; matrix products, arithmetic and copies ran while one was open for 0% -> 0% of each run, Pallas kernels for 2% -> 2%
where the time goes in v2:
time: 36.7 us; the launch traced here: 36.4 us
  starting transfers between devices  15.1 us (41%)
  waiting for transfers between devices  10.4 us (28%)
  Pallas kernels  8.4 us (23%)
  between operations  1.47 us (4%)
  local copies, waits for them, and re-layouts  1.06 us (3%)
    ppermute x6, waiting for transfers between devices, swapped(): lax.ppermute(x, axis, [(i, i ^ distance) for i in range(lax.axis_size(axi...  10.4 us
    ppermute x6, starting transfers between devices, swapped(): lax.ppermute(x, axis, [(i, i ^ distance) for i in range(lax.axis_size(axi...  8.3 us
    ppermute x1, starting transfers between devices, per_device(): second = lax.ppermute(tiny, line, [(i, i + 2) for i in range(line_n - 2)])  4.4 us
    pallas_call x1, Pallas kernels, per_device(): pl.pallas_call(lambda *refs: stem_kernel(side, *refs), name='stem', out_s...  3.32 us
    pallas_call x1, Pallas kernels, per_device(): pl.pallas_call(attention_kernel, name='attention', out_shape=(jax.ShapeDt...  2.38 us
    ppermute x1, starting transfers between devices, per_device(): prior = lax.ppermute(border, line, [(i, i + 1) for i in range(line_n - 1)])  2.36 us
    unnamed x14, local copies, waits for them, and re-layouts  1.06 us
    pallas_call x1, Pallas kernels, per_device(): pl.pallas_call(lambda *refs: merge_kernel(head_n, *refs), name='merge', o...  0.97 us
  transfers between devices with their start and end apart: 8, of which 4 were waited for; matrix products, arithmetic and copies ran while one was open for 0% of the time, Pallas kernels for 2%

profile of v2, /device:TPU:0, one launch (start us, length us, event | category | flops | bytes accessed | tf_op | source)
XLA Modules:
  0.0 36.4 jit_solution(16292535805186482183)
XLA Ops:
  0.0 0.0 copy-start.6
  0.0 0.0 copy-start.5
  1.4 3.3 %stem.1 = (bf16[1024,256]{1,0:T(8,128)(2,1)}, bf16[144,256]{1,0:T(8,128)(2,1)}, bf16[32,256]{1,0:T(8,128)(2,1)}, bf16[16,256]{1,0:T(8,128)(2,1)}) custom-call(s32[1,1]{1,0:T(1,128)} %bitcast.7.refs_0_, s32[1,1]{1,0:T(1,128)} %bitcast.8.refs_1_, s32[1,3]{1,0:T(1,128)} %refs_2_.1, bf16[64,192]{1,0:T(8,128)(2,1)} %bitcast.12, bf16[1,192,4096]{2,1,0:T(8,128)(2,1)} %bitcast.11), custom_call_target="tpu_custom_call" | custom-call | tf_op jit(solution)/shard_map/stem/pallas_call | solution.py:322
  4.7 2.4 %collective-permute-start = (bf16[144,256]{1,0:T(8,128)(2,1)}, bf16[144,256]{1,0:T(8,128)(2,1)S(1)}, u32[]{:S(2)}, u32[]{:S(2)}) collective-permute-start(bf16[144,256]{1,0:T(8,128)(2,1)} %get-tuple-element.19), channel_id=1, source_target_pairs={{0,1},{1,2},{2,3},{3,4},{4,5},{5,6},{6,7},{7,8},{8,9},{9,10},{10,1... | collective-permute-start | bytes 221192 | tf_op jit(solution)/shard_map/ppermute | solution.py:351
  7.1 4.4 %collective-permute-start.1 = (bf16[32,256]{1,0:T(8,128)(2,1)}, bf16[32,256]{1,0:T(8,128)(2,1)S(1)}, u32[]{:S(2)}, u32[]{:S(2)}) collective-permute-start(bf16[32,256]{1,0:T(8,128)(2,1)} %get-tuple-element.20), channel_id=1, source_target_pairs={{0,2},{1,3},{2,4},{3,5},{4,6},{5,7},{6,8},{7,9},{8,10},{9,11},{10,... | collective-permute-start | bytes 49160 | tf_op jit(solution)/shard_map/ppermute | solution.py:352
  11.5 0.0 copy-done.6
  11.5 0.0 copy-done.5
  11.5 0.0 copy-start.4
  11.5 1.0 %copy-done.4 = bf16[1024,256]{1,0:T(8,128)(2,1)S(1)} copy-done((bf16[1024,256]{1,0:T(8,128)(2,1)S(1)}, bf16[1024,256]{1,0:T(8,128)(2,1)}, u32[]{:S(2)}) %copy-start.4) | copy-done | bytes 524312
  12.5 0.0 copy-start.3
  12.5 0.8 %conv.1 = (f32[1024,128]{1,0:T(8,128)S(1)}, bf16[256,512]{1,0:T(8,128)(2,1)S(1)}, bf16[512,1024]{1,0:T(8,128)(2,1)S(1)}) custom-call(bf16[1024,256]{1,0:T(8,128)(2,1)S(1)} %copy-done.4, bf16[576,32]{1,0:T(8,128)(2,1)S(1)} %bitcast.10, bf16[1152,64]{1,0:T(8,128)(2,1)S(1)} %bitcast.9), custom_call_target="tpu_custom_call" | custom-call | flops 1000000000 | bytes 4000000 | tf_op jit(solution)/shard_map/conv/pallas_call | solution.py:353
  13.3 0.0 copy-start
  13.3 0.0 copy-start.1
  13.3 0.0 copy-start.2
  13.4 0.0 collective-permute-done.1.second_ref
  13.4 0.0 collective-permute-done.prior_ref
  13.4 0.0 copy-done.3
  13.4 0.9 %token_.1.t0 = bf16[272,256]{1,0:T(8,128)(2,1)S(1)} custom-call(bf16[16,256]{1,0:T(8,128)(2,1)S(1)} %copy-done.3, f32[1024,128]{1,0:T(8,128)S(1)} %get-tuple-element.18.partial_ref, bf16[144,256]{1,0:T(8,128)(2,1)S(1)} %collective-permute-done.prior_ref, bf16[32,256]{1,0:T(8,128)(2,1)S(1)} %collective-permute-done.1.second_ref, ...), custom_call_target="tpu_custom_call" | custom-call | tf_op jit(solution)/shard_map/token/pallas_call | solution.py:368
  14.3 2.1 %collective-permute-start.3 = (bf16[272,256]{1,0:T(8,128)(2,1)S(1)}, bf16[272,256]{1,0:T(8,128)(2,1)S(1)}, u32[]{:S(2)}, u32[]{:S(2)}) collective-permute-start(bf16[272,256]{1,0:T(8,128)(2,1)S(1)} %token_.1.t0), channel_id=1, source_target_pairs={{0,2},{1,3},{2,0},{3,1},{4,6},{5,7},{6,4},{7,5},{8,10},{9,11},{10,... | collective-permute-start | bytes 417800 | tf_op jit(solution)/shard_map/ppermute | solution.py:305
  16.4 0.6 %collective-permute-start.2 = (bf16[272,256]{1,0:T(8,128)(2,1)S(1)}, bf16[272,256]{1,0:T(8,128)(2,1)S(1)}, u32[]{:S(2)}, u32[]{:S(2)}) collective-permute-start(bf16[272,256]{1,0:T(8,128)(2,1)S(1)} %token_.1.t0), channel_id=1, source_target_pairs={{0,1},{1,0},{2,3},{3,2},{4,5},{5,4},{6,7},{7,6},{8,9},{9,8},{10,11... | collective-permute-start | bytes 417800 | tf_op jit(solution)/shard_map/ppermute | solution.py:305
  17.0 3.6 %collective-permute-done.3.t2 = bf16[272,256]{1,0:T(8,128)(2,1)S(1)} collective-permute-done((bf16[272,256]{1,0:T(8,128)(2,1)S(1)}, bf16[272,256]{1,0:T(8,128)(2,1)S(1)}, u32[]{:S(2)}, u32[]{:S(2)}) %collective-permute-start.3) | collective-permute-done | bytes 139296 | tf_op jit(solution)/shard_map/ppermute | solution.py:305
  20.6 0.1 collective-permute-start.4
  20.8 0.0 collective-permute-done.2.t1
  20.8 1.2 %collective-permute-done.4.t3 = bf16[272,256]{1,0:T(8,128)(2,1)S(1)} collective-permute-done((bf16[272,256]{1,0:T(8,128)(2,1)S(1)}, bf16[272,256]{1,0:T(8,128)(2,1)S(1)}, u32[]{:S(2)}, u32[]{:S(2)}) %collective-permute-start.4) | collective-permute-done | bytes 139296 | tf_op jit(solution)/shard_map/ppermute | solution.py:305
  22.0 0.0 copy-done
  22.0 0.0 copy-done.1
  22.0 0.0 copy-done.2
  22.0 2.4 %attention.1 = (f32[136,128]{1,0:T(8,128)S(1)}, f32[136,128]{1,0:T(8,128)S(1)}, f32[136,128]{1,0:T(8,128)S(1)}, f32[136,128]{1,0:T(8,128)S(1)}) custom-call(s32[1]{0:T(128)} %bitcast.place_ref, bf16[272,256]{1,0:T(8,128)(2,1)S(1)} %token_.1.t0, bf16[272,256]{1,0:T(8,128)(2,1)S(1)} %collective-permute-done.2.t1, ...), custom_call_target="tpu_custom_call" | custom-call | tf_op jit(solution)/shard_map/attention/pallas_call | solution.py:397
  24.4 4.9 %collective-permute-start.5 = (f32[136,128]{1,0:T(8,128)S(1)}, f32[136,128]{1,0:T(8,128)S(1)}, u32[]{:S(2)}, u32[]{:S(2)}) collective-permute-start(f32[136,128]{1,0:T(8,128)S(1)} %get-tuple-element.24), channel_id=1, source_target_pairs={{0,12},{4,8},{8,4},{12,0},{1,13},{5,9},{9,5},{13,1},{2,14},{6,10},... | collective-permute-start | bytes 208904 | tf_op jit(solution)/shard_map/ppermute | solution.py:305
  29.2 0.0 collective-permute-start.6
  29.2 0.6 %collective-permute-start.7 = (f32[136,128]{1,0:T(8,128)S(1)}, f32[136,128]{1,0:T(8,128)S(1)}, u32[]{:S(2)}, u32[]{:S(2)}) collective-permute-start(f32[136,128]{1,0:T(8,128)S(1)} %get-tuple-element.26), channel_id=1, source_target_pairs={{0,4},{4,0},{8,12},{12,8},{1,5},{5,1},{9,13},{13,9},{2,6},{6,2},{1... | collective-permute-start | bytes 208904 | tf_op jit(solution)/shard_map/ppermute | solution.py:305
  29.9 2.2 %collective-permute-done.5.refs_1_ = f32[136,128]{1,0:T(8,128)S(1)} collective-permute-done((f32[136,128]{1,0:T(8,128)S(1)}, f32[136,128]{1,0:T(8,128)S(1)}, u32[]{:S(2)}, u32[]{:S(2)}) %collective-permute-start.5) | collective-permute-done | bytes 69664 | tf_op jit(solution)/shard_map/ppermute | solution.py:305
  32.1 3.4 %collective-permute-done.6.refs_2_ = f32[136,128]{1,0:T(8,128)S(1)} collective-permute-done((f32[136,128]{1,0:T(8,128)S(1)}, f32[136,128]{1,0:T(8,128)S(1)}, u32[]{:S(2)}, u32[]{:S(2)}) %collective-permute-start.6) | collective-permute-done | bytes 69664 | tf_op jit(solution)/shard_map/ppermute | solution.py:305
  35.4 0.0 collective-permute-done.7.refs_3_
  35.4 1.0 %merge.1 = bf16[128,128]{1,0:T(8,128)(2,1)} custom-call(f32[136,128]{1,0:T(8,128)S(1)} %get-tuple-element.23.refs_0_, f32[136,128]{1,0:T(8,128)S(1)} %collective-permute-done.5.refs_1_, f32[136,128]{1,0:T(8,128)S(1)} %collective-permute-done.6.refs_2_, f32[136,128]{1,0:T(8,128)S(1)} %collective-permute-done.7.refs_3_), custom_call_target="tpu_custom_call" | custom-call | tf_op jit(solution)/shard_map/merge/pallas_call | solution.py:414
Async XLA Ops:
  0.0 11.5 %copy-start.6 = (bf16[4,9,16,32]{3,2,1,0:T(8,128)(2,1)S(1)}, bf16[4,9,16,32]{3,2,1,0:T(8,128)(2,1)}, u32[]{:S(2)}) copy-start(bf16[4,9,16,32]{3,2,1,0:T(8,128)(2,1)} %param.12) | copy-start | bytes 110596
  0.0 11.5 %copy-start.5 = (bf16[4,9,32,64]{3,2,1,0:T(8,128)(2,1)S(1)}, bf16[4,9,32,64]{3,2,1,0:T(8,128)(2,1)}, u32[]{:S(2)}) copy-start(bf16[4,9,32,64]{3,2,1,0:T(8,128)(2,1)} %param.13) | copy-start | bytes 442372
  4.7 8.7 %collective-permute-start = (bf16[144,256]{1,0:T(8,128)(2,1)}, bf16[144,256]{1,0:T(8,128)(2,1)S(1)}, u32[]{:S(2)}, u32[]{:S(2)}) collective-permute-start(bf16[144,256]{1,0:T(8,128)(2,1)} %get-tuple-element.19), channel_id=1, source_target_pairs={{0,1},{1,2},{2,3},{3,4},{4,5},{5,6},{6,7},{7,8},{8,9},{9,10},{10,1... | collective-permute-start | bytes 221192 | tf_op jit(solution)/shard_map/ppermute | solution.py:351
  7.1 6.3 %collective-permute-start.1 = (bf16[32,256]{1,0:T(8,128)(2,1)}, bf16[32,256]{1,0:T(8,128)(2,1)S(1)}, u32[]{:S(2)}, u32[]{:S(2)}) collective-permute-start(bf16[32,256]{1,0:T(8,128)(2,1)} %get-tuple-element.20), channel_id=1, source_target_pairs={{0,2},{1,3},{2,4},{3,5},{4,6},{5,7},{6,8},{7,9},{8,10},{9,11},{10,... | collective-permute-start | bytes 49160 | tf_op jit(solution)/shard_map/ppermute | solution.py:352
  11.5 1.0 %copy-start.4 = (bf16[1024,256]{1,0:T(8,128)(2,1)S(1)}, bf16[1024,256]{1,0:T(8,128)(2,1)}, u32[]{:S(2)}) copy-start(bf16[1024,256]{1,0:T(8,128)(2,1)} %get-tuple-element.17.refs_0_) | copy-start | bytes 1572868
  12.5 0.9 %copy-start.3 = (bf16[16,256]{1,0:T(8,128)(2,1)S(1)}, bf16[16,256]{1,0:T(8,128)(2,1)}, u32[]{:S(2)}) copy-start(bf16[16,256]{1,0:T(8,128)(2,1)} %get-tuple-element.16.facts_ref) | copy-start | bytes 24580
  13.3 8.7 %copy-start = (bf16[512,128]{1,0:T(8,128)(2,1)S(1)}, bf16[512,128]{1,0:T(8,128)(2,1)}, u32[]{:S(2)}) copy-start(bf16[512,128]{1,0:T(8,128)(2,1)} %q_ref.1) | copy-start | bytes 393220
  13.3 8.7 %copy-start.1 = (bf16[256,128]{1,0:T(8,128)(2,1)S(1)}, bf16[256,128]{1,0:T(8,128)(2,1)}, u32[]{:S(2)}) copy-start(bf16[256,128]{1,0:T(8,128)(2,1)} %wk_ref.1) | copy-start | bytes 196612
  13.3 8.6 %copy-start.2 = (bf16[256,128]{1,0:T(8,128)(2,1)S(1)}, bf16[256,128]{1,0:T(8,128)(2,1)}, u32[]{:S(2)}) copy-start(bf16[256,128]{1,0:T(8,128)(2,1)} %wv_ref.1) | copy-start | bytes 196612
  14.3 6.3 %collective-permute-start.3 = (bf16[272,256]{1,0:T(8,128)(2,1)S(1)}, bf16[272,256]{1,0:T(8,128)(2,1)S(1)}, u32[]{:S(2)}, u32[]{:S(2)}) collective-permute-start(bf16[272,256]{1,0:T(8,128)(2,1)S(1)} %token_.1.t0), channel_id=1, source_target_pairs={{0,2},{1,3},{2,0},{3,1},{4,6},{5,7},{6,4},{7,5},{8,10},{9,11},{10,... | collective-permute-start | bytes 417800 | tf_op jit(solution)/shard_map/ppermute | solution.py:305
  16.4 4.4 %collective-permute-start.2 = (bf16[272,256]{1,0:T(8,128)(2,1)S(1)}, bf16[272,256]{1,0:T(8,128)(2,1)S(1)}, u32[]{:S(2)}, u32[]{:S(2)}) collective-permute-start(bf16[272,256]{1,0:T(8,128)(2,1)S(1)} %token_.1.t0), channel_id=1, source_target_pairs={{0,1},{1,0},{2,3},{3,2},{4,5},{5,4},{6,7},{7,6},{8,9},{9,8},{10,11... | collective-permute-start | bytes 417800 | tf_op jit(solution)/shard_map/ppermute | solution.py:305
  20.6 1.4 %collective-permute-start.4 = (bf16[272,256]{1,0:T(8,128)(2,1)S(1)}, bf16[272,256]{1,0:T(8,128)(2,1)S(1)}, u32[]{:S(2)}, u32[]{:S(2)}) collective-permute-start(bf16[272,256]{1,0:T(8,128)(2,1)S(1)} %collective-permute-done.3.t2), channel_id=1, source_target_pairs={{0,1},{1,0},{2,3},{3,2},{4,5},{5,4},{6,7},{7,6},{8,9},{9,8},{10,11... | collective-permute-start | bytes 417800 | tf_op jit(solution)/shard_map/ppermute | solution.py:305
  24.4 7.7 %collective-permute-start.5 = (f32[136,128]{1,0:T(8,128)S(1)}, f32[136,128]{1,0:T(8,128)S(1)}, u32[]{:S(2)}, u32[]{:S(2)}) collective-permute-start(f32[136,128]{1,0:T(8,128)S(1)} %get-tuple-element.24), channel_id=1, source_target_pairs={{0,12},{4,8},{8,4},{12,0},{1,13},{5,9},{9,5},{13,1},{2,14},{6,10},... | collective-permute-start | bytes 208904 | tf_op jit(solution)/shard_map/ppermute | solution.py:305
  29.2 6.2 %collective-permute-start.6 = (f32[136,128]{1,0:T(8,128)S(1)}, f32[136,128]{1,0:T(8,128)S(1)}, u32[]{:S(2)}, u32[]{:S(2)}) collective-permute-start(f32[136,128]{1,0:T(8,128)S(1)} %get-tuple-element.25), channel_id=1, source_target_pairs={{0,8},{4,12},{8,0},{12,4},{1,9},{5,13},{9,1},{13,5},{2,10},{6,14},... | collective-permute-start | bytes 208904 | tf_op jit(solution)/shard_map/ppermute | solution.py:305
  29.2 6.2 %collective-permute-start.7 = (f32[136,128]{1,0:T(8,128)S(1)}, f32[136,128]{1,0:T(8,128)S(1)}, u32[]{:S(2)}, u32[]{:S(2)}) collective-permute-start(f32[136,128]{1,0:T(8,128)S(1)} %get-tuple-element.26), channel_id=1, source_target_pairs={{0,4},{4,0},{8,12},{12,8},{1,5},{5,1},{9,13},{13,9},{2,6},{6,2},{1... | collective-permute-start | bytes 208904 | tf_op jit(solution)/shard_map/ppermute | solution.py:305

commit v3 on v2

v3 whole, which is shorter than its diff:
```python
import jax
import jax.numpy as jnp
from jax import lax
from jax.experimental import pallas as pl
from jax.experimental.pallas import tpu as pltpu
from jax.sharding import PartitionSpec as P

HEAD_DIM = 64
NEG_BIG = -1e30
LN_EPS = 1e-05
F32 = jnp.float32
BF16 = jnp.bfloat16
VMEM = pltpu.VMEM
SMEM = pltpu.SMEM
MIB = 1 << 20
FIRST_VMEM = 60 * MIB
PACK = 1 << 16


def vmem_spec():
    return pl.BlockSpec(memory_space=VMEM)


def smem_spec():
    return pl.BlockSpec(memory_space=SMEM)


def expand_weights(flat, in_group, out_group, dense_ref):
    groups = flat.shape[0] // (9 * in_group)
    wide = groups * out_group
    source = lax.broadcasted_iota(jnp.int32, (out_group, wide), 0)
    target = lax.broadcasted_iota(jnp.int32, (out_group, wide), 1)
    spread = (lax.rem(target, out_group) == source).astype(BF16)
    tiled = jnp.dot(flat, spread, preferred_element_type=F32)
    row = lax.broadcasted_iota(jnp.int32, tiled.shape, 0)
    lane = lax.broadcasted_iota(jnp.int32, tiled.shape, 1)
    own = lax.div(row, 9 * in_group) == lax.div(lane, out_group)
    tiled = jnp.where(own, tiled, 0.0).astype(BF16)
    dense_ref[...] = jnp.zeros_like(dense_ref)
    for group in range(groups):
        for tap_row in range(3):
            for tap_col in range(3):
                py, px = int(tap_row != 1), int(tap_col != 1)
                block = 2 * int(tap_row == 0) + int(tap_col == 0)
                first = (9 * group + 3 * tap_row + tap_col) * in_group
                to_row = (2 * py + px) * groups * in_group + group * in_group
                dense_ref[pl.ds(to_row, in_group), pl.ds(block * wide, wide)] = tiled[
                    first : first + in_group
                ]


def shifted_down(x):
    row = lax.broadcasted_iota(jnp.int32, x.shape, 0)
    return jnp.where(row == 0, 0.0, pltpu.roll(x, 1, 0))


def normalised(deep):
    deep = jnp.maximum(deep, 0.0)
    centred = deep - jnp.mean(deep, axis=1, keepdims=True)
    spread = jnp.mean(centred * centred, axis=1, keepdims=True)
    return (centred * lax.rsqrt(spread + LN_EPS)).astype(BF16)


def expand_kernel(w1_ref, w2_ref, dense1_ref, dense2_ref):
    expand_weights(w1_ref[...], w1_ref.shape[0] // 36, w1_ref.shape[1], dense1_ref)
    expand_weights(w2_ref[...], w2_ref.shape[0] // 36, w2_ref.shape[1], dense2_ref)


def first_kernel(side, packed_any, adjacency_any, w_any, w1_any, w2_any, pixels_any, token_ref,
                 edge_ref, border_ref, tiny_ref, packed, adjacency, weight, w1, w2, pixels,
                 cells_ref, even_lines, odd_lines, dense1_ref, dense2_ref, wide1, partial, cells,
                 wide2, sems):
    copies = [
        pltpu.make_async_copy(source, target, sems.at[k])
        for k, (source, target) in enumerate((
            (w1_any, w1), (w2_any, w2), (pixels_any, pixels), (w_any, weight),
            (packed_any, packed), (adjacency_any, adjacency),
        ))
    ]
    for copy in copies:
        copy.start()
    copies[0].wait()
    expand_weights(w1[...], w1.shape[0] // 36, w1.shape[1], dense1_ref)
    copies[1].wait()
    expand_weights(w2[...], w2.shape[0] // 36, w2.shape[1], dense2_ref)
    stem_n, half = weight.shape[0], side // 2
    rows, span = 4 * half, 4 * side
    row = lax.broadcasted_iota(jnp.int32, (rows, 2 * span), 0)
    column = lax.broadcasted_iota(jnp.int32, (rows, 2 * span), 1)
    line = 2 * lax.div(lax.rem(row, 2 * half), half) + lax.div(row, 2 * half)
    wanted = line * side + 2 * lax.rem(row, half)
    pick = (lax.rem(column, span) == wanted + lax.div(column, span)).astype(BF16)
    for copy in copies[2:]:
        copy.wait()
    live = (packed[0, 0] >= PACK).astype(F32)
    tissue = lax.rem(packed[0, 0], PACK)
    gates = [(adjacency[0, k] == 0).astype(F32) for k in range(3)]
    row = lax.broadcasted_iota(jnp.int32, (16, cells_ref.shape[1]), 0)
    facts = jnp.zeros(row.shape, F32)
    for k, fact in enumerate([live] + gates + [live * tissue.astype(F32)]):
        facts = jnp.where(row == k, fact, facts)
    cells_ref[pl.ds(half * half, 16)] = facts.astype(BF16)
    border_ref[pl.ds(4 * half, 16)] = facts.astype(BF16)
    flat = jnp.dot(weight[...], pixels[0], preferred_element_type=F32)
    flat = (jnp.maximum(flat, 0.0) * live).astype(BF16)
    blank = jnp.zeros((stem_n, span), BF16)
    for k in range(side // 4):
        four = flat[:, k * span : (k + 1) * span]
        both = jnp.concatenate(
            [jnp.concatenate([four, blank], axis=0), jnp.concatenate([blank, four], axis=0)],
            axis=1,
        )
        sorted_ = lax.dot_general(
            pick, both, (((1,), (1,)), ((), ())), preferred_element_type=F32
        )
        here = pl.ds(k * 2 * half, 2 * half)
        even_lines[here] = sorted_[: 2 * half]
        odd_lines[here] = sorted_[2 * half :]
        cells_ref[here, pl.ds(0, 2 * stem_n)] = sorted_[: 2 * half].astype(BF16)
        cells_ref[here, pl.ds(2 * stem_n, 2 * stem_n)] = sorted_[2 * half :].astype(BF16)
    border_ref[pl.ds(0, 2 * half)] = cells_ref[pl.ds((half - 2) * half, 2 * half)]
    for which in range(2):
        for py, lines in enumerate((even_lines, odd_lines)):
            border_ref[
                pl.ds((2 + which) * half, half), pl.ds(py * 2 * stem_n, 2 * stem_n)
            ] = lines[pl.ds(half - 2 + which, half, stride=half)].astype(BF16)
    tiny_ref[pl.ds(0, 16)] = cells_ref[pl.ds((half - 1) * half - 16, 16)]
    tiny_ref[pl.ds(16, 16)] = cells_ref[pl.ds(half * half - 16, 16)]
    positions, channels = partial.shape
    chunk = 8 * half
    wide1[pl.ds(0, half)] = jnp.zeros((half, wide1.shape[1]), F32)
    row = lax.broadcasted_iota(jnp.int32, (chunk, channels), 0)
    first = lax.rem(row, half) == 0
    dense = dense1_ref[...]
    lane = [pl.ds(b * channels, channels) for b in range(4)]
    for k in range(positions // chunk):
        wide1[pl.ds(half + k * chunk, chunk)] = jnp.dot(
            cells_ref[pl.ds(k * chunk, chunk)], dense, preferred_element_type=F32
        )
        here = pl.ds(half + k * chunk, chunk)
        up = pl.ds(k * chunk, chunk)
        before = wide1[here, lane[1]] + wide1[up, lane[3]]
        before = jnp.where(first, 0.0, pltpu.roll(before, 1, 0))
        partial[pl.ds(k * chunk, chunk)] = wide1[here, lane[0]] + wide1[up, lane[2]] + before
    edge_ref[pl.ds(0, 2 * half)] = partial[pl.ds(0, 2 * half)]
    edge_ref[pl.ds(2 * half, half)] = partial[pl.ds(0, half, stride=half)]
    edge_ref[pl.ds(3 * half, half)] = partial[pl.ds(1, half, stride=half)]
    edge_ref[pl.ds(4 * half, 8)] = facts[0:8, :channels]
    quarter = half // 2
    for i in range(half):
        for px in range(2):
            cells[
                pl.ds((i // 2) * quarter, quarter), pl.ds((2 * (i % 2) + px) * channels, channels)
            ] = jnp.maximum(partial[pl.ds(i * half + px, quarter, stride=2)], 0.0).astype(BF16)
    tokens = quarter * quarter
    out_n = dense2_ref.shape[1] // 4
    block = [pl.ds(b * out_n, out_n) for b in range(4)]
    wide2[pl.ds(0, quarter)] = jnp.zeros((quarter, wide2.shape[1]), F32)
    here, up = pl.ds(quarter, tokens), pl.ds(0, tokens)
    wide2[here] = jnp.dot(cells[...], dense2_ref[...], preferred_element_type=F32)
    before = wide2[here, block[1]] + wide2[up, block[3]]
    row = lax.broadcasted_iota(jnp.int32, before.shape, 0)
    before = jnp.where(lax.rem(row, quarter) == 0, 0.0, pltpu.roll(before, 1, 0))
    deep = wide2[here, block[0]] + wide2[up, block[2]] + before
    token_ref[pl.ds(0, tokens)] = normalised(deep)
    token_ref[pl.ds(tokens, 16)] = cells_ref[pl.ds(positions, 16)]


def rim_kernel(edge_ref, prior_ref, second_ref, dense1_ref, dense2_ref, rim_ref,
               lines, cells):
    half, channels = (edge_ref.shape[0] - 8) // 4, edge_ref.shape[1]
    quarter = half // 2
    facts = edge_ref[pl.ds(4 * half, 8)]
    live, above, beside, corner, known = [facts[k : k + 1, 0:1] for k in range(5)]
    lane = [slice(b * channels, (b + 1) * channels) for b in range(4)]
    dense1 = dense1_ref[...]
    prior = jnp.dot(prior_ref[pl.ds(0, 4 * half)], dense1, preferred_element_type=F32)
    second = jnp.dot(second_ref[...], dense1, preferred_element_type=F32)
    facts = prior_ref[pl.ds(4 * half, 16), pl.ds(0, channels)].astype(F32)
    live_prior, above_prior, beside_prior = facts[0:1], facts[1:2], facts[2:3]
    row_30 = prior[0:half]
    row_31 = prior[half : 2 * half]
    col_30 = prior[2 * half : 3 * half]
    col_31 = prior[3 * half : 4 * half]
    at_zero = lax.broadcasted_iota(jnp.int32, (half, channels), 0) == 0
    top = above * (row_31[:, lane[2]] + shifted_down(row_31[:, lane[3]]))
    top = top + jnp.where(at_zero, corner * row_31[half - 1 : half, lane[3]], 0.0)
    side = beside * (col_31[:, lane[1]] + shifted_down(col_31[:, lane[3]]))
    own = [edge_ref[pl.ds(k * half, half)] for k in range(4)]
    own[0] = own[0] + top + jnp.where(at_zero, side, 0.0)
    own[1] = own[1] + jnp.where(at_zero, side[1:2], 0.0)
    own[2] = own[2] + side + jnp.where(at_zero, top, 0.0)
    own[3] = own[3] + jnp.where(at_zero, top[1:2], 0.0)
    for k in range(4):
        lines[pl.ds(k * half, half)] = jnp.maximum(own[k], 0.0) * live
    over_last, left_last, last = second[15:16], second[30:31], second[31:32]
    row_sum = row_31[:, lane[0]] + row_30[:, lane[2]]
    row_sum = row_sum + shifted_down(row_31[:, lane[1]] + row_30[:, lane[3]])
    row_sum = row_sum + jnp.where(
        at_zero, beside_prior * (last[:, lane[1]] + over_last[:, lane[3]]), 0.0
    )
    col_sum = col_31[:, lane[0]] + col_30[:, lane[1]]
    col_sum = col_sum + shifted_down(col_31[:, lane[2]] + col_30[:, lane[3]])
    col_sum = col_sum + jnp.where(
        at_zero, above_prior * (last[:, lane[2]] + left_last[:, lane[3]]), 0.0
    )
    lines[pl.ds(4 * half, half)] = jnp.maximum(row_sum, 0.0) * live_prior
    lines[pl.ds(5 * half, half)] = jnp.maximum(col_sum, 0.0) * live_prior
    cells[pl.ds(2 * quarter, 2 * quarter)] = jnp.zeros((2 * quarter, cells.shape[1]), BF16)

    def put(which, py, px, line, parity):
        cells[pl.ds(which * quarter, quarter), pl.ds((2 * py + px) * channels, channels)] = lines[
            pl.ds(line * half + parity, quarter, stride=2)
        ].astype(BF16)

    for a in range(2):
        for b in range(2):
            put(0, a, b, a, b)
            put(1, a, b, 2 + b, a)
        put(2, 1, a, 4, a)
        put(3, a, 1, 5, a)
    out_n = dense2_ref.shape[1] // 4
    wide = jnp.dot(cells[...], dense2_ref[...], preferred_element_type=F32)
    part = [
        [wide[k * quarter : (k + 1) * quarter, b * out_n : (b + 1) * out_n] for b in range(4)]
        for k in range(4)
    ]
    row0, col0, over, left = part
    at_zero = lax.broadcasted_iota(jnp.int32, (quarter, out_n), 0) == 0
    deep_row = row0[0] + shifted_down(row0[1]) + above * (over[2] + shifted_down(over[3]))
    deep_row = deep_row + jnp.where(
        at_zero, beside * left[1] + corner * over[3][quarter - 1 : quarter], 0.0
    )
    deep_col = col0[0] + shifted_down(col0[2]) + beside * (left[1] + shifted_down(left[3]))
    rim_ref[pl.ds(0, quarter)] = normalised(deep_row)
    rim_ref[pl.ds(quarter, quarter)] = normalised(deep_col)
    rim_ref[pl.ds(2 * quarter, 16)] = jnp.broadcast_to(known, (16, out_n)).astype(BF16)


def queries_of(place_ref, q_ref, parts, part_n):
    rows = q_ref.shape[0] // part_n
    found = [
        q_ref[pl.ds(pl.multiple_of((place_ref[0] ^ k) * rows, rows), rows)].astype(F32)
        for k in parts
    ]
    return jnp.concatenate(found, axis=0) * (float(HEAD_DIM) ** -0.5)


def by_head(q):
    lane = lax.broadcasted_iota(jnp.int32, q.shape, 1)
    head_n = q.shape[1] // HEAD_DIM
    return jnp.concatenate(
        [jnp.where(lax.div(lane, HEAD_DIM) == h, q, 0.0) for h in range(head_n)], axis=0
    ).astype(BF16)


def softmax_part(q, pieces):
    rows, width = q.shape
    head_n = width // HEAD_DIM
    lane = lax.broadcasted_iota(jnp.int32, (rows, width), 1)
    q = by_head(q)
    scores = [
        lax.dot_general(q, keys, (((1,), (1,)), ((), ())), preferred_element_type=F32) + bias
        for keys, _, bias in pieces
    ]
    peak = jnp.max(scores[0], axis=1, keepdims=True)
    for more in scores[1:]:
        peak = jnp.maximum(peak, jnp.max(more, axis=1, keepdims=True))
    total = summed = 0.0
    for score, (_, values, _) in zip(scores, pieces):
        weights = jnp.exp(score - peak)
        total = total + jnp.sum(weights, axis=1, keepdims=True)
        summed = summed + jnp.dot(weights.astype(BF16), values, preferred_element_type=F32)
    joined = summed[:rows]
    facts = jnp.zeros((rows, width), F32)
    for h in range(head_n):
        mine = slice(h * rows, (h + 1) * rows)
        joined = jnp.where(lax.div(lane, HEAD_DIM) == h, summed[mine], joined)
        facts = jnp.where(lane == h, peak[mine], facts)
        facts = jnp.where(lane == head_n + h, total[mine], facts)
    return joined, facts


def main_kernel(part_n, place_ref, t0, t1, t2, t3, wk_ref, wv_ref, q_ref, sum_ref, facts_ref,
                keys, values, bias_ref):
    tokens = t0.shape[0] - 16
    quarter = int(round(tokens**0.5))
    width = q_ref.shape[1]
    both = jnp.concatenate([wk_ref[...], wv_ref[...]], axis=1)
    masks = []
    spot = lax.broadcasted_iota(jnp.int32, (1, tokens), 1)
    inside = (spot >= quarter) & (lax.rem(spot, quarter) != 0)
    for b, ref in enumerate((t0, t1, t2, t3)):
        made = jnp.dot(ref[pl.ds(0, tokens)], both, preferred_element_type=F32).astype(BF16)
        keys[pl.ds(b * tokens, tokens)] = made[:, :width]
        values[pl.ds(b * tokens, tokens)] = made[:, width:]
        known = ref[pl.ds(tokens, 16), pl.ds(0, tokens)].astype(F32)[4:5]
        masks.append(jnp.where(inside & (spot.astype(F32) < known), 0.0, NEG_BIG))
    bias = jnp.concatenate(masks, axis=1)
    bias_ref[...] = jnp.broadcast_to(bias, bias_ref.shape)
    rows = sum_ref.shape[0] // (part_n - 1)
    pieces = [(keys[...], values[...], bias)]
    for k in range(1, part_n):
        here = pl.ds((k - 1) * rows, rows)
        q = queries_of(place_ref, q_ref, [k], part_n)
        sum_ref[here], facts_ref[here] = softmax_part(q, pieces)


def rest_kernel(part_n, place_ref, t0, t1, t2, t3, wk_ref, wv_ref, q_ref, sum_ref, before_ref,
                keys, values, bias_ref, *out_refs):
    rim = t0.shape[0] - 16
    quarter = rim // 2
    width = q_ref.shape[1]
    head_n = width // HEAD_DIM
    both = jnp.concatenate([wk_ref[...], wv_ref[...]], axis=1)
    spot = lax.broadcasted_iota(jnp.int32, (1, rim), 1)
    token = jnp.where(spot < quarter, spot, (spot - quarter) * quarter)
    masks = []
    for ref in (t0, t1, t2, t3):
        known = ref[pl.ds(rim, 16), pl.ds(0, rim)].astype(F32)[0:1]
        good = (spot != quarter) & (token.astype(F32) < known)
        masks.append(jnp.where(good, 0.0, NEG_BIG))
    bias = jnp.concatenate(masks, axis=1)
    bias_ref[...] = jnp.broadcast_to(bias, bias_ref.shape)
    all_rim = jnp.concatenate([ref[pl.ds(0, rim)] for ref in (t0, t1, t2, t3)], axis=0)
    made = jnp.dot(all_rim, both, preferred_element_type=F32).astype(BF16)
    keys[...] = made[:, :width]
    values[...] = made[:, width:]
    q = queries_of(place_ref, q_ref, range(1, part_n), part_n)
    joined, facts = softmax_part(q, [(made[:, :width], made[:, width:], bias)])
    lane = lax.broadcasted_iota(jnp.int32, facts.shape, 1)
    before = before_ref[...]
    peak = jnp.maximum(facts, before)
    scale_new = jnp.exp(jnp.where(lane < head_n, facts - peak, 0.0))
    scale_old = jnp.exp(jnp.where(lane < head_n, before - peak, 0.0))
    total = facts * pltpu.roll(scale_new, head_n, 1) + before * pltpu.roll(scale_old, head_n, 1)
    wide_new, wide_old = scale_new[:, 0:1], scale_old[:, 0:1]
    for h in range(1, head_n):
        mine = lax.div(lane, HEAD_DIM) == h
        wide_new = jnp.where(mine, scale_new[:, h : h + 1], wide_new)
        wide_old = jnp.where(mine, scale_old[:, h : h + 1], wide_old)
    joined = joined * wide_new + sum_ref[...] * wide_old
    facts = jnp.where(lane < head_n, peak, total)
    rows = q_ref.shape[0] // part_n
    for k, out_ref in enumerate(out_refs):
        out_ref[pl.ds(0, rows)] = joined[k * rows : (k + 1) * rows]
        out_ref[pl.ds(rows, 8)] = facts[k * rows : (k + 1) * rows].T[0:8]


def own_kernel(part_n, place_ref, q_ref, keys, values, bias_ref, rim_keys, rim_values,
               rim_bias_ref, out_ref):
    joined, facts = softmax_part(
        queries_of(place_ref, q_ref, [0], part_n),
        [
            (keys[...], values[...], bias_ref[pl.ds(0, 1)]),
            (rim_keys[...], rim_values[...], rim_bias_ref[pl.ds(0, 1)]),
        ],
    )
    rows = q_ref.shape[0] // part_n
    out_ref[pl.ds(0, rows)] = joined
    out_ref[pl.ds(rows, 8)] = facts.T[0:8]


def merge_kernel(head_n, *refs):
    in_refs, out_ref = refs[:-1], refs[-1]
    part_rows, width = out_ref.shape
    stats = [ref[pl.ds(part_rows, 8)] for ref in in_refs]
    row8 = lax.broadcasted_iota(jnp.int32, stats[0].shape, 0)
    peak = stats[0]
    for s in stats[1:]:
        peak = jnp.maximum(peak, s)
    scales = [jnp.exp(jnp.where(row8 < head_n, s - peak, 0.0)) for s in stats]
    total = scales[0] * pltpu.roll(stats[0], 8 - head_n, 0)
    for c, s in zip(scales[1:], stats[1:]):
        total = total + c * pltpu.roll(s, 8 - head_n, 0)
    total = jnp.where(row8 < head_n, total, 1.0)
    scales = [c / total for c in scales]
    blank = jnp.zeros((part_rows - 8 * len(scales), part_rows), F32)
    turned = jnp.concatenate(scales + [blank], axis=0).T
    lane = lax.broadcasted_iota(jnp.int32, (part_rows, width), 1)
    result = jnp.zeros((part_rows, width), F32)
    for k, ref in enumerate(in_refs):
        scale = turned[:, 8 * k : 8 * k + 1]
        for h in range(1, head_n):
            scale = jnp.where(
                lax.div(lane, HEAD_DIM) == h, turned[:, 8 * k + h : 8 * k + h + 1], scale
            )
        result = result + ref[pl.ds(0, part_rows)] * scale
    out_ref[...] = result.astype(BF16)


def swapped(x, axis, distance):
    return lax.ppermute(x, axis, [(i, i ^ distance) for i in range(lax.axis_size(axis))])


def per_device(
    pixels, w_stem, w_conv1, w_conv2, w_key, w_value, queries, tile_count, tissue, adjacency
):
    slot_n, area, patch = pixels.shape
    assert slot_n == 1
    side = int(round(area**0.5))
    half, quarter = side // 2, side // 4
    channels = w_stem.shape[1]
    groups, _, in1, out1 = w_conv1.shape
    _, _, in2, out2 = w_conv2.shape
    mid_n, out_n = groups * out1, groups * out2
    tokens = quarter * quarter
    border_rows = 4 * half + 16

    w1 = w_conv1.reshape(groups * 9 * in1, out1)
    w2 = w_conv2.reshape(groups * 9 * in2, out2)
    dense_shapes = ((4 * channels, 4 * mid_n), (4 * mid_n, 4 * out_n))
    message, edge, border, tiny = pl.pallas_call(
        lambda *refs: first_kernel(side, *refs),
        name="first",
        out_shape=(
            jax.ShapeDtypeStruct((tokens + 16, out_n), BF16),
            jax.ShapeDtypeStruct((4 * half + 8, mid_n), F32),
            jax.ShapeDtypeStruct((border_rows, 4 * channels), BF16),
            jax.ShapeDtypeStruct((32, 4 * channels), BF16),
        ),
        in_specs=[pl.BlockSpec(memory_space=pl.ANY)] * 6,
        out_specs=(vmem_spec(),) * 4,
        scratch_shapes=[
            SMEM((1, 1), jnp.int32),
            SMEM((1, 3), jnp.int32),
            VMEM((channels, patch), BF16),
            VMEM(w1.shape, BF16),
            VMEM(w2.shape, BF16),
            VMEM((1, patch, area), BF16),
            VMEM((half * half + 16, 4 * channels), BF16),
            VMEM((half * half, 2 * channels), F32),
            VMEM((half * half, 2 * channels), F32),
            VMEM(dense_shapes[0], BF16),
            VMEM(dense_shapes[1], BF16),
            VMEM((half * half + half, 4 * mid_n), F32),
            VMEM((half * half, mid_n), F32),
            VMEM((tokens, 4 * mid_n), BF16),
            VMEM((tokens + quarter, 4 * out_n), F32),
            pltpu.SemaphoreType.DMA((6,)),
        ],
        compiler_params=pltpu.CompilerParams(vmem_limit_bytes=FIRST_VMEM),
    )(
        (tile_count * PACK + tissue).reshape(1, 1), adjacency, w_stem.T, w1, w2,
        jnp.swapaxes(pixels, 1, 2),
    )

    line = ("tiles", "heads")
    line_n = lax.axis_size("tiles") * lax.axis_size("heads")
    prior = lax.ppermute(border, line, [(i, i + 1) for i in range(line_n - 1)])
    second = lax.ppermute(tiny, line, [(i, i + 2) for i in range(line_n - 2)])
    message, w1, w2 = lax.optimization_barrier((message, w1, w2))
    dense1, dense2 = pl.pallas_call(
        expand_kernel,
        name="expand",
        out_shape=tuple(jax.ShapeDtypeStruct(shape, BF16) for shape in dense_shapes),
        in_specs=[vmem_spec()] * 2,
        out_specs=(vmem_spec(),) * 2,
        compiler_params=pltpu.CompilerParams(vmem_limit_bytes=8 * MIB),
        cost_estimate=pl.CostEstimate(flops=10**9, bytes_accessed=4 * 10**6, transcendentals=0),
    )(w1, w2)
    message, dense1 = lax.optimization_barrier((message, dense1))
    far = swapped(message, "heads", 2)
    near = swapped(message, "heads", 1)
    far_near = swapped(far, "heads", 1)

    rim = pl.pallas_call(
        rim_kernel,
        name="rim",
        out_shape=jax.ShapeDtypeStruct((2 * quarter + 16, out_n), BF16),
        in_specs=[vmem_spec()] * 5,
        out_specs=vmem_spec(),
        scratch_shapes=[
            VMEM((6 * half, mid_n), F32),
            VMEM((4 * quarter, 4 * mid_n), BF16),
        ],
        compiler_params=pltpu.CompilerParams(vmem_limit_bytes=12 * MIB),
        cost_estimate=pl.CostEstimate(flops=20*10**9, bytes_accessed=4 * 10**7, transcendentals=0),
    )(edge, prior, second, dense1, dense2)
    rims = [swapped(rim, "heads", k) for k in (2, 1, 3)]

    tile_n = lax.axis_size("tiles")
    latent_n, width = queries.shape
    head_n = width // HEAD_DIM
    share = latent_n // tile_n
    few = tile_n == 4
    part_n = 4
    part_rows = latent_n // part_n
    place = lax.axis_index("tiles") if few else jnp.int32(0)
    place = place.astype(jnp.int32).reshape(1)
    others = (part_n - 1) * part_rows
    main = pl.pallas_call(
        lambda *refs: main_kernel(part_n, *refs),
        name="main",
        out_shape=(
            jax.ShapeDtypeStruct((others, width), F32),
            jax.ShapeDtypeStruct((others, width), F32),
            jax.ShapeDtypeStruct((4 * tokens, width), BF16),
            jax.ShapeDtypeStruct((4 * tokens, width), BF16),
            jax.ShapeDtypeStruct((8, 4 * tokens), F32),
        ),
        in_specs=[smem_spec()] + [vmem_spec()] * 7,
        out_specs=(vmem_spec(),) * 5,
        compiler_params=pltpu.CompilerParams(vmem_limit_bytes=16 * MIB),
        cost_estimate=pl.CostEstimate(flops=10**6, bytes_accessed=10**4, transcendentals=0),
    )(place, message, near, far, far_near, w_key, w_value, queries)
    rest = pl.pallas_call(
        lambda *refs: rest_kernel(part_n, *refs),
        name="rest",
        out_shape=(
            jax.ShapeDtypeStruct((8 * quarter, width), BF16),
            jax.ShapeDtypeStruct((8 * quarter, width), BF16),
            jax.ShapeDtypeStruct((8, 8 * quarter), F32),
        ) + (jax.ShapeDtypeStruct((part_rows + 8, width), F32),) * (part_n - 1),
        in_specs=[smem_spec()] + [vmem_spec()] * 9,
        out_specs=(vmem_spec(),) * (part_n + 2),
        compiler_params=pltpu.CompilerParams(vmem_limit_bytes=12 * MIB),
        cost_estimate=pl.CostEstimate(
            flops=20 * 10**9, bytes_accessed=4 * 10**7, transcendentals=0
        ),
    )(place, rim, *rims, w_key, w_value, queries, main[0], main[1])
    own = pl.pallas_call(
        lambda *refs: own_kernel(part_n, *refs),
        name="own",
        out_shape=jax.ShapeDtypeStruct((part_rows + 8, width), F32),
        in_specs=[smem_spec()] + [vmem_spec()] * 7,
        out_specs=vmem_spec(),
        compiler_params=pltpu.CompilerParams(vmem_limit_bytes=12 * MIB),
        cost_estimate=pl.CostEstimate(flops=10**9, bytes_accessed=4 * 10**6, transcendentals=0),
    )(place, queries, main[2], main[3], main[4], rest[0], rest[1], rest[2])
    parts = (own,) + tuple(rest[3:])

    if few:
        received = [swapped(parts[k], "tiles", k) for k in (3, 2, 1)]
        return pl.pallas_call(
            lambda *refs: merge_kernel(head_n, *refs),
            name="merge",
            out_shape=jax.ShapeDtypeStruct((part_rows, width), BF16),
            in_specs=[vmem_spec()] * 4,
            out_specs=vmem_spec(),
            compiler_params=pltpu.CompilerParams(vmem_limit_bytes=4 * MIB),
        )(parts[0], *received)
    parts = jnp.stack(parts)
    stats = parts[:, part_rows : part_rows + 4]
    stats = stats.transpose(0, 2, 1).reshape(tile_n, share, 4)
    weighted = parts[:, :part_rows].reshape(tile_n, share, width)
    stats = lax.all_to_all(stats, "tiles", 0, 0)
    weighted = lax.all_to_all(weighted, "tiles", 0, 0)
    peaks, totals = stats[..., :head_n], stats[..., head_n : 2 * head_n]
    scale = jnp.exp(peaks - jnp.max(peaks, axis=0, keepdims=True))
    scale = scale / jnp.sum(scale * totals, axis=0, keepdims=True)
    return jnp.sum(weighted * jnp.repeat(scale, HEAD_DIM, axis=2), axis=0).astype(BF16)


def solution(mesh):
    in_specs = (
        P(("slides", "tiles", "heads"), None, None),
        P(),
        P(),
        P(),
        P(None, "heads"),
        P(None, "heads"),
        P(None, "heads"),
        P(("slides", "tiles", "heads")),
        P(("slides", "tiles", "heads")),
        P(("slides", "tiles", "heads"), None),
    )
    out_specs = P(("slides", "tiles"), "heads")
    return jax.shard_map(
        per_device, mesh=mesh, in_specs=in_specs, out_specs=out_specs, check_vma=False
    )
```

time: 36.7 us -> 35.2 us (0.959)
  waiting for transfers between devices: 10.4 us -> 5.29 us
  Pallas kernels: 8.4 us -> 10.6 us
  starting transfers between devices: 15.1 us -> 17 us
  local copies, waits for them, and re-layouts: 1.06 us -> 0.55 us
    ppermute x6 -> x9, waiting for transfers between devices: 10.4 us -> 5.29 us  [swapped(): lax.ppermute(x, axis, [(i, i ^ distance) for i in range(lax.axis_size(axi...]
    ppermute x6 -> x9, starting transfers between devices: 8.3 us -> 13.2 us  [swapped(): lax.ppermute(x, axis, [(i, i ^ distance) for i in range(lax.axis_size(axi...]
    pallas_call x4 -> x6, Pallas kernels: 7.42 us -> 9.64 us  [the longest x1 4.85 us: per_device(): pl.pallas_call(lambda *refs: first_kernel(side, *refs), name='first', out...]
    ppermute x1, starting transfers between devices: 4.4 us -> 2.4 us  [per_device(): second = lax.ppermute(tiny, line, [(i, i + 2) for i in range(line_n - 2)])]
    ppermute x1, starting transfers between devices: 2.36 us -> 1.46 us  [per_device(): prior = lax.ppermute(border, line, [(i, i + 1) for i in range(line_n - 1)])]
    unnamed x14 -> x18, local copies, waits for them, and re-layouts: 1.06 us -> 0.55 us
  transfers between devices with their start and end apart: 8 -> 11, of which waited for: 4 -> 3; matrix products, arithmetic and copies ran while one was open for 0% -> 0% of each run, Pallas kernels for 2% -> 10%
where the time goes in v3:
time: 35.2 us; the launch traced here: 35 us
  starting transfers between devices  17 us (48%)
  Pallas kernels  10.6 us (30%)
  waiting for transfers between devices  5.29 us (15%)
  between operations  1.53 us (4%)
  local copies, waits for them, and re-layouts  0.55 us (2%)
    ppermute x9, starting transfers between devices, swapped(): lax.ppermute(x, axis, [(i, i ^ distance) for i in range(lax.axis_size(axi...  13.2 us
    ppermute x9, waiting for transfers between devices, swapped(): lax.ppermute(x, axis, [(i, i ^ distance) for i in range(lax.axis_size(axi...  5.29 us
    pallas_call x1, Pallas kernels, per_device(): pl.pallas_call(lambda *refs: first_kernel(side, *refs), name='first', out...  4.85 us
    ppermute x1, starting transfers between devices, per_device(): second = lax.ppermute(tiny, line, [(i, i + 2) for i in range(line_n - 2)])  2.4 us
    pallas_call x1, Pallas kernels, per_device(): pl.pallas_call(lambda *refs: main_kernel(part_n, *refs), name='main', out...  1.89 us
    ppermute x1, starting transfers between devices, per_device(): prior = lax.ppermute(border, line, [(i, i + 1) for i in range(line_n - 1)])  1.46 us
    pallas_call x1, Pallas kernels, per_device(): pl.pallas_call(lambda *refs: rest_kernel(part_n, *refs), name='rest', out...  1.06 us
    pallas_call x1, Pallas kernels, per_device(): pl.pallas_call(lambda *refs: merge_kernel(head_n, *refs), name='merge', o...  0.97 us
  transfers between devices with their start and end apart: 11, of which 3 were waited for; matrix products, arithmetic and copies ran while one was open for 0% of the time, Pallas kernels for 10%

profile of v3, /device:TPU:0, one launch (start us, length us, event | category | flops | bytes accessed | tf_op | source)
XLA Modules:
  0.0 35.0 jit_solution(18316326207189452552)
XLA Ops:
  0.0 0.0 copy-start
  0.0 0.0 copy-start.1
  1.4 4.8 %first.1 = (bf16[272,256]{1,0:T(8,128)(2,1)}, f32[136,128]{1,0:T(8,128)}, bf16[144,256]{1,0:T(8,128)(2,1)}, bf16[32,256]{1,0:T(8,128)(2,1)}) custom-call(s32[1,1]{1,0:T(1,128)} %bitcast.1.refs_0_, s32[1,3]{1,0:T(1,128)} %refs_1_.2, bf16[64,192]{1,0:T(8,128)(2,1)} %bitcast.11, bf16[576,32]{1,0:T(8,128)(2,1)} %bitcast.8, bf16[1152,64]{1,0:T(8,128)(2,1)} %bitcast.6, ...), custom_call_target="tpu_custom_call" | custom-call | tf_op jit(solution)/shard_map/first/pallas_call | solution.py:413
  6.2 0.0 copy-done
  6.2 0.0 copy-done.1
  6.2 0.0 copy-start.2
  6.2 0.0 copy-start.7
  6.3 0.0 copy-start.8
  6.3 0.0 copy-start.6
  6.3 0.4 %expand.1 = (bf16[256,512]{1,0:T(8,128)(2,1)S(1)}, bf16[512,1024]{1,0:T(8,128)(2,1)S(1)}) custom-call(bf16[576,32]{1,0:T(8,128)(2,1)S(1)} %bitcast.9, bf16[1152,64]{1,0:T(8,128)(2,1)S(1)} %bitcast.7), custom_call_target="tpu_custom_call" | custom-call | flops 1000000000 | bytes 4000000 | tf_op jit(solution)/shard_map/expand/pallas_call | solution.py:453
  6.6 0.5 %copy-done.2 = bf16[272,256]{1,0:T(8,128)(2,1)S(1)} copy-done((bf16[272,256]{1,0:T(8,128)(2,1)S(1)}, bf16[272,256]{1,0:T(8,128)(2,1)}, u32[]{:S(2)}) %copy-start.2) | copy-done | bytes 139288
  7.1 2.9 %collective-permute-start.1 = (bf16[272,256]{1,0:T(8,128)(2,1)S(1)}, bf16[272,256]{1,0:T(8,128)(2,1)S(1)}, u32[]{:S(2)}, u32[]{:S(2)}) collective-permute-start(bf16[272,256]{1,0:T(8,128)(2,1)S(1)} %copy-done.2), channel_id=1, source_target_pairs={{0,2},{1,3},{2,0},{3,1},{4,6},{5,7},{6,4},{7,5},{8,10},{9,11},{10,... | collective-permute-start | bytes 417800 | tf_op jit(solution)/shard_map/ppermute | solution.py:393
  10.1 0.0 copy-done.7
  10.1 1.5 %collective-permute-start.3 = (bf16[144,256]{1,0:T(8,128)(2,1)S(1)}, bf16[144,256]{1,0:T(8,128)(2,1)S(1)}, u32[]{:S(2)}, u32[]{:S(2)}) collective-permute-start(bf16[144,256]{1,0:T(8,128)(2,1)S(1)} %copy-done.7), channel_id=1, source_target_pairs={{0,1},{1,2},{2,3},{3,4},{4,5},{5,6},{6,7},{7,8},{8,9},{9,10},{10,1... | collective-permute-start | bytes 221192 | tf_op jit(solution)/shard_map/ppermute | solution.py:450
  11.5 0.0 copy-done.8
  11.6 2.4 %collective-permute-start.4 = (bf16[32,256]{1,0:T(8,128)(2,1)S(1)}, bf16[32,256]{1,0:T(8,128)(2,1)S(1)}, u32[]{:S(2)}, u32[]{:S(2)}) collective-permute-start(bf16[32,256]{1,0:T(8,128)(2,1)S(1)} %copy-done.8), channel_id=1, source_target_pairs={{0,2},{1,3},{2,4},{3,5},{4,6},{5,7},{6,8},{7,9},{8,10},{9,11},{10,... | collective-permute-start | bytes 49160 | tf_op jit(solution)/shard_map/ppermute | solution.py:451
  14.0 2.9 %collective-permute-start = (bf16[272,256]{1,0:T(8,128)(2,1)S(1)}, bf16[272,256]{1,0:T(8,128)(2,1)S(1)}, u32[]{:S(2)}, u32[]{:S(2)}) collective-permute-start(bf16[272,256]{1,0:T(8,128)(2,1)S(1)} %copy-done.2), channel_id=1, source_target_pairs={{0,1},{1,0},{2,3},{3,2},{4,5},{5,4},{6,7},{7,6},{8,9},{9,8},{10,11... | collective-permute-start | bytes 417800 | tf_op jit(solution)/shard_map/ppermute | solution.py:393
  16.8 0.0 collective-permute-done.1.refs_3_
  16.9 0.1 collective-permute-start.2
  16.9 0.0 collective-permute-done.4.second_ref
  16.9 0.0 collective-permute-done.3.prior_ref
  16.9 0.0 copy-done.6
  17.0 0.0 copy-start.3
  17.0 0.0 copy-start.4
  17.0 0.0 copy-start.5
  17.0 0.7 %rim.1.refs_1_ = bf16[48,256]{1,0:T(8,128)(2,1)S(1)} custom-call(f32[136,128]{1,0:T(8,128)S(1)} %copy-done.6, bf16[144,256]{1,0:T(8,128)(2,1)S(1)} %collective-permute-done.3.prior_ref, bf16[32,256]{1,0:T(8,128)(2,1)S(1)} %collective-permute-done.4.second_ref, bf16[256,512]{1,0:T(8,128)(2,1)S(1)} %get-tuple-element.39.dense1_ref, ...), custom_call_target="tpu_custom_call" | custom-call | flops 20000000000 | bytes 40000000 | tf_op jit(solution)/shard_map/rim/pallas_call | solution.py:467
  17.7 2.4 %collective-permute-start.7 = (bf16[48,256]{1,0:T(8,128)(2,1)S(1)}, bf16[48,256]{1,0:T(8,128)(2,1)S(1)}, u32[]{:S(2)}, u32[]{:S(2)}) collective-permute-start(bf16[48,256]{1,0:T(8,128)(2,1)S(1)} %rim.1.refs_1_), channel_id=1, source_target_pairs={{0,3},{1,2},{2,1},{3,0},{4,7},{5,6},{6,5},{7,4},{8,11},{9,10},{10,... | collective-permute-start | bytes 73736 | tf_op jit(solution)/shard_map/ppermute | solution.py:393
  20.0 0.0 collective-permute-start.6
  20.0 0.5 %collective-permute-start.5 = (bf16[48,256]{1,0:T(8,128)(2,1)S(1)}, bf16[48,256]{1,0:T(8,128)(2,1)S(1)}, u32[]{:S(2)}, u32[]{:S(2)}) collective-permute-start(bf16[48,256]{1,0:T(8,128)(2,1)S(1)} %rim.1.refs_1_), channel_id=1, source_target_pairs={{0,2},{1,3},{2,0},{3,1},{4,6},{5,7},{6,4},{7,5},{8,10},{9,11},{10,... | collective-permute-start | bytes 73736 | tf_op jit(solution)/shard_map/ppermute | solution.py:393
  20.5 0.0 collective-permute-done.refs_2_
  20.5 0.0 collective-permute-done.2.refs_4_
  20.5 0.0 copy-done.3
  20.5 0.0 copy-done.4
  20.5 0.0 copy-done.5
  20.5 1.9 %main.1 = (f32[384,128]{1,0:T(8,128)S(1)}, f32[384,128]{1,0:T(8,128)S(1)}, bf16[1024,128]{1,0:T(8,128)(2,1)S(1)}, bf16[1024,128]{1,0:T(8,128)(2,1)S(1)}, f32[8,1024]{1,0:T(8,128)S(1)}) custom-call(s32[1]{0:T(128)} %bitcast.refs_0_, bf16[272,256]{1,0:T(8,128)(2,1)S(1)} %copy-done.2, bf16[272,256]{1,0:T(8,128)(2,1)S(1)} %collective-permute-done.refs_2_, ...), custom_call_target="tpu_custom_call" | custom-call | flops 1000000 | bytes 10000 | tf_op jit(solution)/shard_map/main/pallas_call | solution.py:492
  22.4 0.0 collective-permute-done.7.refs_4_
  22.4 0.0 collective-permute-done.6.refs_3_
  22.5 1.4 %collective-permute-done.5.refs_2_ = bf16[48,256]{1,0:T(8,128)(2,1)S(1)} collective-permute-done((bf16[48,256]{1,0:T(8,128)(2,1)S(1)}, bf16[48,256]{1,0:T(8,128)(2,1)S(1)}, u32[]{:S(2)}, u32[]{:S(2)}) %collective-permute-start.5) | collective-permute-done | bytes 24608 | tf_op jit(solution)/shard_map/ppermute | solution.py:393
  23.9 1.1 %rest.1 = (bf16[128,128]{1,0:T(8,128)(2,1)S(1)}, bf16[128,128]{1,0:T(8,128)(2,1)S(1)}, f32[8,128]{1,0:T(8,128)S(1)}, f32[136,128]{1,0:T(8,128)S(1)}, f32[136,128]{1,0:T(8,128)S(1)}, /*index=5*/f32[136,128]{1,0:T(8,128)S(1)}) custom-call(s32[1]{0:T(128)} %bitcast.refs_0_, bf16[48,256]{1,0:T(8,128)(2,1)S(1)} %rim.1.refs_1_, ...), custom_call_target="tpu_custom_call" | custom-call | flops 20000000000 | bytes 40000000 | tf_op jit(solution)/shard_map/rest/pallas_call | solution.py:507
  24.9 3.2 %collective-permute-start.8 = (f32[136,128]{1,0:T(8,128)S(1)}, f32[136,128]{1,0:T(8,128)S(1)}, u32[]{:S(2)}, u32[]{:S(2)}) collective-permute-start(f32[136,128]{1,0:T(8,128)S(1)} %get-tuple-element.46), channel_id=1, source_target_pairs={{0,12},{4,8},{8,4},{12,0},{1,13},{5,9},{9,5},{13,1},{2,14},{6,10},... | collective-permute-start | bytes 208904 | tf_op jit(solution)/shard_map/ppermute | solution.py:393
  28.2 0.0 collective-permute-start.9
  28.2 1.2 %collective-permute-start.10 = (f32[136,128]{1,0:T(8,128)S(1)}, f32[136,128]{1,0:T(8,128)S(1)}, u32[]{:S(2)}, u32[]{:S(2)}) collective-permute-start(f32[136,128]{1,0:T(8,128)S(1)} %get-tuple-element.48), channel_id=1, source_target_pairs={{0,4},{4,0},{8,12},{12,8},{1,5},{5,1},{9,13},{13,9},{2,6},{6,2},{1... | collective-permute-start | bytes 208904 | tf_op jit(solution)/shard_map/ppermute | solution.py:393
  29.4 0.8 %own.1.refs_0_ = f32[136,128]{1,0:T(8,128)S(1)} custom-call(s32[1]{0:T(128)} %bitcast.refs_0_, bf16[512,128]{1,0:T(8,128)(2,1)S(1)} %copy-done.3, bf16[1024,128]{1,0:T(8,128)(2,1)S(1)} %get-tuple-element.33.refs_2_, bf16[1024,128]{1,0:T(8,128)(2,1)S(1)} %get-tuple-element.34.refs_3_, f32[8,1024]{1,0:T(8,128)S(1)} %get-tuple-element.35.refs_4_, ...), custom_call_target="tpu_custom_call" | custom-call | flops 1000000000 | bytes 4000000 | tf_op jit(solution)/shard_map/own/pallas_call | solution.py:522
  30.2 1.6 %collective-permute-done.8.refs_1_ = f32[136,128]{1,0:T(8,128)S(1)} collective-permute-done((f32[136,128]{1,0:T(8,128)S(1)}, f32[136,128]{1,0:T(8,128)S(1)}, u32[]{:S(2)}, u32[]{:S(2)}) %collective-permute-start.8) | collective-permute-done | bytes 69664 | tf_op jit(solution)/shard_map/ppermute | solution.py:393
  31.7 2.3 %collective-permute-done.9.refs_2_ = f32[136,128]{1,0:T(8,128)S(1)} collective-permute-done((f32[136,128]{1,0:T(8,128)S(1)}, f32[136,128]{1,0:T(8,128)S(1)}, u32[]{:S(2)}, u32[]{:S(2)}) %collective-permute-start.9) | collective-permute-done | bytes 69664 | tf_op jit(solution)/shard_map/ppermute | solution.py:393
  34.0 0.0 collective-permute-done.10.refs_3_
  34.0 1.0 %merge.1 = bf16[128,128]{1,0:T(8,128)(2,1)} custom-call(f32[136,128]{1,0:T(8,128)S(1)} %own.1.refs_0_, f32[136,128]{1,0:T(8,128)S(1)} %collective-permute-done.8.refs_1_, f32[136,128]{1,0:T(8,128)S(1)} %collective-permute-done.9.refs_2_, f32[136,128]{1,0:T(8,128)S(1)} %collective-permute-done.10.refs_3_), custom_call_target="tpu_custom_call" | custom-call | tf_op jit(solution)/shard_map/merge/pallas_call | solution.py:535
Async XLA Ops:
  0.0 6.2 %copy-start = (bf16[4,9,32,64]{3,2,1,0:T(8,128)(2,1)S(1)}, bf16[4,9,32,64]{3,2,1,0:T(8,128)(2,1)}, u32[]{:S(2)}) copy-start(bf16[4,9,32,64]{3,2,1,0:T(8,128)(2,1)} %param.13) | copy-start | bytes 442372
  0.0 6.2 %copy-start.1 = (bf16[4,9,16,32]{3,2,1,0:T(8,128)(2,1)S(1)}, bf16[4,9,16,32]{3,2,1,0:T(8,128)(2,1)}, u32[]{:S(2)}) copy-start(bf16[4,9,16,32]{3,2,1,0:T(8,128)(2,1)} %param.12) | copy-start | bytes 110596
  6.2 0.9 %copy-start.2 = (bf16[272,256]{1,0:T(8,128)(2,1)S(1)}, bf16[272,256]{1,0:T(8,128)(2,1)}, u32[]{:S(2)}) copy-start(bf16[272,256]{1,0:T(8,128)(2,1)} %get-tuple-element.32.refs_1_) | copy-start | bytes 417796
  6.2 3.8 %copy-start.7 = (bf16[144,256]{1,0:T(8,128)(2,1)S(1)}, bf16[144,256]{1,0:T(8,128)(2,1)}, u32[]{:S(2)}) copy-start(bf16[144,256]{1,0:T(8,128)(2,1)} %get-tuple-element.37) | copy-start | bytes 221188
  6.3 5.3 %copy-start.8 = (bf16[32,256]{1,0:T(8,128)(2,1)S(1)}, bf16[32,256]{1,0:T(8,128)(2,1)}, u32[]{:S(2)}) copy-start(bf16[32,256]{1,0:T(8,128)(2,1)} %get-tuple-element.38) | copy-start | bytes 49156
  6.3 10.7 %copy-start.6 = (f32[136,128]{1,0:T(8,128)S(1)}, f32[136,128]{1,0:T(8,128)}, u32[]{:S(2)}) copy-start(f32[136,128]{1,0:T(8,128)} %get-tuple-element.36.edge_ref) | copy-start | bytes 208900
  7.1 9.7 %collective-permute-start.1 = (bf16[272,256]{1,0:T(8,128)(2,1)S(1)}, bf16[272,256]{1,0:T(8,128)(2,1)S(1)}, u32[]{:S(2)}, u32[]{:S(2)}) collective-permute-start(bf16[272,256]{1,0:T(8,128)(2,1)S(1)} %copy-done.2), channel_id=1, source_target_pairs={{0,2},{1,3},{2,0},{3,1},{4,6},{5,7},{6,4},{7,5},{8,10},{9,11},{10,... | collective-permute-start | bytes 417800 | tf_op jit(solution)/shard_map/ppermute | solution.py:393
  10.1 6.9 %collective-permute-start.3 = (bf16[144,256]{1,0:T(8,128)(2,1)S(1)}, bf16[144,256]{1,0:T(8,128)(2,1)S(1)}, u32[]{:S(2)}, u32[]{:S(2)}) collective-permute-start(bf16[144,256]{1,0:T(8,128)(2,1)S(1)} %copy-done.7), channel_id=1, source_target_pairs={{0,1},{1,2},{2,3},{3,4},{4,5},{5,6},{6,7},{7,8},{8,9},{9,10},{10,1... | collective-permute-start | bytes 221192 | tf_op jit(solution)/shard_map/ppermute | solution.py:450
  11.6 5.4 %collective-permute-start.4 = (bf16[32,256]{1,0:T(8,128)(2,1)S(1)}, bf16[32,256]{1,0:T(8,128)(2,1)S(1)}, u32[]{:S(2)}, u32[]{:S(2)}) collective-permute-start(bf16[32,256]{1,0:T(8,128)(2,1)S(1)} %copy-done.8), channel_id=1, source_target_pairs={{0,2},{1,3},{2,4},{3,5},{4,6},{5,7},{6,8},{7,9},{8,10},{9,11},{10,... | collective-permute-start | bytes 49160 | tf_op jit(solution)/shard_map/ppermute | solution.py:451
  14.0 6.6 %collective-permute-start = (bf16[272,256]{1,0:T(8,128)(2,1)S(1)}, bf16[272,256]{1,0:T(8,128)(2,1)S(1)}, u32[]{:S(2)}, u32[]{:S(2)}) collective-permute-start(bf16[272,256]{1,0:T(8,128)(2,1)S(1)} %copy-done.2), channel_id=1, source_target_pairs={{0,1},{1,0},{2,3},{3,2},{4,5},{5,4},{6,7},{7,6},{8,9},{9,8},{10,11... | collective-permute-start | bytes 417800 | tf_op jit(solution)/shard_map/ppermute | solution.py:393
  16.9 3.7 %collective-permute-start.2 = (bf16[272,256]{1,0:T(8,128)(2,1)S(1)}, bf16[272,256]{1,0:T(8,128)(2,1)S(1)}, u32[]{:S(2)}, u32[]{:S(2)}) collective-permute-start(bf16[272,256]{1,0:T(8,128)(2,1)S(1)} %collective-permute-done.1.refs_3_), channel_id=1, source_target_pairs={{0,1},{1,0},{2,3},{3,2},{4,5},{5,4},{6,7},{7,6},{8,9},{9,8},{10,11... | collective-permute-start | bytes 417800 | tf_op jit(solution)/shard_map/ppermute | solution.py:393
  17.0 3.6 %copy-start.3 = (bf16[512,128]{1,0:T(8,128)(2,1)S(1)}, bf16[512,128]{1,0:T(8,128)(2,1)}, u32[]{:S(2)}) copy-start(bf16[512,128]{1,0:T(8,128)(2,1)} %refs_1_.3) | copy-start | bytes 393220
  17.0 3.6 %copy-start.4 = (bf16[256,128]{1,0:T(8,128)(2,1)S(1)}, bf16[256,128]{1,0:T(8,128)(2,1)}, u32[]{:S(2)}) copy-start(bf16[256,128]{1,0:T(8,128)(2,1)} %refs_5_.3) | copy-start | bytes 196612
  17.0 3.6 %copy-start.5 = (bf16[256,128]{1,0:T(8,128)(2,1)S(1)}, bf16[256,128]{1,0:T(8,128)(2,1)}, u32[]{:S(2)}) copy-start(bf16[256,128]{1,0:T(8,128)(2,1)} %refs_6_.3) | copy-start | bytes 196612
  17.7 4.8 %collective-permute-start.7 = (bf16[48,256]{1,0:T(8,128)(2,1)S(1)}, bf16[48,256]{1,0:T(8,128)(2,1)S(1)}, u32[]{:S(2)}, u32[]{:S(2)}) collective-permute-start(bf16[48,256]{1,0:T(8,128)(2,1)S(1)} %rim.1.refs_1_), channel_id=1, source_target_pairs={{0,3},{1,2},{2,1},{3,0},{4,7},{5,6},{6,5},{7,4},{8,11},{9,10},{10,... | collective-permute-start | bytes 73736 | tf_op jit(solution)/shard_map/ppermute | solution.py:393
  20.0 2.4 %collective-permute-start.6 = (bf16[48,256]{1,0:T(8,128)(2,1)S(1)}, bf16[48,256]{1,0:T(8,128)(2,1)S(1)}, u32[]{:S(2)}, u32[]{:S(2)}) collective-permute-start(bf16[48,256]{1,0:T(8,128)(2,1)S(1)} %rim.1.refs_1_), channel_id=1, source_target_pairs={{0,1},{1,0},{2,3},{3,2},{4,5},{5,4},{6,7},{7,6},{8,9},{9,8},{10,11... | collective-permute-start | bytes 73736 | tf_op jit(solution)/shard_map/ppermute | solution.py:393
  20.0 3.8 %collective-permute-start.5 = (bf16[48,256]{1,0:T(8,128)(2,1)S(1)}, bf16[48,256]{1,0:T(8,128)(2,1)S(1)}, u32[]{:S(2)}, u32[]{:S(2)}) collective-permute-start(bf16[48,256]{1,0:T(8,128)(2,1)S(1)} %rim.1.refs_1_), channel_id=1, source_target_pairs={{0,2},{1,3},{2,0},{3,1},{4,6},{5,7},{6,4},{7,5},{8,10},{9,11},{10,... | collective-permute-start | bytes 73736 | tf_op jit(solution)/shard_map/ppermute | solution.py:393
  24.9 6.8 %collective-permute-start.8 = (f32[136,128]{1,0:T(8,128)S(1)}, f32[136,128]{1,0:T(8,128)S(1)}, u32[]{:S(2)}, u32[]{:S(2)}) collective-permute-start(f32[136,128]{1,0:T(8,128)S(1)} %get-tuple-element.46), channel_id=1, source_target_pairs={{0,12},{4,8},{8,4},{12,0},{1,13},{5,9},{9,5},{13,1},{2,14},{6,10},... | collective-permute-start | bytes 208904 | tf_op jit(solution)/shard_map/ppermute | solution.py:393
  28.2 5.9 %collective-permute-start.9 = (f32[136,128]{1,0:T(8,128)S(1)}, f32[136,128]{1,0:T(8,128)S(1)}, u32[]{:S(2)}, u32[]{:S(2)}) collective-permute-start(f32[136,128]{1,0:T(8,128)S(1)} %get-tuple-element.47), channel_id=1, source_target_pairs={{0,8},{4,12},{8,0},{12,4},{1,9},{5,13},{9,1},{13,5},{2,10},{6,14},... | collective-permute-start | bytes 208904 | tf_op jit(solution)/shard_map/ppermute | solution.py:393
  28.2 5.9 %collective-permute-start.10 = (f32[136,128]{1,0:T(8,128)S(1)}, f32[136,128]{1,0:T(8,128)S(1)}, u32[]{:S(2)}, u32[]{:S(2)}) collective-permute-start(f32[136,128]{1,0:T(8,128)S(1)} %get-tuple-element.48), channel_id=1, source_target_pairs={{0,4},{4,0},{8,12},{12,8},{1,5},{5,1},{9,13},{13,9},{2,6},{6,2},{1... | collective-permute-start | bytes 208904 | tf_op jit(solution)/shard_map/ppermute | solution.py:393

commit v4 on v3

--- a/solution.py
+++ b/solution.py
@@ -15,6 +15,7 @@
 MIB = 1 << 20
 FIRST_VMEM = 60 * MIB
 PACK = 1 << 16
+ORDER = (3, 0, 2, 1)
 
 
 def vmem_spec():
@@ -25,7 +26,19 @@
     return pl.BlockSpec(memory_space=SMEM)
 
 
-def expand_weights(flat, in_group, out_group, dense_ref):
+def wide_dots(cells, dense_ref):
+    part, out_n = dense_ref.shape[0] // 4, dense_ref.shape[1] // 4
+    return [
+        jnp.dot(
+            cells[:, first * part : last * part],
+            dense_ref[pl.ds(first * part, (last - first) * part), pl.ds(b * out_n, out_n)],
+            preferred_element_type=F32,
+        )
+        for b, (first, last) in enumerate(((0, 4), (0, 2), (1, 3), (1, 2)))
+    ]
+
+
+def expand_weights(flat, in_group, out_group, dense_ref, order=(0, 1, 2, 3)):
     groups = flat.shape[0] // (9 * in_group)
     wide = groups * out_group
     source = lax.broadcasted_iota(jnp.int32, (out_group, wide), 0)
@@ -43,7 +56,7 @@
                 py, px = int(tap_row != 1), int(tap_col != 1)
                 block = 2 * int(tap_row == 0) + int(tap_col == 0)
                 first = (9 * group + 3 * tap_row + tap_col) * in_group
-                to_row = (2 * py + px) * groups * in_group + group * in_group
+                to_row = order[2 * py + px] * groups * in_group + group * in_group
                 dense_ref[pl.ds(to_row, in_group), pl.ds(block * wide, wide)] = tiled[
                     first : first + in_group
                 ]
@@ -63,7 +76,7 @@
 
 def expand_kernel(w1_ref, w2_ref, dense1_ref, dense2_ref):
     expand_weights(w1_ref[...], w1_ref.shape[0] // 36, w1_ref.shape[1], dense1_ref)
-    expand_weights(w2_ref[...], w2_ref.shape[0] // 36, w2_ref.shape[1], dense2_ref)
+    expand_weights(w2_ref[...], w2_ref.shape[0] // 36, w2_ref.shape[1], dense2_ref, ORDER)
 
 
 def first_kernel(side, packed_any, adjacency_any, w_any, w1_any, w2_any, pixels_any, token_ref,
@@ -82,7 +95,7 @@
     copies[0].wait()
     expand_weights(w1[...], w1.shape[0] // 36, w1.shape[1], dense1_ref)
     copies[1].wait()
-    expand_weights(w2[...], w2.shape[0] // 36, w2.shape[1], dense2_ref)
+    expand_weights(w2[...], w2.shape[0] // 36, w2.shape[1], dense2_ref, ORDER)
     stem_n, half = weight.shape[0], side // 2
     rows, span = 4 * half, 4 * side
     row = lax.broadcasted_iota(jnp.int32, (rows, 2 * span), 0)
@@ -150,14 +163,16 @@
     for i in range(half):
         for px in range(2):
             cells[
-                pl.ds((i // 2) * quarter, quarter), pl.ds((2 * (i % 2) + px) * channels, channels)
+                pl.ds((i // 2) * quarter, quarter),
+                pl.ds(ORDER[2 * (i % 2) + px] * channels, channels),
             ] = jnp.maximum(partial[pl.ds(i * half + px, quarter, stride=2)], 0.0).astype(BF16)
     tokens = quarter * quarter
     out_n = dense2_ref.shape[1] // 4
     block = [pl.ds(b * out_n, out_n) for b in range(4)]
     wide2[pl.ds(0, quarter)] = jnp.zeros((quarter, wide2.shape[1]), F32)
     here, up = pl.ds(quarter, tokens), pl.ds(0, tokens)
-    wide2[here] = jnp.dot(cells[...], dense2_ref[...], preferred_element_type=F32)
+    for b, product in enumerate(wide_dots(cells[...], dense2_ref)):
+        wide2[here, block[b]] = product
     before = wide2[here, block[1]] + wide2[up, block[3]]
     row = lax.broadcasted_iota(jnp.int32, before.shape, 0)
     before = jnp.where(lax.rem(row, quarter) == 0, 0.0, pltpu.roll(before, 1, 0))
@@ -209,7 +224,7 @@
     cells[pl.ds(2 * quarter, 2 * quarter)] = jnp.zeros((2 * quarter, cells.shape[1]), BF16)
 
     def put(which, py, px, line, parity):
-        cells[pl.ds(which * quarter, quarter), pl.ds((2 * py + px) * channels, channels)] = lines[
+        cells[pl.ds(which * quarter, quarter), pl.ds(ORDER[2 * py + px] * channels, channels)] = lines[
             pl.ds(line * half + parity, quarter, stride=2)
         ].astype(BF16)
 
@@ -220,11 +235,8 @@
         put(2, 1, a, 4, a)
         put(3, a, 1, 5, a)
     out_n = dense2_ref.shape[1] // 4
-    wide = jnp.dot(cells[...], dense2_ref[...], preferred_element_type=F32)
-    part = [
-        [wide[k * quarter : (k + 1) * quarter, b * out_n : (b + 1) * out_n] for b in range(4)]
-        for k in range(4)
-    ]
+    wide = wide_dots(cells[...], dense2_ref)
+    part = [[wide[b][k * quarter : (k + 1) * quarter] for b in range(4)] for k in range(4)]
     row0, col0, over, left = part
     at_zero = lax.broadcasted_iota(jnp.int32, (quarter, out_n), 0) == 0
     deep_row = row0[0] + shifted_down(row0[1]) + above * (over[2] + shifted_down(over[3]))
@@ -459,9 +471,9 @@
         compiler_params=pltpu.CompilerParams(vmem_limit_bytes=8 * MIB),
         cost_estimate=pl.CostEstimate(flops=10**9, bytes_accessed=4 * 10**6, transcendentals=0),
     )(w1, w2)
-    message, dense1 = lax.optimization_barrier((message, dense1))
     far = swapped(message, "heads", 2)
-    near = swapped(message, "heads", 1)
+    message_n, dense1, prior = lax.optimization_barrier((message, dense1, prior))
+    near = swapped(message_n, "heads", 1)
     far_near = swapped(far, "heads", 1)
 
     rim = pl.pallas_call(
@@ -531,7 +543,7 @@
     parts = (own,) + tuple(rest[3:])
 
     if few:
-        received = [swapped(parts[k], "tiles", k) for k in (3, 2, 1)]
+        received = [swapped(parts[k], "tiles", k) for k in (1, 2, 3)]
         return pl.pallas_call(
             lambda *refs: merge_kernel(head_n, *refs),
             name="merge",

time: 35.2 us -> 34.3 us (0.974)
  local copies, waits for them, and re-layouts: 0.55 us -> 0.03 us
    unnamed x18 -> x14, local copies, waits for them, and re-layouts: 0.55 us -> 0.03 us
    ppermute x9, starting transfers between devices: 13.2 us -> 12.7 us  [swapped(): lax.ppermute(x, axis, [(i, i ^ distance) for i in range(lax.axis_size(axi...]
  transfers between devices with their start and end apart: 11 -> 11, of which waited for: 3 -> 4; matrix products, arithmetic and copies ran while one was open for 0% -> 0% of each run, Pallas kernels for 10% -> 11%
where the time goes in v4:
time: 34.3 us; the launch traced here: 34.1 us
  starting transfers between devices  16.7 us (49%)
  Pallas kernels  10.3 us (30%)
  waiting for transfers between devices  5.62 us (16%)
  between operations  1.5 us (4%)
    ppermute x9, starting transfers between devices, swapped(): lax.ppermute(x, axis, [(i, i ^ distance) for i in range(lax.axis_size(axi...  12.7 us
    ppermute x9, waiting for transfers between devices, swapped(): lax.ppermute(x, axis, [(i, i ^ distance) for i in range(lax.axis_size(axi...  5.61 us
    pallas_call x1, Pallas kernels, per_device(): pl.pallas_call(lambda *refs: first_kernel(side, *refs), name='first', out...  4.57 us
    ppermute x1, starting transfers between devices, per_device(): second = lax.ppermute(tiny, line, [(i, i + 2) for i in range(line_n - 2)])  2.53 us
    pallas_call x1, Pallas kernels, per_device(): pl.pallas_call(lambda *refs: main_kernel(part_n, *refs), name='main', out...  1.89 us
    ppermute x1, starting transfers between devices, per_device(): prior = lax.ppermute(border, line, [(i, i + 1) for i in range(line_n - 1)])  1.44 us
    pallas_call x1, Pallas kernels, per_device(): pl.pallas_call(lambda *refs: rest_kernel(part_n, *refs), name='rest', out...  1.06 us
    pallas_call x1, Pallas kernels, per_device(): pl.pallas_call(lambda *refs: merge_kernel(head_n, *refs), name='merge', o...  0.97 us
  transfers between devices with their start and end apart: 11, of which 4 were waited for; matrix products, arithmetic and copies ran while one was open for 0% of the time, Pallas kernels for 11%

profile of v4, /device:TPU:0, one launch (start us, length us, event | category | flops | bytes accessed | tf_op | source)
XLA Modules:
  0.0 34.1 jit_solution(15402622039844172100)
XLA Ops:
  0.0 0.0 copy-start.1
  0.0 0.0 copy-start
  1.4 4.6 %first.1 = (bf16[272,256]{1,0:T(8,128)(2,1)}, f32[136,128]{1,0:T(8,128)}, bf16[144,256]{1,0:T(8,128)(2,1)}, bf16[32,256]{1,0:T(8,128)(2,1)}) custom-call(s32[1,1]{1,0:T(1,128)} %bitcast.1.refs_0_, s32[1,3]{1,0:T(1,128)} %refs_1_.2, bf16[64,192]{1,0:T(8,128)(2,1)} %bitcast.11, bf16[576,32]{1,0:T(8,128)(2,1)} %bitcast.8, bf16[1152,64]{1,0:T(8,128)(2,1)} %bitcast.6, ...), custom_call_target="tpu_custom_call" | custom-call | tf_op jit(solution)/shard_map/first/pallas_call | solution.py:425
  5.9 3.0 %collective-permute-start.2 = (bf16[272,256]{1,0:T(8,128)(2,1)}, bf16[272,256]{1,0:T(8,128)(2,1)S(1)}, u32[]{:S(2)}, u32[]{:S(2)}) collective-permute-start(bf16[272,256]{1,0:T(8,128)(2,1)} %get-tuple-element.34.refs_1_), channel_id=1, source_target_pairs={{0,2},{1,3},{2,0},{3,1},{4,6},{5,7},{6,4},{7,5},{8,10},{9,11},{10,... | collective-permute-start | bytes 417800 | tf_op jit(solution)/shard_map/ppermute | solution.py:405
  8.9 1.4 %collective-permute-start = (bf16[144,256]{1,0:T(8,128)(2,1)}, bf16[144,256]{1,0:T(8,128)(2,1)S(1)}, u32[]{:S(2)}, u32[]{:S(2)}) collective-permute-start(bf16[144,256]{1,0:T(8,128)(2,1)} %get-tuple-element.33), channel_id=1, source_target_pairs={{0,1},{1,2},{2,3},{3,4},{4,5},{5,6},{6,7},{7,8},{8,9},{9,10},{10,1... | collective-permute-start | bytes 221192 | tf_op jit(solution)/shard_map/ppermute | solution.py:462
  10.4 0.0 copy-start.2
  10.4 0.0 copy-start.6
  10.4 2.5 %collective-permute-start.4 = (bf16[32,256]{1,0:T(8,128)(2,1)}, bf16[32,256]{1,0:T(8,128)(2,1)S(1)}, u32[]{:S(2)}, u32[]{:S(2)}) collective-permute-start(bf16[32,256]{1,0:T(8,128)(2,1)} %get-tuple-element.40), channel_id=1, source_target_pairs={{0,2},{1,3},{2,4},{3,5},{4,6},{5,7},{6,8},{7,9},{8,10},{9,11},{10,... | collective-permute-start | bytes 49160 | tf_op jit(solution)/shard_map/ppermute | solution.py:463
  12.9 0.0 copy-done.1
  13.0 0.0 copy-done
  13.0 0.4 %expand.1 = (bf16[256,512]{1,0:T(8,128)(2,1)S(1)}, bf16[512,1024]{1,0:T(8,128)(2,1)S(1)}) custom-call(bf16[576,32]{1,0:T(8,128)(2,1)S(1)} %bitcast.9, bf16[1152,64]{1,0:T(8,128)(2,1)S(1)} %bitcast.7), custom_call_target="tpu_custom_call" | custom-call | flops 1000000000 | bytes 4000000 | tf_op jit(solution)/shard_map/expand/pallas_call | solution.py:465
  13.3 0.0 collective-permute-done.prior_ref
  13.3 0.0 copy-done.2
  13.3 2.9 %collective-permute-start.1 = (bf16[272,256]{1,0:T(8,128)(2,1)S(1)}, bf16[272,256]{1,0:T(8,128)(2,1)S(1)}, u32[]{:S(2)}, u32[]{:S(2)}) collective-permute-start(bf16[272,256]{1,0:T(8,128)(2,1)S(1)} %copy-done.2), channel_id=1, source_target_pairs={{0,1},{1,0},{2,3},{3,2},{4,5},{5,4},{6,7},{7,6},{8,9},{9,8},{10,11... | collective-permute-start | bytes 417800 | tf_op jit(solution)/shard_map/ppermute | solution.py:405
  16.2 0.0 collective-permute-done.2.refs_3_
  16.3 0.1 collective-permute-start.3
  16.3 0.0 collective-permute-done.4.second_ref
  16.3 0.0 copy-done.6
  16.3 0.0 copy-start.3
  16.3 0.0 copy-start.4
  16.4 0.0 copy-start.5
  16.4 0.6 %rim.1.refs_1_ = bf16[48,256]{1,0:T(8,128)(2,1)S(1)} custom-call(f32[136,128]{1,0:T(8,128)S(1)} %copy-done.6, bf16[144,256]{1,0:T(8,128)(2,1)S(1)} %collective-permute-done.prior_ref, bf16[32,256]{1,0:T(8,128)(2,1)S(1)} %collective-permute-done.4.second_ref, bf16[256,512]{1,0:T(8,128)(2,1)S(1)} %get-tuple-element.41.dense1_ref, ...), custom_call_target="tpu_custom_call" | custom-call | flops 20000000000 | bytes 40000000 | tf_op jit(solution)/shard_map/rim/pallas_call | solution.py:479
  17.0 1.3 %collective-permute-start.5 = (bf16[48,256]{1,0:T(8,128)(2,1)S(1)}, bf16[48,256]{1,0:T(8,128)(2,1)S(1)}, u32[]{:S(2)}, u32[]{:S(2)}) collective-permute-start(bf16[48,256]{1,0:T(8,128)(2,1)S(1)} %rim.1.refs_1_), channel_id=1, source_target_pairs={{0,2},{1,3},{2,0},{3,1},{4,6},{5,7},{6,4},{7,5},{8,10},{9,11},{10,... | collective-permute-start | bytes 73736 | tf_op jit(solution)/shard_map/ppermute | solution.py:405
  18.3 1.0 %collective-permute-start.6 = (bf16[48,256]{1,0:T(8,128)(2,1)S(1)}, bf16[48,256]{1,0:T(8,128)(2,1)S(1)}, u32[]{:S(2)}, u32[]{:S(2)}) collective-permute-start(bf16[48,256]{1,0:T(8,128)(2,1)S(1)} %rim.1.refs_1_), channel_id=1, source_target_pairs={{0,1},{1,0},{2,3},{3,2},{4,5},{5,4},{6,7},{7,6},{8,9},{9,8},{10,11... | collective-permute-start | bytes 73736 | tf_op jit(solution)/shard_map/ppermute | solution.py:405
  19.3 0.0 collective-permute-start.7
  19.3 0.0 collective-permute-done.1.refs_2_
  19.3 0.0 collective-permute-done.3.refs_4_
  19.3 0.0 copy-done.3
  19.3 0.0 copy-done.4
  19.3 0.0 copy-done.5
  19.3 1.9 %main.1 = (f32[384,128]{1,0:T(8,128)S(1)}, f32[384,128]{1,0:T(8,128)S(1)}, bf16[1024,128]{1,0:T(8,128)(2,1)S(1)}, bf16[1024,128]{1,0:T(8,128)(2,1)S(1)}, f32[8,1024]{1,0:T(8,128)S(1)}) custom-call(s32[1]{0:T(128)} %bitcast.refs_0_, bf16[272,256]{1,0:T(8,128)(2,1)S(1)} %copy-done.2, bf16[272,256]{1,0:T(8,128)(2,1)S(1)} %collective-permute-done.1.refs_2_, ...), custom_call_target="tpu_custom_call" | custom-call | flops 1000000 | bytes 10000 | tf_op jit(solution)/shard_map/main/pallas_call | solution.py:504
  21.2 0.0 collective-permute-done.5.refs_2_
  21.2 0.0 collective-permute-done.6.refs_3_
  21.3 1.3 %collective-permute-done.7.refs_4_ = bf16[48,256]{1,0:T(8,128)(2,1)S(1)} collective-permute-done((bf16[48,256]{1,0:T(8,128)(2,1)S(1)}, bf16[48,256]{1,0:T(8,128)(2,1)S(1)}, u32[]{:S(2)}, u32[]{:S(2)}) %collective-permute-start.7) | collective-permute-done | bytes 24608 | tf_op jit(solution)/shard_map/ppermute | solution.py:405
  22.6 1.1 %rest.1 = (bf16[128,128]{1,0:T(8,128)(2,1)S(1)}, bf16[128,128]{1,0:T(8,128)(2,1)S(1)}, f32[8,128]{1,0:T(8,128)S(1)}, f32[136,128]{1,0:T(8,128)S(1)}, f32[136,128]{1,0:T(8,128)S(1)}, /*index=5*/f32[136,128]{1,0:T(8,128)S(1)}) custom-call(s32[1]{0:T(128)} %bitcast.refs_0_, bf16[48,256]{1,0:T(8,128)(2,1)S(1)} %rim.1.refs_1_, ...), custom_call_target="tpu_custom_call" | custom-call | flops 20000000000 | bytes 40000000 | tf_op jit(solution)/shard_map/rest/pallas_call | solution.py:519
  23.7 3.6 %collective-permute-start.10 = (f32[136,128]{1,0:T(8,128)S(1)}, f32[136,128]{1,0:T(8,128)S(1)}, u32[]{:S(2)}, u32[]{:S(2)}) collective-permute-start(f32[136,128]{1,0:T(8,128)S(1)} %get-tuple-element.50), channel_id=1, source_target_pairs={{0,12},{4,8},{8,4},{12,0},{1,13},{5,9},{9,5},{13,1},{2,14},{6,10},... | collective-permute-start | bytes 208904 | tf_op jit(solution)/shard_map/ppermute | solution.py:405
  27.3 0.0 collective-permute-start.8
  27.3 0.8 %collective-permute-start.9 = (f32[136,128]{1,0:T(8,128)S(1)}, f32[136,128]{1,0:T(8,128)S(1)}, u32[]{:S(2)}, u32[]{:S(2)}) collective-permute-start(f32[136,128]{1,0:T(8,128)S(1)} %get-tuple-element.49), channel_id=1, source_target_pairs={{0,8},{4,12},{8,0},{12,4},{1,9},{5,13},{9,1},{13,5},{2,10},{6,14},... | collective-permute-start | bytes 208904 | tf_op jit(solution)/shard_map/ppermute | solution.py:405
  28.1 0.8 %own.1.refs_0_ = f32[136,128]{1,0:T(8,128)S(1)} custom-call(s32[1]{0:T(128)} %bitcast.refs_0_, bf16[512,128]{1,0:T(8,128)(2,1)S(1)} %copy-done.3, bf16[1024,128]{1,0:T(8,128)(2,1)S(1)} %get-tuple-element.35.refs_2_, bf16[1024,128]{1,0:T(8,128)(2,1)S(1)} %get-tuple-element.36.refs_3_, f32[8,1024]{1,0:T(8,128)S(1)} %get-tuple-element.37.refs_4_, ...), custom_call_target="tpu_custom_call" | custom-call | flops 1000000000 | bytes 4000000 | tf_op jit(solution)/shard_map/own/pallas_call | solution.py:534
  28.9 1.7 %collective-permute-done.10.refs_3_ = f32[136,128]{1,0:T(8,128)S(1)} collective-permute-done((f32[136,128]{1,0:T(8,128)S(1)}, f32[136,128]{1,0:T(8,128)S(1)}, u32[]{:S(2)}, u32[]{:S(2)}) %collective-permute-start.10) | collective-permute-done | bytes 69664 | tf_op jit(solution)/shard_map/ppermute | solution.py:405
  30.5 1.8 %collective-permute-done.8.refs_1_ = f32[136,128]{1,0:T(8,128)S(1)} collective-permute-done((f32[136,128]{1,0:T(8,128)S(1)}, f32[136,128]{1,0:T(8,128)S(1)}, u32[]{:S(2)}, u32[]{:S(2)}) %collective-permute-start.8) | collective-permute-done | bytes 69664 | tf_op jit(solution)/shard_map/ppermute | solution.py:405
  32.4 0.8 %collective-permute-done.9.refs_2_ = f32[136,128]{1,0:T(8,128)S(1)} collective-permute-done((f32[136,128]{1,0:T(8,128)S(1)}, f32[136,128]{1,0:T(8,128)S(1)}, u32[]{:S(2)}, u32[]{:S(2)}) %collective-permute-start.9) | collective-permute-done | bytes 69664 | tf_op jit(solution)/shard_map/ppermute | solution.py:405
  33.2 1.0 %merge.1 = bf16[128,128]{1,0:T(8,128)(2,1)} custom-call(f32[136,128]{1,0:T(8,128)S(1)} %own.1.refs_0_, f32[136,128]{1,0:T(8,128)S(1)} %collective-permute-done.8.refs_1_, f32[136,128]{1,0:T(8,128)S(1)} %collective-permute-done.9.refs_2_, f32[136,128]{1,0:T(8,128)S(1)} %collective-permute-done.10.refs_3_), custom_call_target="tpu_custom_call" | custom-call | tf_op jit(solution)/shard_map/merge/pallas_call | solution.py:547
Async XLA Ops:
  0.0 12.9 %copy-start.1 = (bf16[4,9,16,32]{3,2,1,0:T(8,128)(2,1)S(1)}, bf16[4,9,16,32]{3,2,1,0:T(8,128)(2,1)}, u32[]{:S(2)}) copy-start(bf16[4,9,16,32]{3,2,1,0:T(8,128)(2,1)} %param.12) | copy-start | bytes 110596
  0.0 13.0 %copy-start = (bf16[4,9,32,64]{3,2,1,0:T(8,128)(2,1)S(1)}, bf16[4,9,32,64]{3,2,1,0:T(8,128)(2,1)}, u32[]{:S(2)}) copy-start(bf16[4,9,32,64]{3,2,1,0:T(8,128)(2,1)} %param.13) | copy-start | bytes 442372
  5.9 10.3 %collective-permute-start.2 = (bf16[272,256]{1,0:T(8,128)(2,1)}, bf16[272,256]{1,0:T(8,128)(2,1)S(1)}, u32[]{:S(2)}, u32[]{:S(2)}) collective-permute-start(bf16[272,256]{1,0:T(8,128)(2,1)} %get-tuple-element.34.refs_1_), channel_id=1, source_target_pairs={{0,2},{1,3},{2,0},{3,1},{4,6},{5,7},{6,4},{7,5},{8,10},{9,11},{10,... | collective-permute-start | bytes 417800 | tf_op jit(solution)/shard_map/ppermute | solution.py:405
  8.9 4.4 %collective-permute-start = (bf16[144,256]{1,0:T(8,128)(2,1)}, bf16[144,256]{1,0:T(8,128)(2,1)S(1)}, u32[]{:S(2)}, u32[]{:S(2)}) collective-permute-start(bf16[144,256]{1,0:T(8,128)(2,1)} %get-tuple-element.33), channel_id=1, source_target_pairs={{0,1},{1,2},{2,3},{3,4},{4,5},{5,6},{6,7},{7,8},{8,9},{9,10},{10,1... | collective-permute-start | bytes 221192 | tf_op jit(solution)/shard_map/ppermute | solution.py:462
  10.4 2.9 %copy-start.2 = (bf16[272,256]{1,0:T(8,128)(2,1)S(1)}, bf16[272,256]{1,0:T(8,128)(2,1)}, u32[]{:S(2)}) copy-start(bf16[272,256]{1,0:T(8,128)(2,1)} %get-tuple-element.34.refs_1_) | copy-start | bytes 417796
  10.4 5.9 %copy-start.6 = (f32[136,128]{1,0:T(8,128)S(1)}, f32[136,128]{1,0:T(8,128)}, u32[]{:S(2)}) copy-start(f32[136,128]{1,0:T(8,128)} %get-tuple-element.38.edge_ref) | copy-start | bytes 208900
  10.4 5.9 %collective-permute-start.4 = (bf16[32,256]{1,0:T(8,128)(2,1)}, bf16[32,256]{1,0:T(8,128)(2,1)S(1)}, u32[]{:S(2)}, u32[]{:S(2)}) collective-permute-start(bf16[32,256]{1,0:T(8,128)(2,1)} %get-tuple-element.40), channel_id=1, source_target_pairs={{0,2},{1,3},{2,4},{3,5},{4,6},{5,7},{6,8},{7,9},{8,10},{9,11},{10,... | collective-permute-start | bytes 49160 | tf_op jit(solution)/shard_map/ppermute | solution.py:463
  13.3 6.0 %collective-permute-start.1 = (bf16[272,256]{1,0:T(8,128)(2,1)S(1)}, bf16[272,256]{1,0:T(8,128)(2,1)S(1)}, u32[]{:S(2)}, u32[]{:S(2)}) collective-permute-start(bf16[272,256]{1,0:T(8,128)(2,1)S(1)} %copy-done.2), channel_id=1, source_target_pairs={{0,1},{1,0},{2,3},{3,2},{4,5},{5,4},{6,7},{7,6},{8,9},{9,8},{10,11... | collective-permute-start | bytes 417800 | tf_op jit(solution)/shard_map/ppermute | solution.py:405
  16.3 3.1 %collective-permute-start.3 = (bf16[272,256]{1,0:T(8,128)(2,1)S(1)}, bf16[272,256]{1,0:T(8,128)(2,1)S(1)}, u32[]{:S(2)}, u32[]{:S(2)}) collective-permute-start(bf16[272,256]{1,0:T(8,128)(2,1)S(1)} %collective-permute-done.2.refs_3_), channel_id=1, source_target_pairs={{0,1},{1,0},{2,3},{3,2},{4,5},{5,4},{6,7},{7,6},{8,9},{9,8},{10,11... | collective-permute-start | bytes 417800 | tf_op jit(solution)/shard_map/ppermute | solution.py:405
  16.3 3.0 %copy-start.3 = (bf16[512,128]{1,0:T(8,128)(2,1)S(1)}, bf16[512,128]{1,0:T(8,128)(2,1)}, u32[]{:S(2)}) copy-start(bf16[512,128]{1,0:T(8,128)(2,1)} %refs_1_.3) | copy-start | bytes 393220
  16.3 3.0 %copy-start.4 = (bf16[256,128]{1,0:T(8,128)(2,1)S(1)}, bf16[256,128]{1,0:T(8,128)(2,1)}, u32[]{:S(2)}) copy-start(bf16[256,128]{1,0:T(8,128)(2,1)} %refs_5_.3) | copy-start | bytes 196612
  16.4 3.0 %copy-start.5 = (bf16[256,128]{1,0:T(8,128)(2,1)S(1)}, bf16[256,128]{1,0:T(8,128)(2,1)}, u32[]{:S(2)}) copy-start(bf16[256,128]{1,0:T(8,128)(2,1)} %refs_6_.3) | copy-start | bytes 196612
  17.0 4.3 %collective-permute-start.5 = (bf16[48,256]{1,0:T(8,128)(2,1)S(1)}, bf16[48,256]{1,0:T(8,128)(2,1)S(1)}, u32[]{:S(2)}, u32[]{:S(2)}) collective-permute-start(bf16[48,256]{1,0:T(8,128)(2,1)S(1)} %rim.1.refs_1_), channel_id=1, source_target_pairs={{0,2},{1,3},{2,0},{3,1},{4,6},{5,7},{6,4},{7,5},{8,10},{9,11},{10,... | collective-permute-start | bytes 73736 | tf_op jit(solution)/shard_map/ppermute | solution.py:405
  18.3 3.0 %collective-permute-start.6 = (bf16[48,256]{1,0:T(8,128)(2,1)S(1)}, bf16[48,256]{1,0:T(8,128)(2,1)S(1)}, u32[]{:S(2)}, u32[]{:S(2)}) collective-permute-start(bf16[48,256]{1,0:T(8,128)(2,1)S(1)} %rim.1.refs_1_), channel_id=1, source_target_pairs={{0,1},{1,0},{2,3},{3,2},{4,5},{5,4},{6,7},{7,6},{8,9},{9,8},{10,11... | collective-permute-start | bytes 73736 | tf_op jit(solution)/shard_map/ppermute | solution.py:405
  19.3 3.3 %collective-permute-start.7 = (bf16[48,256]{1,0:T(8,128)(2,1)S(1)}, bf16[48,256]{1,0:T(8,128)(2,1)S(1)}, u32[]{:S(2)}, u32[]{:S(2)}) collective-permute-start(bf16[48,256]{1,0:T(8,128)(2,1)S(1)} %rim.1.refs_1_), channel_id=1, source_target_pairs={{0,3},{1,2},{2,1},{3,0},{4,7},{5,6},{6,5},{7,4},{8,11},{9,10},{10,... | collective-permute-start | bytes 73736 | tf_op jit(solution)/shard_map/ppermute | solution.py:405
  23.7 6.9 %collective-permute-start.10 = (f32[136,128]{1,0:T(8,128)S(1)}, f32[136,128]{1,0:T(8,128)S(1)}, u32[]{:S(2)}, u32[]{:S(2)}) collective-permute-start(f32[136,128]{1,0:T(8,128)S(1)} %get-tuple-element.50), channel_id=1, source_target_pairs={{0,12},{4,8},{8,4},{12,0},{1,13},{5,9},{9,5},{13,1},{2,14},{6,10},... | collective-permute-start | bytes 208904 | tf_op jit(solution)/shard_map/ppermute | solution.py:405
  27.3 5.1 %collective-permute-start.8 = (f32[136,128]{1,0:T(8,128)S(1)}, f32[136,128]{1,0:T(8,128)S(1)}, u32[]{:S(2)}, u32[]{:S(2)}) collective-permute-start(f32[136,128]{1,0:T(8,128)S(1)} %get-tuple-element.48), channel_id=1, source_target_pairs={{0,4},{4,0},{8,12},{12,8},{1,5},{5,1},{9,13},{13,9},{2,6},{6,2},{1... | collective-permute-start | bytes 208904 | tf_op jit(solution)/shard_map/ppermute | solution.py:405
  27.3 5.9 %collective-permute-start.9 = (f32[136,128]{1,0:T(8,128)S(1)}, f32[136,128]{1,0:T(8,128)S(1)}, u32[]{:S(2)}, u32[]{:S(2)}) collective-permute-start(f32[136,128]{1,0:T(8,128)S(1)} %get-tuple-element.49), channel_id=1, source_target_pairs={{0,8},{4,12},{8,0},{12,4},{1,9},{5,13},{9,1},{13,5},{2,10},{6,14},... | collective-permute-start | bytes 208904 | tf_op jit(solution)/shard_map/ppermute | solution.py:405

commit v5 on v4

--- a/solution.py
+++ b/solution.py
@@ -13,8 +13,7 @@
 VMEM = pltpu.VMEM
 SMEM = pltpu.SMEM
 MIB = 1 << 20
-FIRST_VMEM = 60 * MIB
-PACK = 1 << 16
+FIRST_VMEM = 20 * MIB
 ORDER = (3, 0, 2, 1)
 
 
@@ -79,22 +78,20 @@
     expand_weights(w2_ref[...], w2_ref.shape[0] // 36, w2_ref.shape[1], dense2_ref, ORDER)
 
 
-def first_kernel(side, packed_any, adjacency_any, w_any, w1_any, w2_any, pixels_any, token_ref,
-                 edge_ref, border_ref, tiny_ref, packed, adjacency, weight, w1, w2, pixels,
-                 cells_ref, even_lines, odd_lines, dense1_ref, dense2_ref, wide1, partial, cells,
-                 wide2, sems):
-    copies = [
-        pltpu.make_async_copy(source, target, sems.at[k])
-        for k, (source, target) in enumerate((
-            (w1_any, w1), (w2_any, w2), (pixels_any, pixels), (w_any, weight),
-            (packed_any, packed), (adjacency_any, adjacency),
-        ))
-    ]
-    for copy in copies:
-        copy.start()
-    copies[0].wait()
+def opening_kernel(out_ref):
+    out_ref[...] = jnp.zeros_like(out_ref)
+
+
+def counts_kernel(count_ref, tissue_ref, opened_ref, out_ref):
+    live = (count_ref[0] > 0).astype(F32)
+    row = lax.broadcasted_iota(jnp.int32, out_ref.shape, 0)
+    out_ref[...] = jnp.where(row == 0, live, live * tissue_ref[0].astype(F32))
+
+
+def first_kernel(side, counts_ref, adjacency_ref, weight, w1, w2, pixels, token_ref,
+                 edge_ref, border_ref, tiny_ref, cells_ref, even_lines, odd_lines, dense1_ref,
+                 dense2_ref, wide1, partial, cells, wide2):
     expand_weights(w1[...], w1.shape[0] // 36, w1.shape[1], dense1_ref)
-    copies[1].wait()
     expand_weights(w2[...], w2.shape[0] // 36, w2.shape[1], dense2_ref, ORDER)
     stem_n, half = weight.shape[0], side // 2
     rows, span = 4 * half, 4 * side
@@ -103,14 +100,11 @@
     line = 2 * lax.div(lax.rem(row, 2 * half), half) + lax.div(row, 2 * half)
     wanted = line * side + 2 * lax.rem(row, half)
     pick = (lax.rem(column, span) == wanted + lax.div(column, span)).astype(BF16)
-    for copy in copies[2:]:
-        copy.wait()
-    live = (packed[0, 0] >= PACK).astype(F32)
-    tissue = lax.rem(packed[0, 0], PACK)
-    gates = [(adjacency[0, k] == 0).astype(F32) for k in range(3)]
+    live, known = counts_ref[pl.ds(0, 1), pl.ds(0, 1)], counts_ref[pl.ds(1, 1), pl.ds(0, 1)]
+    gates = [(adjacency_ref[:, k : k + 1] == 0).astype(F32) for k in range(3)]
     row = lax.broadcasted_iota(jnp.int32, (16, cells_ref.shape[1]), 0)
     facts = jnp.zeros(row.shape, F32)
-    for k, fact in enumerate([live] + gates + [live * tissue.astype(F32)]):
+    for k, fact in enumerate([live] + gates + [known]):
         facts = jnp.where(row == k, fact, facts)
     cells_ref[pl.ds(half * half, 16)] = facts.astype(BF16)
     border_ref[pl.ds(4 * half, 16)] = facts.astype(BF16)
@@ -422,6 +416,25 @@
     w1 = w_conv1.reshape(groups * 9 * in1, out1)
     w2 = w_conv2.reshape(groups * 9 * in2, out2)
     dense_shapes = ((4 * channels, 4 * mid_n), (4 * mid_n, 4 * out_n))
+    opened = pl.pallas_call(
+        opening_kernel,
+        name="opening",
+        out_shape=jax.ShapeDtypeStruct((8, 128), F32),
+        out_specs=vmem_spec(),
+        compiler_params=pltpu.CompilerParams(vmem_limit_bytes=1 * MIB),
+        cost_estimate=pl.CostEstimate(
+            flops=20 * 10**9, bytes_accessed=4 * 10**7, transcendentals=0
+        ),
+    )()
+    opened, tile_count, tissue = lax.optimization_barrier((opened, tile_count, tissue))
+    counts = pl.pallas_call(
+        counts_kernel,
+        name="counts",
+        out_shape=jax.ShapeDtypeStruct((8, 128), F32),
+        in_specs=[smem_spec()] * 2 + [vmem_spec()],
+        out_specs=vmem_spec(),
+        compiler_params=pltpu.CompilerParams(vmem_limit_bytes=1 * MIB),
+    )(tile_count, tissue, opened)
     message, edge, border, tiny = pl.pallas_call(
         lambda *refs: first_kernel(side, *refs),
         name="first",
@@ -431,15 +444,9 @@
             jax.ShapeDtypeStruct((border_rows, 4 * channels), BF16),
             jax.ShapeDtypeStruct((32, 4 * channels), BF16),
         ),
-        in_specs=[pl.BlockSpec(memory_space=pl.ANY)] * 6,
+        in_specs=[vmem_spec()] * 6,
         out_specs=(vmem_spec(),) * 4,
         scratch_shapes=[
-            SMEM((1, 1), jnp.int32),
-            SMEM((1, 3), jnp.int32),
-            VMEM((channels, patch), BF16),
-            VMEM(w1.shape, BF16),
-            VMEM(w2.shape, BF16),
-            VMEM((1, patch, area), BF16),
             VMEM((half * half + 16, 4 * channels), BF16),
             VMEM((half * half, 2 * channels), F32),
             VMEM((half * half, 2 * channels), F32),
@@ -449,11 +456,10 @@
             VMEM((half * half, mid_n), F32),
             VMEM((tokens, 4 * mid_n), BF16),
             VMEM((tokens + quarter, 4 * out_n), F32),
-            pltpu.SemaphoreType.DMA((6,)),
         ],
         compiler_params=pltpu.CompilerParams(vmem_limit_bytes=FIRST_VMEM),
     )(
-        (tile_count * PACK + tissue).reshape(1, 1), adjacency, w_stem.T, w1, w2,
+        counts, adjacency, w_stem.T, w1, w2,
         jnp.swapaxes(pixels, 1, 2),
     )
 

time: 34.3 us -> 32 us (0.933)
  Pallas kernels: 10.3 us -> 8.04 us
    pallas_call x1, Pallas kernels: 4.57 us -> 2.34 us  [per_device(): pl.pallas_call(lambda *refs: first_kernel(side, *refs), name='first', out...]
  transfers between devices with their start and end apart: 11 -> 11, of which waited for: 4 -> 4; matrix products, arithmetic and copies ran while one was open for 0% -> 0% of each run, Pallas kernels for 11% -> 12%
where the time goes in v5:
time: 32 us; the launch traced here: 31.8 us
  starting transfers between devices  16.5 us (52%)
  Pallas kernels  8.04 us (25%)
  waiting for transfers between devices  5.54 us (17%)
  between operations  1.59 us (5%)
    ppermute x9, starting transfers between devices, swapped(): lax.ppermute(x, axis, [(i, i ^ distance) for i in range(lax.axis_size(axi...  12.6 us
    ppermute x9, waiting for transfers between devices, swapped(): lax.ppermute(x, axis, [(i, i ^ distance) for i in range(lax.axis_size(axi...  5.53 us
    ppermute x1, starting transfers between devices, per_device(): second = lax.ppermute(tiny, line, [(i, i + 2) for i in range(line_n - 2)])  2.39 us
    pallas_call x1, Pallas kernels, per_device(): pl.pallas_call(lambda *refs: first_kernel(side, *refs), name='first', out...  2.34 us
    pallas_call x1, Pallas kernels, per_device(): pl.pallas_call(lambda *refs: main_kernel(part_n, *refs), name='main', out...  1.88 us
    ppermute x1, starting transfers between devices, per_device(): prior = lax.ppermute(border, line, [(i, i + 1) for i in range(line_n - 1)])  1.45 us
    pallas_call x1, Pallas kernels, per_device(): pl.pallas_call(lambda *refs: rest_kernel(part_n, *refs), name='rest', out...  1.06 us
    pallas_call x1, Pallas kernels, per_device(): pl.pallas_call(lambda *refs: merge_kernel(head_n, *refs), name='merge', o...  0.97 us
  transfers between devices with their start and end apart: 11, of which 4 were waited for; matrix products, arithmetic and copies ran while one was open for 0% of the time, Pallas kernels for 12%

profile of v5, /device:TPU:0, one launch (start us, length us, event | category | flops | bytes accessed | tf_op | source)
XLA Modules:
  0.0 31.8 jit_solution(327604281582268710)
XLA Ops:
  0.0 0.0 copy-start.2
  0.0 0.0 copy-start.1
  0.0 0.0 copy-start.6
  0.0 0.0 copy-start
  0.0 0.0 copy-start.7
  1.5 0.0 copy-done.2
  1.5 0.0 copy-done.1
  1.5 0.0 copy-done.6
  1.5 0.1 copy-done
  1.6 0.0 copy-done.7
  1.6 2.3 %first.1 = (bf16[272,256]{1,0:T(8,128)(2,1)S(1)}, f32[136,128]{1,0:T(8,128)S(1)}, bf16[144,256]{1,0:T(8,128)(2,1)S(1)}, bf16[32,256]{1,0:T(8,128)(2,1)S(1)}) custom-call(f32[8,128]{1,0:T(8,128)S(1)} %counts.1.refs_0_, s32[1,3]{1,0:T(1,128)S(1)} %copy-done.7, bf16[64,192]{1,0:T(8,128)(2,1)S(1)} %bitcast.10, bf16[576,32]{1,0:T(8,128)(2,1)S(1)} %bitcast.8, ...), custom_call_target="tpu_custom_call" | custom-call | tf_op jit(solution)/shard_map/first/pallas_call | solution.py:438
  4.0 3.0 %collective-permute-start.2 = (bf16[272,256]{1,0:T(8,128)(2,1)S(1)}, bf16[272,256]{1,0:T(8,128)(2,1)S(1)}, u32[]{:S(2)}, u32[]{:S(2)}) collective-permute-start(bf16[272,256]{1,0:T(8,128)(2,1)S(1)} %get-tuple-element.40.refs_1_), channel_id=1, source_target_pairs={{0,2},{1,3},{2,0},{3,1},{4,6},{5,7},{6,4},{7,5},{8,10},{9,11},{10,... | collective-permute-start | bytes 417800 | tf_op jit(solution)/shard_map/ppermute | solution.py:399
  7.0 1.5 %collective-permute-start = (bf16[144,256]{1,0:T(8,128)(2,1)S(1)}, bf16[144,256]{1,0:T(8,128)(2,1)S(1)}, u32[]{:S(2)}, u32[]{:S(2)}) collective-permute-start(bf16[144,256]{1,0:T(8,128)(2,1)S(1)} %get-tuple-element.39), channel_id=1, source_target_pairs={{0,1},{1,2},{2,3},{3,4},{4,5},{5,6},{6,7},{7,8},{8,9},{9,10},{10,1... | collective-permute-start | bytes 221192 | tf_op jit(solution)/shard_map/ppermute | solution.py:468
  8.4 2.4 %collective-permute-start.4 = (bf16[32,256]{1,0:T(8,128)(2,1)S(1)}, bf16[32,256]{1,0:T(8,128)(2,1)S(1)}, u32[]{:S(2)}, u32[]{:S(2)}) collective-permute-start(bf16[32,256]{1,0:T(8,128)(2,1)S(1)} %get-tuple-element.46), channel_id=1, source_target_pairs={{0,2},{1,3},{2,4},{3,5},{4,6},{5,7},{6,8},{7,9},{8,10},{9,11},{10,... | collective-permute-start | bytes 49160 | tf_op jit(solution)/shard_map/ppermute | solution.py:469
  10.8 0.4 %expand.1 = (bf16[256,512]{1,0:T(8,128)(2,1)S(1)}, bf16[512,1024]{1,0:T(8,128)(2,1)S(1)}) custom-call(bf16[576,32]{1,0:T(8,128)(2,1)S(1)} %bitcast.9, bf16[1152,64]{1,0:T(8,128)(2,1)S(1)} %bitcast.7), custom_call_target="tpu_custom_call" | custom-call | flops 1000000000 | bytes 4000000 | tf_op jit(solution)/shard_map/expand/pallas_call | solution.py:471
  11.2 0.0 collective-permute-done.prior_ref
  11.2 2.9 %collective-permute-start.1 = (bf16[272,256]{1,0:T(8,128)(2,1)S(1)}, bf16[272,256]{1,0:T(8,128)(2,1)S(1)}, u32[]{:S(2)}, u32[]{:S(2)}) collective-permute-start(bf16[272,256]{1,0:T(8,128)(2,1)S(1)} %get-tuple-element.40.refs_1_), channel_id=1, source_target_pairs={{0,1},{1,0},{2,3},{3,2},{4,5},{5,4},{6,7},{7,6},{8,9},{9,8},{10,11... | collective-permute-start | bytes 417800 | tf_op jit(solution)/shard_map/ppermute | solution.py:399
  14.1 0.0 collective-permute-done.2.refs_3_
  14.1 0.1 collective-permute-start.3
  14.2 0.0 collective-permute-done.4.second_ref
  14.2 0.0 copy-start.3
  14.2 0.0 copy-start.4
  14.2 0.0 copy-start.5
  14.2 0.6 %rim.1.refs_1_ = bf16[48,256]{1,0:T(8,128)(2,1)S(1)} custom-call(f32[136,128]{1,0:T(8,128)S(1)} %get-tuple-element.44.edge_ref, bf16[144,256]{1,0:T(8,128)(2,1)S(1)} %collective-permute-done.prior_ref, bf16[32,256]{1,0:T(8,128)(2,1)S(1)} %collective-permute-done.4.second_ref, bf16[256,512]{1,0:T(8,128)(2,1)S(1)} %get-tuple-element.47.dense1_ref, ...), custom_call_target="tpu_custom_call" | custom-call | flops 20000000000 | bytes 40000000 | tf_op jit(solution)/shard_map/rim/pallas_call | solution.py:485
  14.8 1.1 %collective-permute-start.5 = (bf16[48,256]{1,0:T(8,128)(2,1)S(1)}, bf16[48,256]{1,0:T(8,128)(2,1)S(1)}, u32[]{:S(2)}, u32[]{:S(2)}) collective-permute-start(bf16[48,256]{1,0:T(8,128)(2,1)S(1)} %rim.1.refs_1_), channel_id=1, source_target_pairs={{0,2},{1,3},{2,0},{3,1},{4,6},{5,7},{6,4},{7,5},{8,10},{9,11},{10,... | collective-permute-start | bytes 73736 | tf_op jit(solution)/shard_map/ppermute | solution.py:399
  16.0 1.0 %collective-permute-start.6 = (bf16[48,256]{1,0:T(8,128)(2,1)S(1)}, bf16[48,256]{1,0:T(8,128)(2,1)S(1)}, u32[]{:S(2)}, u32[]{:S(2)}) collective-permute-start(bf16[48,256]{1,0:T(8,128)(2,1)S(1)} %rim.1.refs_1_), channel_id=1, source_target_pairs={{0,1},{1,0},{2,3},{3,2},{4,5},{5,4},{6,7},{7,6},{8,9},{9,8},{10,11... | collective-permute-start | bytes 73736 | tf_op jit(solution)/shard_map/ppermute | solution.py:399
  16.9 0.1 collective-permute-start.7
  17.0 0.0 collective-permute-done.1.refs_2_
  17.0 0.0 collective-permute-done.3.refs_4_
  17.0 0.0 copy-done.3
  17.0 0.0 copy-done.4
  17.1 0.0 copy-done.5
  17.1 1.9 %main.1 = (f32[384,128]{1,0:T(8,128)S(1)}, f32[384,128]{1,0:T(8,128)S(1)}, bf16[1024,128]{1,0:T(8,128)(2,1)S(1)}, bf16[1024,128]{1,0:T(8,128)(2,1)S(1)}, f32[8,1024]{1,0:T(8,128)S(1)}) custom-call(s32[1]{0:T(128)} %bitcast.refs_0_, bf16[272,256]{1,0:T(8,128)(2,1)S(1)} %get-tuple-element.40.refs_1_, bf16[272,256]{1,0:T(8,128)(2,1)S(1)} %collective-permute-done.1.refs_2_, ...), custom_call_target="tpu_custom_call" | custom-call | flops 1000000 | bytes 10000 | tf_op jit(solution)/shard_map/main/pallas_call | solution.py:510
  19.0 0.0 collective-permute-done.5.refs_2_
  19.0 0.0 collective-permute-done.6.refs_3_
  19.0 1.3 %collective-permute-done.7.refs_4_ = bf16[48,256]{1,0:T(8,128)(2,1)S(1)} collective-permute-done((bf16[48,256]{1,0:T(8,128)(2,1)S(1)}, bf16[48,256]{1,0:T(8,128)(2,1)S(1)}, u32[]{:S(2)}, u32[]{:S(2)}) %collective-permute-start.7) | collective-permute-done | bytes 24608 | tf_op jit(solution)/shard_map/ppermute | solution.py:399
  20.3 1.1 %rest.1 = (bf16[128,128]{1,0:T(8,128)(2,1)S(1)}, bf16[128,128]{1,0:T(8,128)(2,1)S(1)}, f32[8,128]{1,0:T(8,128)S(1)}, f32[136,128]{1,0:T(8,128)S(1)}, f32[136,128]{1,0:T(8,128)S(1)}, /*index=5*/f32[136,128]{1,0:T(8,128)S(1)}) custom-call(s32[1]{0:T(128)} %bitcast.refs_0_, bf16[48,256]{1,0:T(8,128)(2,1)S(1)} %rim.1.refs_1_, ...), custom_call_target="tpu_custom_call" | custom-call | flops 20000000000 | bytes 40000000 | tf_op jit(solution)/shard_map/rest/pallas_call | solution.py:525
  21.3 3.6 %collective-permute-start.10 = (f32[136,128]{1,0:T(8,128)S(1)}, f32[136,128]{1,0:T(8,128)S(1)}, u32[]{:S(2)}, u32[]{:S(2)}) collective-permute-start(f32[136,128]{1,0:T(8,128)S(1)} %get-tuple-element.56), channel_id=1, source_target_pairs={{0,12},{4,8},{8,4},{12,0},{1,13},{5,9},{9,5},{13,1},{2,14},{6,10},... | collective-permute-start | bytes 208904 | tf_op jit(solution)/shard_map/ppermute | solution.py:399
  24.9 0.0 collective-permute-start.8
  24.9 0.8 %collective-permute-start.9 = (f32[136,128]{1,0:T(8,128)S(1)}, f32[136,128]{1,0:T(8,128)S(1)}, u32[]{:S(2)}, u32[]{:S(2)}) collective-permute-start(f32[136,128]{1,0:T(8,128)S(1)} %get-tuple-element.55), channel_id=1, source_target_pairs={{0,8},{4,12},{8,0},{12,4},{1,9},{5,13},{9,1},{13,5},{2,10},{6,14},... | collective-permute-start | bytes 208904 | tf_op jit(solution)/shard_map/ppermute | solution.py:399
  25.8 0.8 %own.1.refs_0_ = f32[136,128]{1,0:T(8,128)S(1)} custom-call(s32[1]{0:T(128)} %bitcast.refs_0_, bf16[512,128]{1,0:T(8,128)(2,1)S(1)} %copy-done.3, bf16[1024,128]{1,0:T(8,128)(2,1)S(1)} %get-tuple-element.41.refs_2_, bf16[1024,128]{1,0:T(8,128)(2,1)S(1)} %get-tuple-element.42.refs_3_, f32[8,1024]{1,0:T(8,128)S(1)} %get-tuple-element.43.refs_4_, ...), custom_call_target="tpu_custom_call" | custom-call | flops 1000000000 | bytes 4000000 | tf_op jit(solution)/shard_map/own/pallas_call | solution.py:540
  26.6 1.7 %collective-permute-done.10.refs_3_ = f32[136,128]{1,0:T(8,128)S(1)} collective-permute-done((f32[136,128]{1,0:T(8,128)S(1)}, f32[136,128]{1,0:T(8,128)S(1)}, u32[]{:S(2)}, u32[]{:S(2)}) %collective-permute-start.10) | collective-permute-done | bytes 69664 | tf_op jit(solution)/shard_map/ppermute | solution.py:399
  28.2 1.8 %collective-permute-done.8.refs_1_ = f32[136,128]{1,0:T(8,128)S(1)} collective-permute-done((f32[136,128]{1,0:T(8,128)S(1)}, f32[136,128]{1,0:T(8,128)S(1)}, u32[]{:S(2)}, u32[]{:S(2)}) %collective-permute-start.8) | collective-permute-done | bytes 69664 | tf_op jit(solution)/shard_map/ppermute | solution.py:399
  30.0 0.8 %collective-permute-done.9.refs_2_ = f32[136,128]{1,0:T(8,128)S(1)} collective-permute-done((f32[136,128]{1,0:T(8,128)S(1)}, f32[136,128]{1,0:T(8,128)S(1)}, u32[]{:S(2)}, u32[]{:S(2)}) %collective-permute-start.9) | collective-permute-done | bytes 69664 | tf_op jit(solution)/shard_map/ppermute | solution.py:399
  30.8 1.0 %merge.1 = bf16[128,128]{1,0:T(8,128)(2,1)} custom-call(f32[136,128]{1,0:T(8,128)S(1)} %own.1.refs_0_, f32[136,128]{1,0:T(8,128)S(1)} %collective-permute-done.8.refs_1_, f32[136,128]{1,0:T(8,128)S(1)} %collective-permute-done.9.refs_2_, f32[136,128]{1,0:T(8,128)S(1)} %collective-permute-done.10.refs_3_), custom_call_target="tpu_custom_call" | custom-call | tf_op jit(solution)/shard_map/merge/pallas_call | solution.py:553
  (2 shorter events, 0.0 us)
Async XLA Ops:
  0.0 1.5 %copy-start.2 = (bf16[4,9,16,32]{3,2,1,0:T(8,128)(2,1)S(1)}, bf16[4,9,16,32]{3,2,1,0:T(8,128)(2,1)}, u32[]{:S(2)}) copy-start(bf16[4,9,16,32]{3,2,1,0:T(8,128)(2,1)} %param.12) | copy-start | bytes 110596
  0.0 1.5 %copy-start.1 = (bf16[4,9,32,64]{3,2,1,0:T(8,128)(2,1)S(1)}, bf16[4,9,32,64]{3,2,1,0:T(8,128)(2,1)}, u32[]{:S(2)}) copy-start(bf16[4,9,32,64]{3,2,1,0:T(8,128)(2,1)} %param.13) | copy-start | bytes 442372
  0.0 1.5 %copy-start.6 = (bf16[192,64]{0,1:T(8,128)(2,1)S(1)}, bf16[192,64]{0,1:T(8,128)(2,1)}, u32[]{:S(2)}) copy-start(bf16[192,64]{0,1:T(8,128)(2,1)} %param.11) | copy-start | bytes 73732
  0.0 1.6 %copy-start = (bf16[1,4096,192]{1,2,0:T(8,128)(2,1)S(1)}, bf16[1,4096,192]{1,2,0:T(8,128)(2,1)}, u32[]{:S(2)}) copy-start(bf16[1,4096,192]{1,2,0:T(8,128)(2,1)} %param.10) | copy-start | bytes 4718596
  0.0 1.6 %copy-start.7 = (s32[1,3]{1,0:T(1,128)S(1)}, s32[1,3]{1,0:T(1,128)}, u32[]{:S(2)}) copy-start(s32[1,3]{1,0:T(1,128)} %refs_1_.2) | copy-start | bytes 40
  4.0 10.1 %collective-permute-start.2 = (bf16[272,256]{1,0:T(8,128)(2,1)S(1)}, bf16[272,256]{1,0:T(8,128)(2,1)S(1)}, u32[]{:S(2)}, u32[]{:S(2)}) collective-permute-start(bf16[272,256]{1,0:T(8,128)(2,1)S(1)} %get-tuple-element.40.refs_1_), channel_id=1, source_target_pairs={{0,2},{1,3},{2,0},{3,1},{4,6},{5,7},{6,4},{7,5},{8,10},{9,11},{10,... | collective-permute-start | bytes 417800 | tf_op jit(solution)/shard_map/ppermute | solution.py:399
  7.0 4.2 %collective-permute-start = (bf16[144,256]{1,0:T(8,128)(2,1)S(1)}, bf16[144,256]{1,0:T(8,128)(2,1)S(1)}, u32[]{:S(2)}, u32[]{:S(2)}) collective-permute-start(bf16[144,256]{1,0:T(8,128)(2,1)S(1)} %get-tuple-element.39), channel_id=1, source_target_pairs={{0,1},{1,2},{2,3},{3,4},{4,5},{5,6},{6,7},{7,8},{8,9},{9,10},{10,1... | collective-permute-start | bytes 221192 | tf_op jit(solution)/shard_map/ppermute | solution.py:468
  8.4 5.8 %collective-permute-start.4 = (bf16[32,256]{1,0:T(8,128)(2,1)S(1)}, bf16[32,256]{1,0:T(8,128)(2,1)S(1)}, u32[]{:S(2)}, u32[]{:S(2)}) collective-permute-start(bf16[32,256]{1,0:T(8,128)(2,1)S(1)} %get-tuple-element.46), channel_id=1, source_target_pairs={{0,2},{1,3},{2,4},{3,5},{4,6},{5,7},{6,8},{7,9},{8,10},{9,11},{10,... | collective-permute-start | bytes 49160 | tf_op jit(solution)/shard_map/ppermute | solution.py:469
  11.2 5.9 %collective-permute-start.1 = (bf16[272,256]{1,0:T(8,128)(2,1)S(1)}, bf16[272,256]{1,0:T(8,128)(2,1)S(1)}, u32[]{:S(2)}, u32[]{:S(2)}) collective-permute-start(bf16[272,256]{1,0:T(8,128)(2,1)S(1)} %get-tuple-element.40.refs_1_), channel_id=1, source_target_pairs={{0,1},{1,0},{2,3},{3,2},{4,5},{5,4},{6,7},{7,6},{8,9},{9,8},{10,11... | collective-permute-start | bytes 417800 | tf_op jit(solution)/shard_map/ppermute | solution.py:399
  14.1 2.9 %collective-permute-start.3 = (bf16[272,256]{1,0:T(8,128)(2,1)S(1)}, bf16[272,256]{1,0:T(8,128)(2,1)S(1)}, u32[]{:S(2)}, u32[]{:S(2)}) collective-permute-start(bf16[272,256]{1,0:T(8,128)(2,1)S(1)} %collective-permute-done.2.refs_3_), channel_id=1, source_target_pairs={{0,1},{1,0},{2,3},{3,2},{4,5},{5,4},{6,7},{7,6},{8,9},{9,8},{10,11... | collective-permute-start | bytes 417800 | tf_op jit(solution)/shard_map/ppermute | solution.py:399
  14.2 2.9 %copy-start.3 = (bf16[512,128]{1,0:T(8,128)(2,1)S(1)}, bf16[512,128]{1,0:T(8,128)(2,1)}, u32[]{:S(2)}) copy-start(bf16[512,128]{1,0:T(8,128)(2,1)} %refs_1_.3) | copy-start | bytes 393220
  14.2 2.9 %copy-start.4 = (bf16[256,128]{1,0:T(8,128)(2,1)S(1)}, bf16[256,128]{1,0:T(8,128)(2,1)}, u32[]{:S(2)}) copy-start(bf16[256,128]{1,0:T(8,128)(2,1)} %refs_5_.3) | copy-start | bytes 196612
  14.2 2.9 %copy-start.5 = (bf16[256,128]{1,0:T(8,128)(2,1)S(1)}, bf16[256,128]{1,0:T(8,128)(2,1)}, u32[]{:S(2)}) copy-start(bf16[256,128]{1,0:T(8,128)(2,1)} %refs_6_.3) | copy-start | bytes 196612
  14.8 4.1 %collective-permute-start.5 = (bf16[48,256]{1,0:T(8,128)(2,1)S(1)}, bf16[48,256]{1,0:T(8,128)(2,1)S(1)}, u32[]{:S(2)}, u32[]{:S(2)}) collective-permute-start(bf16[48,256]{1,0:T(8,128)(2,1)S(1)} %rim.1.refs_1_), channel_id=1, source_target_pairs={{0,2},{1,3},{2,0},{3,1},{4,6},{5,7},{6,4},{7,5},{8,10},{9,11},{10,... | collective-permute-start | bytes 73736 | tf_op jit(solution)/shard_map/ppermute | solution.py:399
  16.0 3.0 %collective-permute-start.6 = (bf16[48,256]{1,0:T(8,128)(2,1)S(1)}, bf16[48,256]{1,0:T(8,128)(2,1)S(1)}, u32[]{:S(2)}, u32[]{:S(2)}) collective-permute-start(bf16[48,256]{1,0:T(8,128)(2,1)S(1)} %rim.1.refs_1_), channel_id=1, source_target_pairs={{0,1},{1,0},{2,3},{3,2},{4,5},{5,4},{6,7},{7,6},{8,9},{9,8},{10,11... | collective-permute-start | bytes 73736 | tf_op jit(solution)/shard_map/ppermute | solution.py:399
  16.9 3.3 %collective-permute-start.7 = (bf16[48,256]{1,0:T(8,128)(2,1)S(1)}, bf16[48,256]{1,0:T(8,128)(2,1)S(1)}, u32[]{:S(2)}, u32[]{:S(2)}) collective-permute-start(bf16[48,256]{1,0:T(8,128)(2,1)S(1)} %rim.1.refs_1_), channel_id=1, source_target_pairs={{0,3},{1,2},{2,1},{3,0},{4,7},{5,6},{6,5},{7,4},{8,11},{9,10},{10,... | collective-permute-start | bytes 73736 | tf_op jit(solution)/shard_map/ppermute | solution.py:399
  21.3 6.9 %collective-permute-start.10 = (f32[136,128]{1,0:T(8,128)S(1)}, f32[136,128]{1,0:T(8,128)S(1)}, u32[]{:S(2)}, u32[]{:S(2)}) collective-permute-start(f32[136,128]{1,0:T(8,128)S(1)} %get-tuple-element.56), channel_id=1, source_target_pairs={{0,12},{4,8},{8,4},{12,0},{1,13},{5,9},{9,5},{13,1},{2,14},{6,10},... | collective-permute-start | bytes 208904 | tf_op jit(solution)/shard_map/ppermute | solution.py:399
  24.9 5.1 %collective-permute-start.8 = (f32[136,128]{1,0:T(8,128)S(1)}, f32[136,128]{1,0:T(8,128)S(1)}, u32[]{:S(2)}, u32[]{:S(2)}) collective-permute-start(f32[136,128]{1,0:T(8,128)S(1)} %get-tuple-element.54), channel_id=1, source_target_pairs={{0,4},{4,0},{8,12},{12,8},{1,5},{5,1},{9,13},{13,9},{2,6},{6,2},{1... | collective-permute-start | bytes 208904 | tf_op jit(solution)/shard_map/ppermute | solution.py:399
  24.9 5.9 %collective-permute-start.9 = (f32[136,128]{1,0:T(8,128)S(1)}, f32[136,128]{1,0:T(8,128)S(1)}, u32[]{:S(2)}, u32[]{:S(2)}) collective-permute-start(f32[136,128]{1,0:T(8,128)S(1)} %get-tuple-element.55), channel_id=1, source_target_pairs={{0,8},{4,12},{8,0},{12,4},{1,9},{5,13},{9,1},{13,5},{2,10},{6,14},... | collective-permute-start | bytes 208904 | tf_op jit(solution)/shard_map/ppermute | solution.py:399

commit v6 on v5

--- a/solution.py
+++ b/solution.py
@@ -73,11 +73,6 @@
     return (centred * lax.rsqrt(spread + LN_EPS)).astype(BF16)
 
 
-def expand_kernel(w1_ref, w2_ref, dense1_ref, dense2_ref):
-    expand_weights(w1_ref[...], w1_ref.shape[0] // 36, w1_ref.shape[1], dense1_ref)
-    expand_weights(w2_ref[...], w2_ref.shape[0] // 36, w2_ref.shape[1], dense2_ref, ORDER)
-
-
 def opening_kernel(out_ref):
     out_ref[...] = jnp.zeros_like(out_ref)
 
@@ -89,8 +84,8 @@
 
 
 def first_kernel(side, counts_ref, adjacency_ref, weight, w1, w2, pixels, token_ref,
-                 edge_ref, border_ref, tiny_ref, cells_ref, even_lines, odd_lines, dense1_ref,
-                 dense2_ref, wide1, partial, cells, wide2):
+                 edge_ref, border_ref, tiny_ref, dense1_ref, dense2_ref, cells_ref, even_lines,
+                 odd_lines, wide1, partial, cells, wide2):
     expand_weights(w1[...], w1.shape[0] // 36, w1.shape[1], dense1_ref)
     expand_weights(w2[...], w2.shape[0] // 36, w2.shape[1], dense2_ref, ORDER)
     stem_n, half = weight.shape[0], side // 2
@@ -134,7 +129,7 @@
     tiny_ref[pl.ds(0, 16)] = cells_ref[pl.ds((half - 1) * half - 16, 16)]
     tiny_ref[pl.ds(16, 16)] = cells_ref[pl.ds(half * half - 16, 16)]
     positions, channels = partial.shape
-    chunk = 8 * half
+    chunk = 4 * half
     wide1[pl.ds(0, half)] = jnp.zeros((half, wide1.shape[1]), F32)
     row = lax.broadcasted_iota(jnp.int32, (chunk, channels), 0)
     first = lax.rem(row, half) == 0
@@ -435,7 +430,7 @@
         out_specs=vmem_spec(),
         compiler_params=pltpu.CompilerParams(vmem_limit_bytes=1 * MIB),
     )(tile_count, tissue, opened)
-    message, edge, border, tiny = pl.pallas_call(
+    message, edge, border, tiny, dense1, dense2 = pl.pallas_call(
         lambda *refs: first_kernel(side, *refs),
         name="first",
         out_shape=(
@@ -443,15 +438,13 @@
             jax.ShapeDtypeStruct((4 * half + 8, mid_n), F32),
             jax.ShapeDtypeStruct((border_rows, 4 * channels), BF16),
             jax.ShapeDtypeStruct((32, 4 * channels), BF16),
-        ),
+        ) + tuple(jax.ShapeDtypeStruct(shape, BF16) for shape in dense_shapes),
         in_specs=[vmem_spec()] * 6,
-        out_specs=(vmem_spec(),) * 4,
+        out_specs=(vmem_spec(),) * 6,
         scratch_shapes=[
             VMEM((half * half + 16, 4 * channels), BF16),
             VMEM((half * half, 2 * channels), F32),
             VMEM((half * half, 2 * channels), F32),
-            VMEM(dense_shapes[0], BF16),
-            VMEM(dense_shapes[1], BF16),
             VMEM((half * half + half, 4 * mid_n), F32),
             VMEM((half * half, mid_n), F32),
             VMEM((tokens, 4 * mid_n), BF16),
@@ -467,18 +460,8 @@
     line_n = lax.axis_size("tiles") * lax.axis_size("heads")
     prior = lax.ppermute(border, line, [(i, i + 1) for i in range(line_n - 1)])
     second = lax.ppermute(tiny, line, [(i, i + 2) for i in range(line_n - 2)])
-    message, w1, w2 = lax.optimization_barrier((message, w1, w2))
-    dense1, dense2 = pl.pallas_call(
-        expand_kernel,
-        name="expand",
-        out_shape=tuple(jax.ShapeDtypeStruct(shape, BF16) for shape in dense_shapes),
-        in_specs=[vmem_spec()] * 2,
-        out_specs=(vmem_spec(),) * 2,
-        compiler_params=pltpu.CompilerParams(vmem_limit_bytes=8 * MIB),
-        cost_estimate=pl.CostEstimate(flops=10**9, bytes_accessed=4 * 10**6, transcendentals=0),
-    )(w1, w2)
     far = swapped(message, "heads", 2)
-    message_n, dense1, prior = lax.optimization_barrier((message, dense1, prior))
+    message_n, prior = lax.optimization_barrier((message, prior))
     near = swapped(message_n, "heads", 1)
     far_near = swapped(far, "heads", 1)
 
@@ -549,7 +532,7 @@
     parts = (own,) + tuple(rest[3:])
 
     if few:
-        received = [swapped(parts[k], "tiles", k) for k in (1, 2, 3)]
+        received = [swapped(parts[k], "tiles", k) for k in (3, 2, 1)]
         return pl.pallas_call(
             lambda *refs: merge_kernel(head_n, *refs),
             name="merge",

time: 32 us -> 32 us (level)
  starting transfers between devices: 16.5 us -> 17.1 us
  Pallas kernels: 8.04 us -> 7.65 us
    ppermute x9, starting transfers between devices: 12.6 us -> 13.2 us  [swapped(): lax.ppermute(x, axis, [(i, i ^ distance) for i in range(lax.axis_size(axi...]
    pallas_call x1 -> x0, Pallas kernels: 0.35 us -> none  [per_device(): pl.pallas_call(expand_kernel, name='expand', out_shape=tuple((jax.ShapeDt...]
  transfers between devices with their start and end apart: 11 -> 11, of which waited for: 4 -> 3; matrix products, arithmetic and copies ran while one was open for 0% -> 0% of each run, Pallas kernels for 12% -> 10%
where the time goes in v6:
time: 32 us; the launch traced here: 31.8 us
  starting transfers between devices  17.1 us (53%)
  Pallas kernels  7.65 us (24%)
  waiting for transfers between devices  5.28 us (16%)
  between operations  1.59 us (5%)
    ppermute x9, starting transfers between devices, swapped(): lax.ppermute(x, axis, [(i, i ^ distance) for i in range(lax.axis_size(axi...  13.2 us
    ppermute x9, waiting for transfers between devices, swapped(): lax.ppermute(x, axis, [(i, i ^ distance) for i in range(lax.axis_size(axi...  5.28 us
    ppermute x1, starting transfers between devices, per_device(): second = lax.ppermute(tiny, line, [(i, i + 2) for i in range(line_n - 2)])  2.38 us
    pallas_call x1, Pallas kernels, per_device(): pl.pallas_call(lambda *refs: first_kernel(side, *refs), name='first', out...  2.3 us
    pallas_call x1, Pallas kernels, per_device(): pl.pallas_call(lambda *refs: main_kernel(part_n, *refs), name='main', out...  1.89 us
    ppermute x1, starting transfers between devices, per_device(): prior = lax.ppermute(border, line, [(i, i + 1) for i in range(line_n - 1)])  1.46 us
    pallas_call x1, Pallas kernels, per_device(): pl.pallas_call(lambda *refs: rest_kernel(part_n, *refs), name='rest', out...  1.06 us
    pallas_call x1, Pallas kernels, per_device(): pl.pallas_call(lambda *refs: merge_kernel(head_n, *refs), name='merge', o...  0.97 us
  transfers between devices with their start and end apart: 11, of which 3 were waited for; matrix products, arithmetic and copies ran while one was open for 0% of the time, Pallas kernels for 10%

profile of v6, /device:TPU:0, one launch (start us, length us, event | category | flops | bytes accessed | tf_op | source)
XLA Modules:
  0.0 31.8 jit_solution(3450457458091592081)
XLA Ops:
  0.0 0.0 copy-start.7
  0.0 0.0 copy-start.1
  0.0 0.0 copy-start.2
  0.0 0.0 copy-start.6
  0.0 0.0 copy-start
  1.5 0.0 copy-done.7
  1.5 0.0 copy-done.1
  1.5 0.0 copy-done.2
  1.5 0.0 copy-done.6
  1.5 0.1 copy-done
  1.6 2.3 %first.1 = (bf16[272,256]{1,0:T(8,128)(2,1)S(1)}, f32[136,128]{1,0:T(8,128)S(1)}, bf16[144,256]{1,0:T(8,128)(2,1)S(1)}, bf16[32,256]{1,0:T(8,128)(2,1)S(1)}, bf1...) custom-call(f32[8,128]{1,0:T(8,128)S(1)} %counts.1.refs_0_, s32[1,3]{1,0:T(1,128)S(1)} %copy-done.7, ...), custom_call_target="tpu_custom_call" | custom-call | tf_op jit(solution)/shard_map/first/pallas_call | solution.py:433
  3.9 3.0 %collective-permute-start.2 = (bf16[272,256]{1,0:T(8,128)(2,1)S(1)}, bf16[272,256]{1,0:T(8,128)(2,1)S(1)}, u32[]{:S(2)}, u32[]{:S(2)}) collective-permute-start(bf16[272,256]{1,0:T(8,128)(2,1)S(1)} %get-tuple-element.32.refs_1_), channel_id=1, source_target_pairs={{0,2},{1,3},{2,0},{3,1},{4,6},{5,7},{6,4},{7,5},{8,10},{9,11},{10,... | collective-permute-start | bytes 417800 | tf_op jit(solution)/shard_map/ppermute | solution.py:394
  7.0 1.5 %collective-permute-start = (bf16[144,256]{1,0:T(8,128)(2,1)S(1)}, bf16[144,256]{1,0:T(8,128)(2,1)S(1)}, u32[]{:S(2)}, u32[]{:S(2)}) collective-permute-start(bf16[144,256]{1,0:T(8,128)(2,1)S(1)} %get-tuple-element.31), channel_id=1, source_target_pairs={{0,1},{1,2},{2,3},{3,4},{4,5},{5,6},{6,7},{7,8},{8,9},{9,10},{10,1... | collective-permute-start | bytes 221192 | tf_op jit(solution)/shard_map/ppermute | solution.py:461
  8.4 2.4 %collective-permute-start.4 = (bf16[32,256]{1,0:T(8,128)(2,1)S(1)}, bf16[32,256]{1,0:T(8,128)(2,1)S(1)}, u32[]{:S(2)}, u32[]{:S(2)}) collective-permute-start(bf16[32,256]{1,0:T(8,128)(2,1)S(1)} %get-tuple-element.38), channel_id=1, source_target_pairs={{0,2},{1,3},{2,4},{3,5},{4,6},{5,7},{6,8},{7,9},{8,10},{9,11},{10,... | collective-permute-start | bytes 49160 | tf_op jit(solution)/shard_map/ppermute | solution.py:462
  10.8 0.0 collective-permute-done.prior_ref
  10.8 2.9 %collective-permute-start.1 = (bf16[272,256]{1,0:T(8,128)(2,1)S(1)}, bf16[272,256]{1,0:T(8,128)(2,1)S(1)}, u32[]{:S(2)}, u32[]{:S(2)}) collective-permute-start(bf16[272,256]{1,0:T(8,128)(2,1)S(1)} %get-tuple-element.32.refs_1_), channel_id=1, source_target_pairs={{0,1},{1,0},{2,3},{3,2},{4,5},{5,4},{6,7},{7,6},{8,9},{9,8},{10,11... | collective-permute-start | bytes 417800 | tf_op jit(solution)/shard_map/ppermute | solution.py:394
  13.7 0.0 collective-permute-done.2.refs_3_
  13.7 0.1 collective-permute-start.3
  13.8 0.0 collective-permute-done.4.second_ref
  13.8 0.0 copy-start.3
  13.8 0.0 copy-start.4
  13.8 0.0 copy-start.5
  13.8 0.6 %rim.1.refs_1_ = bf16[48,256]{1,0:T(8,128)(2,1)S(1)} custom-call(f32[136,128]{1,0:T(8,128)S(1)} %get-tuple-element.36.edge_ref, bf16[144,256]{1,0:T(8,128)(2,1)S(1)} %collective-permute-done.prior_ref, bf16[32,256]{1,0:T(8,128)(2,1)S(1)} %collective-permute-done.4.second_ref, bf16[256,512]{1,0:T(8,128)(2,1)S(1)} %get-tuple-element.39.dense1_ref, ...), custom_call_target="tpu_custom_call" | custom-call | flops 20000000000 | bytes 40000000 | tf_op jit(solution)/shard_map/rim/pallas_call | solution.py:468
  14.5 2.3 %collective-permute-start.7 = (bf16[48,256]{1,0:T(8,128)(2,1)S(1)}, bf16[48,256]{1,0:T(8,128)(2,1)S(1)}, u32[]{:S(2)}, u32[]{:S(2)}) collective-permute-start(bf16[48,256]{1,0:T(8,128)(2,1)S(1)} %rim.1.refs_1_), channel_id=1, source_target_pairs={{0,3},{1,2},{2,1},{3,0},{4,7},{5,6},{6,5},{7,4},{8,11},{9,10},{10,... | collective-permute-start | bytes 73736 | tf_op jit(solution)/shard_map/ppermute | solution.py:394
  16.8 0.0 collective-permute-start.6
  16.8 0.5 %collective-permute-start.5 = (bf16[48,256]{1,0:T(8,128)(2,1)S(1)}, bf16[48,256]{1,0:T(8,128)(2,1)S(1)}, u32[]{:S(2)}, u32[]{:S(2)}) collective-permute-start(bf16[48,256]{1,0:T(8,128)(2,1)S(1)} %rim.1.refs_1_), channel_id=1, source_target_pairs={{0,2},{1,3},{2,0},{3,1},{4,6},{5,7},{6,4},{7,5},{8,10},{9,11},{10,... | collective-permute-start | bytes 73736 | tf_op jit(solution)/shard_map/ppermute | solution.py:394
  17.3 0.0 collective-permute-done.1.refs_2_
  17.3 0.0 collective-permute-done.3.refs_4_
  17.3 0.0 copy-done.3
  17.3 0.0 copy-done.4
  17.3 0.0 copy-done.5
  17.3 1.9 %main.1 = (f32[384,128]{1,0:T(8,128)S(1)}, f32[384,128]{1,0:T(8,128)S(1)}, bf16[1024,128]{1,0:T(8,128)(2,1)S(1)}, bf16[1024,128]{1,0:T(8,128)(2,1)S(1)}, f32[8,1024]{1,0:T(8,128)S(1)}) custom-call(s32[1]{0:T(128)} %bitcast.refs_0_, bf16[272,256]{1,0:T(8,128)(2,1)S(1)} %get-tuple-element.32.refs_1_, bf16[272,256]{1,0:T(8,128)(2,1)S(1)} %collective-permute-done.1.refs_2_, ...), custom_call_target="tpu_custom_call" | custom-call | flops 1000000 | bytes 10000 | tf_op jit(solution)/shard_map/main/pallas_call | solution.py:493
  19.2 0.0 collective-permute-done.7.refs_4_
  19.2 0.0 collective-permute-done.6.refs_3_
  19.2 1.4 %collective-permute-done.5.refs_2_ = bf16[48,256]{1,0:T(8,128)(2,1)S(1)} collective-permute-done((bf16[48,256]{1,0:T(8,128)(2,1)S(1)}, bf16[48,256]{1,0:T(8,128)(2,1)S(1)}, u32[]{:S(2)}, u32[]{:S(2)}) %collective-permute-start.5) | collective-permute-done | bytes 24608 | tf_op jit(solution)/shard_map/ppermute | solution.py:394
  20.6 1.1 %rest.1 = (bf16[128,128]{1,0:T(8,128)(2,1)S(1)}, bf16[128,128]{1,0:T(8,128)(2,1)S(1)}, f32[8,128]{1,0:T(8,128)S(1)}, f32[136,128]{1,0:T(8,128)S(1)}, f32[136,128]{1,0:T(8,128)S(1)}, /*index=5*/f32[136,128]{1,0:T(8,128)S(1)}) custom-call(s32[1]{0:T(128)} %bitcast.refs_0_, bf16[48,256]{1,0:T(8,128)(2,1)S(1)} %rim.1.refs_1_, ...), custom_call_target="tpu_custom_call" | custom-call | flops 20000000000 | bytes 40000000 | tf_op jit(solution)/shard_map/rest/pallas_call | solution.py:508
  21.7 3.2 %collective-permute-start.8 = (f32[136,128]{1,0:T(8,128)S(1)}, f32[136,128]{1,0:T(8,128)S(1)}, u32[]{:S(2)}, u32[]{:S(2)}) collective-permute-start(f32[136,128]{1,0:T(8,128)S(1)} %get-tuple-element.46), channel_id=1, source_target_pairs={{0,12},{4,8},{8,4},{12,0},{1,13},{5,9},{9,5},{13,1},{2,14},{6,10},... | collective-permute-start | bytes 208904 | tf_op jit(solution)/shard_map/ppermute | solution.py:394
  24.9 0.0 collective-permute-start.9
  24.9 1.2 %collective-permute-start.10 = (f32[136,128]{1,0:T(8,128)S(1)}, f32[136,128]{1,0:T(8,128)S(1)}, u32[]{:S(2)}, u32[]{:S(2)}) collective-permute-start(f32[136,128]{1,0:T(8,128)S(1)} %get-tuple-element.48), channel_id=1, source_target_pairs={{0,4},{4,0},{8,12},{12,8},{1,5},{5,1},{9,13},{13,9},{2,6},{6,2},{1... | collective-permute-start | bytes 208904 | tf_op jit(solution)/shard_map/ppermute | solution.py:394
  26.1 0.8 %own.1.refs_0_ = f32[136,128]{1,0:T(8,128)S(1)} custom-call(s32[1]{0:T(128)} %bitcast.refs_0_, bf16[512,128]{1,0:T(8,128)(2,1)S(1)} %copy-done.3, bf16[1024,128]{1,0:T(8,128)(2,1)S(1)} %get-tuple-element.33.refs_2_, bf16[1024,128]{1,0:T(8,128)(2,1)S(1)} %get-tuple-element.34.refs_3_, f32[8,1024]{1,0:T(8,128)S(1)} %get-tuple-element.35.refs_4_, ...), custom_call_target="tpu_custom_call" | custom-call | flops 1000000000 | bytes 4000000 | tf_op jit(solution)/shard_map/own/pallas_call | solution.py:523
  26.9 1.6 %collective-permute-done.8.refs_1_ = f32[136,128]{1,0:T(8,128)S(1)} collective-permute-done((f32[136,128]{1,0:T(8,128)S(1)}, f32[136,128]{1,0:T(8,128)S(1)}, u32[]{:S(2)}, u32[]{:S(2)}) %collective-permute-start.8) | collective-permute-done | bytes 69664 | tf_op jit(solution)/shard_map/ppermute | solution.py:394
  28.5 2.3 %collective-permute-done.9.refs_2_ = f32[136,128]{1,0:T(8,128)S(1)} collective-permute-done((f32[136,128]{1,0:T(8,128)S(1)}, f32[136,128]{1,0:T(8,128)S(1)}, u32[]{:S(2)}, u32[]{:S(2)}) %collective-permute-start.9) | collective-permute-done | bytes 69664 | tf_op jit(solution)/shard_map/ppermute | solution.py:394
  30.8 0.0 collective-permute-done.10.refs_3_
  30.8 1.0 %merge.1 = bf16[128,128]{1,0:T(8,128)(2,1)} custom-call(f32[136,128]{1,0:T(8,128)S(1)} %own.1.refs_0_, f32[136,128]{1,0:T(8,128)S(1)} %collective-permute-done.8.refs_1_, f32[136,128]{1,0:T(8,128)S(1)} %collective-permute-done.9.refs_2_, f32[136,128]{1,0:T(8,128)S(1)} %collective-permute-done.10.refs_3_), custom_call_target="tpu_custom_call" | custom-call | tf_op jit(solution)/shard_map/merge/pallas_call | solution.py:536
  (2 shorter events, 0.0 us)
Async XLA Ops:
  0.0 1.5 %copy-start.7 = (s32[1,3]{1,0:T(1,128)S(1)}, s32[1,3]{1,0:T(1,128)}, u32[]{:S(2)}) copy-start(s32[1,3]{1,0:T(1,128)} %refs_1_.2) | copy-start | bytes 40
  0.0 1.5 %copy-start.1 = (bf16[4,9,32,64]{3,2,1,0:T(8,128)(2,1)S(1)}, bf16[4,9,32,64]{3,2,1,0:T(8,128)(2,1)}, u32[]{:S(2)}) copy-start(bf16[4,9,32,64]{3,2,1,0:T(8,128)(2,1)} %param.13) | copy-start | bytes 442372
  0.0 1.5 %copy-start.2 = (bf16[4,9,16,32]{3,2,1,0:T(8,128)(2,1)S(1)}, bf16[4,9,16,32]{3,2,1,0:T(8,128)(2,1)}, u32[]{:S(2)}) copy-start(bf16[4,9,16,32]{3,2,1,0:T(8,128)(2,1)} %param.12) | copy-start | bytes 110596
  0.0 1.5 %copy-start.6 = (bf16[192,64]{0,1:T(8,128)(2,1)S(1)}, bf16[192,64]{0,1:T(8,128)(2,1)}, u32[]{:S(2)}) copy-start(bf16[192,64]{0,1:T(8,128)(2,1)} %param.11) | copy-start | bytes 73732
  0.0 1.6 %copy-start = (bf16[1,4096,192]{1,2,0:T(8,128)(2,1)S(1)}, bf16[1,4096,192]{1,2,0:T(8,128)(2,1)}, u32[]{:S(2)}) copy-start(bf16[1,4096,192]{1,2,0:T(8,128)(2,1)} %param.10) | copy-start | bytes 4718596
  3.9 9.8 %collective-permute-start.2 = (bf16[272,256]{1,0:T(8,128)(2,1)S(1)}, bf16[272,256]{1,0:T(8,128)(2,1)S(1)}, u32[]{:S(2)}, u32[]{:S(2)}) collective-permute-start(bf16[272,256]{1,0:T(8,128)(2,1)S(1)} %get-tuple-element.32.refs_1_), channel_id=1, source_target_pairs={{0,2},{1,3},{2,0},{3,1},{4,6},{5,7},{6,4},{7,5},{8,10},{9,11},{10,... | collective-permute-start | bytes 417800 | tf_op jit(solution)/shard_map/ppermute | solution.py:394
  7.0 3.9 %collective-permute-start = (bf16[144,256]{1,0:T(8,128)(2,1)S(1)}, bf16[144,256]{1,0:T(8,128)(2,1)S(1)}, u32[]{:S(2)}, u32[]{:S(2)}) collective-permute-start(bf16[144,256]{1,0:T(8,128)(2,1)S(1)} %get-tuple-element.31), channel_id=1, source_target_pairs={{0,1},{1,2},{2,3},{3,4},{4,5},{5,6},{6,7},{7,8},{8,9},{9,10},{10,1... | collective-permute-start | bytes 221192 | tf_op jit(solution)/shard_map/ppermute | solution.py:461
  8.4 5.4 %collective-permute-start.4 = (bf16[32,256]{1,0:T(8,128)(2,1)S(1)}, bf16[32,256]{1,0:T(8,128)(2,1)S(1)}, u32[]{:S(2)}, u32[]{:S(2)}) collective-permute-start(bf16[32,256]{1,0:T(8,128)(2,1)S(1)} %get-tuple-element.38), channel_id=1, source_target_pairs={{0,2},{1,3},{2,4},{3,5},{4,6},{5,7},{6,8},{7,9},{8,10},{9,11},{10,... | collective-permute-start | bytes 49160 | tf_op jit(solution)/shard_map/ppermute | solution.py:462
  10.8 6.5 %collective-permute-start.1 = (bf16[272,256]{1,0:T(8,128)(2,1)S(1)}, bf16[272,256]{1,0:T(8,128)(2,1)S(1)}, u32[]{:S(2)}, u32[]{:S(2)}) collective-permute-start(bf16[272,256]{1,0:T(8,128)(2,1)S(1)} %get-tuple-element.32.refs_1_), channel_id=1, source_target_pairs={{0,1},{1,0},{2,3},{3,2},{4,5},{5,4},{6,7},{7,6},{8,9},{9,8},{10,11... | collective-permute-start | bytes 417800 | tf_op jit(solution)/shard_map/ppermute | solution.py:394
  13.7 3.6 %collective-permute-start.3 = (bf16[272,256]{1,0:T(8,128)(2,1)S(1)}, bf16[272,256]{1,0:T(8,128)(2,1)S(1)}, u32[]{:S(2)}, u32[]{:S(2)}) collective-permute-start(bf16[272,256]{1,0:T(8,128)(2,1)S(1)} %collective-permute-done.2.refs_3_), channel_id=1, source_target_pairs={{0,1},{1,0},{2,3},{3,2},{4,5},{5,4},{6,7},{7,6},{8,9},{9,8},{10,11... | collective-permute-start | bytes 417800 | tf_op jit(solution)/shard_map/ppermute | solution.py:394
  13.8 3.5 %copy-start.3 = (bf16[512,128]{1,0:T(8,128)(2,1)S(1)}, bf16[512,128]{1,0:T(8,128)(2,1)}, u32[]{:S(2)}) copy-start(bf16[512,128]{1,0:T(8,128)(2,1)} %refs_1_.3) | copy-start | bytes 393220
  13.8 3.5 %copy-start.4 = (bf16[256,128]{1,0:T(8,128)(2,1)S(1)}, bf16[256,128]{1,0:T(8,128)(2,1)}, u32[]{:S(2)}) copy-start(bf16[256,128]{1,0:T(8,128)(2,1)} %refs_5_.3) | copy-start | bytes 196612
  13.8 3.5 %copy-start.5 = (bf16[256,128]{1,0:T(8,128)(2,1)S(1)}, bf16[256,128]{1,0:T(8,128)(2,1)}, u32[]{:S(2)}) copy-start(bf16[256,128]{1,0:T(8,128)(2,1)} %refs_6_.3) | copy-start | bytes 196612
  14.5 4.8 %collective-permute-start.7 = (bf16[48,256]{1,0:T(8,128)(2,1)S(1)}, bf16[48,256]{1,0:T(8,128)(2,1)S(1)}, u32[]{:S(2)}, u32[]{:S(2)}) collective-permute-start(bf16[48,256]{1,0:T(8,128)(2,1)S(1)} %rim.1.refs_1_), channel_id=1, source_target_pairs={{0,3},{1,2},{2,1},{3,0},{4,7},{5,6},{6,5},{7,4},{8,11},{9,10},{10,... | collective-permute-start | bytes 73736 | tf_op jit(solution)/shard_map/ppermute | solution.py:394
  16.8 2.4 %collective-permute-start.6 = (bf16[48,256]{1,0:T(8,128)(2,1)S(1)}, bf16[48,256]{1,0:T(8,128)(2,1)S(1)}, u32[]{:S(2)}, u32[]{:S(2)}) collective-permute-start(bf16[48,256]{1,0:T(8,128)(2,1)S(1)} %rim.1.refs_1_), channel_id=1, source_target_pairs={{0,1},{1,0},{2,3},{3,2},{4,5},{5,4},{6,7},{7,6},{8,9},{9,8},{10,11... | collective-permute-start | bytes 73736 | tf_op jit(solution)/shard_map/ppermute | solution.py:394
  16.8 3.8 %collective-permute-start.5 = (bf16[48,256]{1,0:T(8,128)(2,1)S(1)}, bf16[48,256]{1,0:T(8,128)(2,1)S(1)}, u32[]{:S(2)}, u32[]{:S(2)}) collective-permute-start(bf16[48,256]{1,0:T(8,128)(2,1)S(1)} %rim.1.refs_1_), channel_id=1, source_target_pairs={{0,2},{1,3},{2,0},{3,1},{4,6},{5,7},{6,4},{7,5},{8,10},{9,11},{10,... | collective-permute-start | bytes 73736 | tf_op jit(solution)/shard_map/ppermute | solution.py:394
  21.7 6.8 %collective-permute-start.8 = (f32[136,128]{1,0:T(8,128)S(1)}, f32[136,128]{1,0:T(8,128)S(1)}, u32[]{:S(2)}, u32[]{:S(2)}) collective-permute-start(f32[136,128]{1,0:T(8,128)S(1)} %get-tuple-element.46), channel_id=1, source_target_pairs={{0,12},{4,8},{8,4},{12,0},{1,13},{5,9},{9,5},{13,1},{2,14},{6,10},... | collective-permute-start | bytes 208904 | tf_op jit(solution)/shard_map/ppermute | solution.py:394
  24.9 5.9 %collective-permute-start.9 = (f32[136,128]{1,0:T(8,128)S(1)}, f32[136,128]{1,0:T(8,128)S(1)}, u32[]{:S(2)}, u32[]{:S(2)}) collective-permute-start(f32[136,128]{1,0:T(8,128)S(1)} %get-tuple-element.47), channel_id=1, source_target_pairs={{0,8},{4,12},{8,0},{12,4},{1,9},{5,13},{9,1},{13,5},{2,10},{6,14},... | collective-permute-start | bytes 208904 | tf_op jit(solution)/shard_map/ppermute | solution.py:394
  24.9 5.9 %collective-permute-start.10 = (f32[136,128]{1,0:T(8,128)S(1)}, f32[136,128]{1,0:T(8,128)S(1)}, u32[]{:S(2)}, u32[]{:S(2)}) collective-permute-start(f32[136,128]{1,0:T(8,128)S(1)} %get-tuple-element.48), channel_id=1, source_target_pairs={{0,4},{4,0},{8,12},{12,8},{1,5},{5,1},{9,13},{13,9},{2,6},{6,2},{1... | collective-permute-start | bytes 208904 | tf_op jit(solution)/shard_map/ppermute | solution.py:394
